TPU v7x, 128 devices: a whole 4x4x4 slice. The times are simulated.
128 devices in a mesh: row: 16 (over y_hi, z, core), col: 8 (over x, y_lo).
Axes of the slice: x: 4, y: 4 (y_hi: 2, y_lo: 2; y = y_hi * 2 + y_lo), z: 4, core: 2. Of those that a mesh axis runs over, the one named last changes fastest.
Arguments:
- pivot_inverse: float32 [1024, 1024], P('row'), may hold values from -1 to 2, as said below
- panel: float32 [32, 1024, 1024], P('row', 'col'), may hold values from -1 to 1
- trailing: float32 [320, 1024, 1024], P('row', None, 'col'), may hold values from -6 to 6
- tile_list: int32 [320, 2], P('row'), may hold values from -1 to 31, as said below
Outputs:
- solved_panel: float32 [32, 1024, 1024], P('row', 'col')
- updated: float32 [320, 1024, 1024], P('row', None, 'col')
Inputs may be any that keep to these rules, and one draw needn't show every extreme that they name: `pivot_inverse`: lower triangular, diagonal between 0.5 and 2. `tile_list`: slots t of group g are g * 20 to g * 20 + 19. Column 0 lies in 0 to 1; column 1 is a panel tile or -1 for an empty slot. The live slots of a group come first and name distinct pairs; each group in the first half of the groups holds exactly 6 live slots, each in the second half exactly 20. Empty slots hold 0 in column 0.
All inputs are finite; a program needn't handle non-finite values.
Results may differ from a plain program's by a relative error of at most 0.00007.
Values sent between devices are 32-bit elements; how exact they have to be, the bound alone decides.
No kernel may reach another device: no remote copies, remote signals or barrier semaphores. Data moves between devices by JAX's collectives and lax.ppermute only.
A program may use at most 128 MiB of HBM per device.

v0:
```python
import jax
import jax.numpy as jnp
from jax import lax
from jax.sharding import PartitionSpec as P

highest = lax.Precision.HIGHEST


def slot_term(left_tile, right_rows):
    return jnp.einsum("ak,bk->ab", left_tile, right_rows, precision=highest)


def per_device(pivot_inverse, panel, trailing, tile_list):
    full_pivot = lax.all_gather(pivot_inverse, "row", axis=0, tiled=True)
    slice_rows = panel.shape[1]
    tile_order = panel.shape[2]
    solved = jnp.einsum("pak,jk->paj", panel, full_pivot, precision=highest)
    whole_tiles = lax.all_gather(solved, "col", axis=1, tiled=True)
    slices = lax.all_gather(solved, "row", axis=0, tiled=True)
    empty_term = jnp.zeros((tile_order, slice_rows), jnp.float32)

    def owner_slot(listed):
        return lax.cond(
            listed[1] >= 0,
            lambda: slot_term(whole_tiles[listed[0]], slices[jnp.maximum(listed[1], 0)]),
            lambda: empty_term,
        )

    updates = lax.map(owner_slot, tile_list)
    return (solved, trailing - updates)


def solution(mesh):
    placed = (P("row", None), P("row", "col", None), P("row", None, "col"), P("row", None))
    return jax.shard_map(
        per_device,
        mesh=mesh,
        in_specs=placed,
        out_specs=(P("row", "col", None), P("row", None, "col")),
        check_vma=False,
    )
```

profile of v0, /device:TPU:17, one launch (start us, length us, event | category | flops | bytes accessed | tf_op | source)
XLA Modules:
  0.0 581.7 jit_solution(2758607278741506493)
XLA Ops:
  8.0 58.1 %all-gather.4.cloned.1.call-done = f32[1024,1024]{1,0:T(8,128)} async-done(((f32[64,1024]{1,0:T(8,128)}), f32[1024,1024]{1,0:T(8,128)}) %all-gather.4.cloned.1.call-update) | async-done | bytes 4194320 | tf_op jit(solution)/shard_map/all_gather | solution.py:14
  66.1 6.8 %fusion.9 = f32[2,128,1024]{2,1,0:T(8,128)} fusion(f32[2,128,1024]{2,1,0:T(8,128)S(1)} %copy-done, f32[1024,1024]{1,0:T(8,128)} %all-gather.4.cloned.1.call-done), kind=kOutput, calls=%fused_computation.9 | convolution fusion | flops 3221225472 | bytes 6291456 | tf_op jit(solution)/shard_map/pak,jk->paj/dot_general | solution.py:17
  74.5 166.4 %all-gather.6.cloned.1.call-done = f32[2,1024,1024]{2,1,0:T(8,128)} async-done(((f32[2,128,1024]{2,1,0:T(8,128)}), f32[2,1024,1024]{2,1,0:T(8,128)}) %all-gather.6.cloned.1.call-update) | async-done | bytes 8388624 | tf_op jit(solution)/shard_map/all_gather | solution.py:18
  240.9 116.1 %all-gather.8.cloned.1.call-done = f32[32,128,1024]{2,1,0:T(8,128)} async-done(((f32[2,128,1024]{2,1,0:T(8,128)}), f32[32,128,1024]{2,1,0:T(8,128)}) %all-gather.8.cloned.1.call-update) | async-done | bytes 16777232 | tf_op jit(solution)/shard_map/all_gather | solution.py:19
  357.0 205.8 %while.10 = (s32[]{:T(128)}, f32[20,1024,128]{2,1,0:T(8,128)}, s32[20,2]{1,0:T(8,128)S(1)}, f32[2,1024,1024]{2,1,0:T(8,128)}, f32[32,128,1024]{2,1,0:T(8,128)}, /*index=5*/s32[]{:T(128)}, s32[1,1]{1,0:T(1,128)}) while((s32[]{:T(128)}, f32[20,1024,128]{2,1,0:T(8,128)}, s32[20,2]{1,0:T(8,128)S(1)}, f32[2,1024,1024]{2,1,0:T(8,128)}, ...), condition=%wide.region_3.4_spmd, body=%wide.region_0.3_spmd.sunk | while | flops 1610612736 | bytes 6292697 | solution.py:29
  358.1 8.3 %conditional.2 = (f32[1,1024,128]{2,1,0:T(8,128)S(1)}) conditional(s32[]{:T(128)} %bitcast.18, () %tuple.35, (s32[1,2]{1,0:T(1,128)S(1)}, f32[2,1024,1024]{2,1,0:T(8,128)}, f32[32,128,1024]{2,1,0:T(8,128)}) %tuple.36), branch_computations={%region_1.1_spmd, %region_2.2_spmd} | conditional | flops 1610612736 | bytes 5243466 | solution.py:23
  361.1 5.3 fusion.3
  366.5 0.8 constant_dynamic-update-slice_fusion.2
  368.4 8.3 %conditional.2 = (f32[1,1024,128]{2,1,0:T(8,128)S(1)}) conditional(s32[]{:T(128)} %bitcast.18, () %tuple.35, (s32[1,2]{1,0:T(1,128)S(1)}, f32[2,1024,1024]{2,1,0:T(8,128)}, f32[32,128,1024]{2,1,0:T(8,128)}) %tuple.36), branch_computations={%region_1.1_spmd, %region_2.2_spmd} | conditional | flops 1610612736 | bytes 5243466 | solution.py:23
  371.4 5.3 fusion.3
  376.7 0.8 constant_dynamic-update-slice_fusion.2
  378.7 8.3 %conditional.2 = (f32[1,1024,128]{2,1,0:T(8,128)S(1)}) conditional(s32[]{:T(128)} %bitcast.18, () %tuple.35, (s32[1,2]{1,0:T(1,128)S(1)}, f32[2,1024,1024]{2,1,0:T(8,128)}, f32[32,128,1024]{2,1,0:T(8,128)}) %tuple.36), branch_computations={%region_1.1_spmd, %region_2.2_spmd} | conditional | flops 1610612736 | bytes 5243466 | solution.py:23
  381.7 5.3 fusion.3
  387.0 0.8 constant_dynamic-update-slice_fusion.2
  389.0 8.3 %conditional.2 = (f32[1,1024,128]{2,1,0:T(8,128)S(1)}) conditional(s32[]{:T(128)} %bitcast.18, () %tuple.35, (s32[1,2]{1,0:T(1,128)S(1)}, f32[2,1024,1024]{2,1,0:T(8,128)}, f32[32,128,1024]{2,1,0:T(8,128)}) %tuple.36), branch_computations={%region_1.1_spmd, %region_2.2_spmd} | conditional | flops 1610612736 | bytes 5243466 | solution.py:23
  392.0 5.3 fusion.3
  397.3 0.8 constant_dynamic-update-slice_fusion.2
  399.3 8.3 %conditional.2 = (f32[1,1024,128]{2,1,0:T(8,128)S(1)}) conditional(s32[]{:T(128)} %bitcast.18, () %tuple.35, (s32[1,2]{1,0:T(1,128)S(1)}, f32[2,1024,1024]{2,1,0:T(8,128)}, f32[32,128,1024]{2,1,0:T(8,128)}) %tuple.36), branch_computations={%region_1.1_spmd, %region_2.2_spmd} | conditional | flops 1610612736 | bytes 5243466 | solution.py:23
  402.3 5.3 fusion.3
  407.6 0.8 constant_dynamic-update-slice_fusion.2
  409.6 8.3 %conditional.2 = (f32[1,1024,128]{2,1,0:T(8,128)S(1)}) conditional(s32[]{:T(128)} %bitcast.18, () %tuple.35, (s32[1,2]{1,0:T(1,128)S(1)}, f32[2,1024,1024]{2,1,0:T(8,128)}, f32[32,128,1024]{2,1,0:T(8,128)}) %tuple.36), branch_computations={%region_1.1_spmd, %region_2.2_spmd} | conditional | flops 1610612736 | bytes 5243466 | solution.py:23
  412.6 5.3 fusion.3
  417.9 0.8 constant_dynamic-update-slice_fusion.2
  419.9 8.3 %conditional.2 = (f32[1,1024,128]{2,1,0:T(8,128)S(1)}) conditional(s32[]{:T(128)} %bitcast.18, () %tuple.35, (s32[1,2]{1,0:T(1,128)S(1)}, f32[2,1024,1024]{2,1,0:T(8,128)}, f32[32,128,1024]{2,1,0:T(8,128)}) %tuple.36), branch_computations={%region_1.1_spmd, %region_2.2_spmd} | conditional | flops 1610612736 | bytes 5243466 | solution.py:23
  422.9 5.3 fusion.3
  428.2 0.8 constant_dynamic-update-slice_fusion.2
  430.2 8.3 %conditional.2 = (f32[1,1024,128]{2,1,0:T(8,128)S(1)}) conditional(s32[]{:T(128)} %bitcast.18, () %tuple.35, (s32[1,2]{1,0:T(1,128)S(1)}, f32[2,1024,1024]{2,1,0:T(8,128)}, f32[32,128,1024]{2,1,0:T(8,128)}) %tuple.36), branch_computations={%region_1.1_spmd, %region_2.2_spmd} | conditional | flops 1610612736 | bytes 5243466 | solution.py:23
  433.2 5.3 fusion.3
  438.5 0.8 constant_dynamic-update-slice_fusion.2
  440.5 8.3 %conditional.2 = (f32[1,1024,128]{2,1,0:T(8,128)S(1)}) conditional(s32[]{:T(128)} %bitcast.18, () %tuple.35, (s32[1,2]{1,0:T(1,128)S(1)}, f32[2,1024,1024]{2,1,0:T(8,128)}, f32[32,128,1024]{2,1,0:T(8,128)}) %tuple.36), branch_computations={%region_1.1_spmd, %region_2.2_spmd} | conditional | flops 1610612736 | bytes 5243466 | solution.py:23
  443.4 5.3 fusion.3
  448.8 0.8 constant_dynamic-update-slice_fusion.2
  450.7 8.3 %conditional.2 = (f32[1,1024,128]{2,1,0:T(8,128)S(1)}) conditional(s32[]{:T(128)} %bitcast.18, () %tuple.35, (s32[1,2]{1,0:T(1,128)S(1)}, f32[2,1024,1024]{2,1,0:T(8,128)}, f32[32,128,1024]{2,1,0:T(8,128)}) %tuple.36), branch_computations={%region_1.1_spmd, %region_2.2_spmd} | conditional | flops 1610612736 | bytes 5243466 | solution.py:23
  453.7 5.3 fusion.3
  459.1 0.8 constant_dynamic-update-slice_fusion.2
  461.0 8.3 %conditional.2 = (f32[1,1024,128]{2,1,0:T(8,128)S(1)}) conditional(s32[]{:T(128)} %bitcast.18, () %tuple.35, (s32[1,2]{1,0:T(1,128)S(1)}, f32[2,1024,1024]{2,1,0:T(8,128)}, f32[32,128,1024]{2,1,0:T(8,128)}) %tuple.36), branch_computations={%region_1.1_spmd, %region_2.2_spmd} | conditional | flops 1610612736 | bytes 5243466 | solution.py:23
  464.0 5.3 fusion.3
  469.3 0.8 constant_dynamic-update-slice_fusion.2
  471.3 8.3 %conditional.2 = (f32[1,1024,128]{2,1,0:T(8,128)S(1)}) conditional(s32[]{:T(128)} %bitcast.18, () %tuple.35, (s32[1,2]{1,0:T(1,128)S(1)}, f32[2,1024,1024]{2,1,0:T(8,128)}, f32[32,128,1024]{2,1,0:T(8,128)}) %tuple.36), branch_computations={%region_1.1_spmd, %region_2.2_spmd} | conditional | flops 1610612736 | bytes 5243466 | solution.py:23
  474.3 5.3 fusion.3
  481.6 8.3 %conditional.2 = (f32[1,1024,128]{2,1,0:T(8,128)S(1)}) conditional(s32[]{:T(128)} %bitcast.18, () %tuple.35, (s32[1,2]{1,0:T(1,128)S(1)}, f32[2,1024,1024]{2,1,0:T(8,128)}, f32[32,128,1024]{2,1,0:T(8,128)}) %tuple.36), branch_computations={%region_1.1_spmd, %region_2.2_spmd} | conditional | flops 1610612736 | bytes 5243466 | solution.py:23
  484.6 5.3 fusion.3
  489.9 0.8 constant_dynamic-update-slice_fusion.2
  491.9 8.3 %conditional.2 = (f32[1,1024,128]{2,1,0:T(8,128)S(1)}) conditional(s32[]{:T(128)} %bitcast.18, () %tuple.35, (s32[1,2]{1,0:T(1,128)S(1)}, f32[2,1024,1024]{2,1,0:T(8,128)}, f32[32,128,1024]{2,1,0:T(8,128)}) %tuple.36), branch_computations={%region_1.1_spmd, %region_2.2_spmd} | conditional | flops 1610612736 | bytes 5243466 | solution.py:23
  494.9 5.3 fusion.3
  500.2 0.8 constant_dynamic-update-slice_fusion.2
  502.2 8.3 %conditional.2 = (f32[1,1024,128]{2,1,0:T(8,128)S(1)}) conditional(s32[]{:T(128)} %bitcast.18, () %tuple.35, (s32[1,2]{1,0:T(1,128)S(1)}, f32[2,1024,1024]{2,1,0:T(8,128)}, f32[32,128,1024]{2,1,0:T(8,128)}) %tuple.36), branch_computations={%region_1.1_spmd, %region_2.2_spmd} | conditional | flops 1610612736 | bytes 5243466 | solution.py:23
  505.2 5.3 fusion.3
  512.5 8.3 %conditional.2 = (f32[1,1024,128]{2,1,0:T(8,128)S(1)}) conditional(s32[]{:T(128)} %bitcast.18, () %tuple.35, (s32[1,2]{1,0:T(1,128)S(1)}, f32[2,1024,1024]{2,1,0:T(8,128)}, f32[32,128,1024]{2,1,0:T(8,128)}) %tuple.36), branch_computations={%region_1.1_spmd, %region_2.2_spmd} | conditional | flops 1610612736 | bytes 5243466 | solution.py:23
  515.5 5.3 fusion.3
  520.8 0.8 constant_dynamic-update-slice_fusion.2
  522.8 8.3 %conditional.2 = (f32[1,1024,128]{2,1,0:T(8,128)S(1)}) conditional(s32[]{:T(128)} %bitcast.18, () %tuple.35, (s32[1,2]{1,0:T(1,128)S(1)}, f32[2,1024,1024]{2,1,0:T(8,128)}, f32[32,128,1024]{2,1,0:T(8,128)}) %tuple.36), branch_computations={%region_1.1_spmd, %region_2.2_spmd} | conditional | flops 1610612736 | bytes 5243466 | solution.py:23
  525.8 5.3 fusion.3
  531.1 0.8 constant_dynamic-update-slice_fusion.2
  533.0 8.3 %conditional.2 = (f32[1,1024,128]{2,1,0:T(8,128)S(1)}) conditional(s32[]{:T(128)} %bitcast.18, () %tuple.35, (s32[1,2]{1,0:T(1,128)S(1)}, f32[2,1024,1024]{2,1,0:T(8,128)}, f32[32,128,1024]{2,1,0:T(8,128)}) %tuple.36), branch_computations={%region_1.1_spmd, %region_2.2_spmd} | conditional | flops 1610612736 | bytes 5243466 | solution.py:23
  536.0 5.3 fusion.3
  541.4 0.8 constant_dynamic-update-slice_fusion.2
  543.3 8.3 %conditional.2 = (f32[1,1024,128]{2,1,0:T(8,128)S(1)}) conditional(s32[]{:T(128)} %bitcast.18, () %tuple.35, (s32[1,2]{1,0:T(1,128)S(1)}, f32[2,1024,1024]{2,1,0:T(8,128)}, f32[32,128,1024]{2,1,0:T(8,128)}) %tuple.36), branch_computations={%region_1.1_spmd, %region_2.2_spmd} | conditional | flops 1610612736 | bytes 5243466 | solution.py:23
  546.3 5.3 fusion.3
  551.7 0.8 constant_dynamic-update-slice_fusion.2
  553.6 8.3 %conditional.2 = (f32[1,1024,128]{2,1,0:T(8,128)S(1)}) conditional(s32[]{:T(128)} %bitcast.18, () %tuple.35, (s32[1,2]{1,0:T(1,128)S(1)}, f32[2,1024,1024]{2,1,0:T(8,128)}, f32[32,128,1024]{2,1,0:T(8,128)}) %tuple.36), branch_computations={%region_1.1_spmd, %region_2.2_spmd} | conditional | flops 1610612736 | bytes 5243466 | solution.py:23
  556.6 5.3 fusion.3
  561.9 0.8 constant_dynamic-update-slice_fusion.2
  562.8 12.4 %sub.3 = f32[20,1024,128]{2,1,0:T(8,128)} subtract(f32[20,1024,128]{2,1,0:T(8,128)} %param.10, f32[20,1024,128]{2,1,0:T(8,128)} %get-tuple-element.43) | non-fusion elementwise | flops 2621440 | bytes 31457280 | tf_op jit(solution)/shard_map/sub | solution.py:30
  (72 shorter events, 28.1 us)
Async XLA Ops:
  7.2 58.9 %copy-start = (f32[2,128,1024]{2,1,0:T(8,128)S(1)}, f32[2,128,1024]{2,1,0:T(8,128)}, u32[]{:S(2)}) copy-start(f32[2,128,1024]{2,1,0:T(8,128)} %param.9) | copy-start | bytes 3145732
  7.2 58.9 %all-gather.4.cloned.1.call-start = ((), (), s32[]{:S(2)}) async-start(), calls=%async_computation | async-start | bytes 4456448 | tf_op jit(solution)/shard_map/all_gather | solution.py:14
  7.9 233.0 %all-gather.6.cloned.1.call-start = ((), (), s32[]{:S(2)}) async-start(), calls=%async_computation.1 | async-start | bytes 9437184 | tf_op jit(solution)/shard_map/all_gather | solution.py:18
  73.0 284.0 %all-gather.8.cloned.1.call-start = ((), (), s32[]{:S(2)}) async-start(), calls=%async_computation.2 | async-start | bytes 17825792 | tf_op jit(solution)/shard_map/all_gather | solution.py:19
Sparse Core Ops, SparseCore 0:
  10.5 55.5 all-gather.3
  73.1 167.7 all-gather.5
  244.0 112.9 all-gather.7
where the time goes:
time: 583 us; the launch traced here: 582 us
  waiting for transfers between devices  342 us (59%)
  matrix products  113 us (19%)
  loops' own time  58.7 us (10%)
  local copies, waits for them, and re-layouts  41.6 us (7%)
  between operations  13.8 us (2%)
  other arithmetic  12.4 us (2%)
    all_gather x1, waiting for transfers between devices, per_device(): whole_tiles = lax.all_gather(solved, 'col', axis=1, tiled=True)  166 us
    all_gather x1, waiting for transfers between devices, per_device(): slices = lax.all_gather(solved, 'row', axis=0, tiled=True)  116 us
    dot_general x20, matrix products, slot_term(): return jnp.einsum('ak,bk->ab', left_tile, right_rows, precision=highest)  106 us
    all_gather x1, waiting for transfers between devices, per_device(): full_pivot = lax.all_gather(pivot_inverse, 'row', axis=0, tiled=True)  58.1 us
    another operation x20, loops' own time, owner_slot(): lax.cond(listed[1] >= 0, lambda: slot_term(whole_tiles[listed[0]], slices...  47 us
    dynamic_update_slice x20, local copies, waits for them, and re-layouts, per_device(): updates = lax.map(owner_slot, tile_list)  16.7 us
    slice x20, local copies, waits for them, and re-layouts, owner_slot(): listed[1]  12.9 us
    sub x1, other arithmetic, per_device(): return (solved, trailing - updates)  12.4 us
  transfers between devices with their start and end apart: 3, of which 3 were waited for; matrix products, arithmetic and copies ran while one was open for 0% of the time, Pallas kernels for 0%

commit v1 on v0

v1 whole, which is shorter than its diff:
```python
import functools

import jax
import jax.numpy as jnp
from jax import lax
from jax.experimental import pallas as pl
from jax.experimental.pallas import tpu as pltpu
from jax.sharding import PartitionSpec as P

SLOTS = 20
ROWS = 128
ORDER = 1024
AXES = ("row", "col")
high = lax.Precision.HIGH


def place(index):
    row, col = divmod(index, 8)
    return col // 2, (row // 8) * 2 + col % 2, (row // 2) % 4, row % 2


def index_of(x, y, z, core):
    return (((y // 2) * 4 + z) * 2 + core) * 8 + x * 2 + y % 2


def send(value, move):
    pairs = [(i, index_of(*move(*place(i)))) for i in range(128)]
    return lax.ppermute(value, AXES, pairs)


def to_sibling(x, y, z, core):
    return x, y, z, 1 - core


def along_z(x, y, z, core):
    return x, y, (z + 1 - 2 * core) % 4, core


def along_x(x, y, z, core):
    return (x + 1 - 2 * core) % 4, y, z, core


def far_y(x, y, z, core):
    return x, (y + 2) % 4, z, core


def near_y(x, y, z, core):
    return x, y ^ 1, z, core


def gather_pivot(rows):
    swap = functools.partial(send, move=to_sibling)
    far = send(rows, far_y)
    pair = jnp.concatenate([rows, far], 0)
    chip = jnp.concatenate([pair, swap(pair)], 0)
    z1 = send(chip, along_z)
    z2 = send(z1[:128], along_z)
    sz1 = swap(z1)
    sz2 = swap(z2)
    return chip, z1, sz1, z2, sz2


def pivot_whole(parts, far, z, core):
    chip, z1, sz1, z2, sz2 = parts
    order = jnp.concatenate([chip, z1, sz1, z2, sz2], 0).reshape(16, 64, ORDER)
    block = jnp.arange(16, dtype=jnp.int32)
    block_far, block_z, block_core = block // 8, (block // 2) % 4, block % 2
    near = (block_far != far).astype(jnp.int32)
    dz = (block_z - z) % 4
    other = (block_core != core).astype(jnp.int32)
    mine = jnp.where(core == 0, dz == 3, dz == 1)
    at = jnp.where(
        dz == 0,
        near + 2 * other,
        jnp.where(
            dz == 2,
            12 + near + 2 * other,
            jnp.where(mine, 4 + near + 2 * other, 8 + near + 2 * (1 - other)),
        ),
    )
    return order[at].reshape(ORDER, ORDER)


def update_kernel(order, left, buffer, position, live, rows_at, *refs):
    trailing, hi_own, lo_own, hi_far, lo_far = refs[:5]
    sources = refs[5:17]
    out = refs[17]
    slab, sems = refs[18:]
    step = pl.program_id(0)

    def fetch(at):
        half = at % 2
        for which, source in enumerate(sources):
            @pl.when(buffer[at] == which)
            def _():
                pltpu.make_async_copy(source.at[position[at]], slab.at[half], sems.at[half]).start()

    @pl.when(jnp.logical_and(step == 0, live[0] == 1))
    def _():
        fetch(0)

    after = jnp.minimum(step + 1, SLOTS - 1)

    @pl.when(jnp.logical_and(step + 1 < SLOTS, live[after] == 1))
    def _():
        fetch(after)

    @pl.when(live[step] == 1)
    def _():
        half = step % 2
        pltpu.make_async_copy(sources[0].at[0], slab.at[half], sems.at[half]).wait()
        right = slab[half]
        right_hi = right.astype(jnp.bfloat16)
        right_lo = (right - right_hi.astype(jnp.float32)).astype(jnp.bfloat16)
        both = jnp.concatenate([right_hi, right_lo], 0)
        dims = (((1,), (1,)), ((), ()))
        for base, (hi, lo) in enumerate(((hi_own, lo_own), (hi_far, lo_far))):
            term = lax.dot_general(hi[0], both, dims, preferred_element_type=jnp.float32)
            term += lax.dot_general(lo[0], both, dims, preferred_element_type=jnp.float32)
            total = term[:, :ROWS] + term[:, ROWS:]
            for j in range(4):
                at = pl.ds(pl.multiple_of(rows_at[base * 4 + j], ROWS), ROWS)
                out[0, at, :] = trailing[0, at, :] - total[j * ROWS : (j + 1) * ROWS]

    @pl.when(live[step] == 0)
    def _():
        out[...] = trailing[...]


def update(trailing, lefts, sources, tables):
    def slot(step, order, *_):
        return order[step], 0, 0

    def tile(step, order, left, *_):
        return left[step], 0, 0

    slot_spec = pl.BlockSpec((1, ORDER, ROWS), slot)
    left_spec = pl.BlockSpec((1, ORDER // 2, ORDER), tile)
    return pl.pallas_call(
        update_kernel,
        grid_spec=pltpu.PrefetchScalarGridSpec(
            num_scalar_prefetch=6,
            grid=(SLOTS,),
            in_specs=[slot_spec] + [left_spec] * 4 + [pl.BlockSpec(memory_space=pl.ANY)] * 12,
            out_specs=slot_spec,
            scratch_shapes=[pltpu.VMEM((2, ROWS, ORDER), jnp.float32), pltpu.SemaphoreType.DMA((2,))],
        ),
        out_shape=jax.ShapeDtypeStruct(trailing.shape, trailing.dtype),
        compiler_params=pltpu.CompilerParams(vmem_limit_bytes=48 << 20),
    )(*tables, trailing, *lefts, *sources)


def halves(blocks, square):
    stacked = jnp.stack(blocks, 1)
    product = jnp.einsum("pxak,kj->pxaj", stacked, square, precision=high)
    top = lax.reduce_precision(product, 8, 7)
    flat = (2, 4 * ROWS, ORDER)
    return top.astype(jnp.bfloat16).reshape(flat), (product - top).astype(jnp.bfloat16).reshape(flat)


def per_device(pivot_inverse, panel, trailing, tile_list):
    row, col = lax.axis_index("row"), lax.axis_index("col")
    far, z, core = row // 8, (row // 2) % 4, row % 2
    x, near = col // 2, col % 2
    swap = functools.partial(send, move=to_sibling)

    sib = swap(panel)
    chip = jnp.concatenate([panel, sib], 0)
    near_own = send(panel, near_y)
    x1 = send(chip, along_x)
    pivot_parts = gather_pivot(pivot_inverse)
    z1 = send(chip, along_z)
    near_chip = jnp.concatenate([near_own, swap(near_own)], 0)
    far_own = send(panel, far_y)
    x2 = send(x1[:2], along_x)
    sx1 = swap(x1[2:])
    nx1 = send(near_chip, along_x)
    z2 = send(z1[:2], along_z)
    sz1 = swap(z1)
    far_sib = swap(far_own)
    far_chip = jnp.concatenate([far_own, far_sib], 0)
    fz1 = send(far_chip, along_z)
    nx2 = send(nx1[:2], along_x)
    nsx1 = swap(nx1[2:])
    sz2 = swap(z2)
    fz2 = send(z2, far_y)
    sfz1 = swap(fz1)
    sfz2 = swap(fz2)

    full_pivot = pivot_whole(pivot_parts, far, z, core)
    solved = jnp.einsum("pak,jk->paj", panel, full_pivot, precision=high)
    square = jnp.einsum("ki,kj->ij", full_pivot, full_pivot, precision=high)
    lefts = halves([panel, x1[:2], sx1, x2], square) + halves([near_own, nx1[:2], nsx1, nx2], square)
    toward = jnp.where(core == 0, -1, 1)
    shifts = jnp.stack([x, (x + toward) % 4, (x - toward) % 4, (x + 2) % 4])
    rows_at = jnp.concatenate([(shifts * 2 + near) * ROWS, (shifts * 2 + 1 - near) * ROWS]).astype(jnp.int32)

    left, right = tile_list[:, 0], tile_list[:, 1]
    live = right >= 0
    key = jnp.where(live, left, 2) * SLOTS + jnp.arange(SLOTS, dtype=jnp.int32)
    rank = jnp.sum((key[None, :] < key[:, None]).astype(jnp.int32), 1)
    pick = (rank[None, :] == jnp.arange(SLOTS, dtype=jnp.int32)[:, None]).astype(jnp.int32)
    order = jnp.sum(pick * jnp.arange(SLOTS, dtype=jnp.int32)[None, :], 1)
    left = jnp.sum(pick * jnp.where(live, left, 1)[None, :], 1)
    right = jnp.sum(pick * jnp.maximum(right, 0)[None, :], 1)
    live = jnp.sum(pick * live.astype(jnp.int32)[None, :], 1)
    inner, owner = right % 2, right // 2
    owner_far, owner_z, owner_core = owner // 8, (owner // 2) % 4, owner % 2
    dz = (owner_z - z) % 4
    other = (owner_core != core).astype(jnp.int32)
    mine = jnp.where(core == 0, dz == 3, dz == 1)
    buffer = jnp.where(dz == 0, other, jnp.where(dz == 2, 2 + other, jnp.where(mine, 4, 5)))
    buffer = buffer + jnp.where(owner_far != far, 6, 0)
    position = inner + jnp.where(dz % 2 == 0, 0, 2 * jnp.where(mine, other, 1 - other))

    sources = [panel, sib, z2, sz2, z1, sz1, far_own, far_sib, fz2, sfz2, fz1, sfz1]
    tables = [t.astype(jnp.int32) for t in (order, left, buffer, position, live)] + [rows_at]
    return solved, update(trailing, lefts, sources, tables)


def solution(mesh):
    placed = (P("row", None), P("row", "col", None), P("row", None, "col"), P("row", None))
    return jax.shard_map(
        per_device,
        mesh=mesh,
        in_specs=placed,
        out_specs=(P("row", "col", None), P("row", None, "col")),
        check_vma=False,
    )
```

time: 583 us -> 210 us (0.36)
  waiting for transfers between devices: 342 us -> 66.8 us
  matrix products: 113 us -> 32.3 us
  loops' own time: 58.7 us -> 0 us
  Pallas kernels: 0 us -> 35.8 us
  starting transfers between devices: 0.12 us -> 32.4 us
  between operations: 13.8 us -> 1 us
  local copies, waits for them, and re-layouts: 41.6 us -> 31.7 us
    all_gather x3 -> x0, waiting for transfers between devices: 341 us -> none  [the longest x1 166 us: per_device(): whole_tiles = lax.all_gather(solved, 'col', axis=1, tiled=True)]
    dot_general x21 -> x4, matrix products: 113 us -> 32.3 us  [the longest x2 21.2 us: halves(): product = jnp.einsum('pxak,kj->pxaj', stacked, square, precision=high)]
    ppermute x0 -> x25, waiting for transfers between devices: none -> 66.8 us  [send(): return lax.ppermute(value, AXES, pairs)]
    another operation x21 -> x0, loops' own time: 58.7 us -> none  [the longest x20 47 us: owner_slot(): lax.cond(listed[1] >= 0, lambda: slot_term(whole_tiles[listed[0]], slices...]
    pallas_call x0 -> x1, Pallas kernels: none -> 35.8 us  [update(): pl.pallas_call(update_kernel, grid_spec=pltpu.PrefetchScalarGridSpec(num_...]
    ppermute x0 -> x25, starting transfers between devices: none -> 32.4 us  [send(): return lax.ppermute(value, AXES, pairs)]
    slice x40 -> x2, local copies, waits for them, and re-layouts: 24.1 us -> 3.46 us  [the longest x1 2.35 us: per_device(): z2 = send(z1[:2], along_z)]
    dynamic_update_slice x20 -> x0, local copies, waits for them, and re-layouts: 16.7 us -> none  [per_device(): updates = lax.map(owner_slot, tile_list)]
  transfers between devices with their start and end apart: 3 -> 25, of which waited for: 3 -> 5; matrix products, arithmetic and copies ran while one was open for 0% -> 34% of each run, Pallas kernels for 0% -> 0%
where the time goes in v1:
time: 210 us; the launch traced here: 209 us
  waiting for transfers between devices  66.8 us (32%)
  Pallas kernels  35.8 us (17%)
  starting transfers between devices  32.4 us (15%)
  matrix products  32.3 us (15%)
  local copies, waits for them, and re-layouts  31.7 us (15%)
  other arithmetic  9.45 us (4%)
    ppermute x25, waiting for transfers between devices, send(): return lax.ppermute(value, AXES, pairs)  66.8 us
    pallas_call x1, Pallas kernels, update(): pl.pallas_call(update_kernel, grid_spec=pltpu.PrefetchScalarGridSpec(num_...  35.8 us
    ppermute x25, starting transfers between devices, send(): return lax.ppermute(value, AXES, pairs)  32.4 us
    dot_general x2, matrix products, halves(): product = jnp.einsum('pxak,kj->pxaj', stacked, square, precision=high)  21.2 us
    unnamed x32, local copies, waits for them, and re-layouts  14.4 us
    dot_general x1, matrix products, per_device(): square = jnp.einsum('ki,kj->ij', full_pivot, full_pivot, precision=high)  8.24 us
    another operation x2, local copies, waits for them, and re-layouts, halves(): stacked = jnp.stack(blocks, 1)  6.92 us
    gather x1, local copies, waits for them, and re-layouts, pivot_whole(): return order[at].reshape(ORDER, ORDER)  4.95 us
  transfers between devices with their start and end apart: 25, of which 5 were waited for; matrix products, arithmetic and copies ran while one was open for 34% of the time, Pallas kernels for 0%

profile of v1, /device:TPU:17, one launch (start us, length us, event | category | flops | bytes accessed | tf_op | source)
XLA Modules:
  0.0 209.4 jit_solution(9888317232919582416)
XLA Ops:
  0.6 0.0 copy-start.5
  0.7 0.8 collective-permute-start.6
  1.4 1.0 collective-permute-start.10
  2.4 0.3 collective-permute-start
  2.8 2.6 %collective-permute-start.19 = (f32[2,128,1024]{2,1,0:T(8,128)}, f32[2,128,1024]{2,1,0:T(8,128)S(1)}, u32[]{:S(2)}, u32[]{:S(2)}) collective-permute-start(f32[2,128,1024]{2,1,0:T(8,128)} %refs_5_.1), channel_id=1, source_target_pairs={{0,64},{1,65},{2,66},{3,67},{4,68},{5,69},{6,70},{7,71},{8,72},{9,... | collective-permute-start | bytes 3145736 | tf_op jit(solution)/shard_map/ppermute | solution.py:28
  5.4 2.4 %constant_dynamic-update-slice_fusion.8 = f32[4,128,1024]{2,1,0:T(8,128)} fusion(f32[2,128,1024]{2,1,0:T(8,128)} %refs_5_.1), kind=kLoop, calls=%fused_computation.33 | loop fusion | bytes 2097152
  7.8 24.1 %collective-permute-done = f32[64,1024]{1,0:T(8,128)S(1)} collective-permute-done((f32[64,1024]{1,0:T(8,128)}, f32[64,1024]{1,0:T(8,128)S(1)}, u32[]{:S(2)}, u32[]{:S(2)}) %collective-permute-start) | collective-permute-done | bytes 262176 | tf_op jit(solution)/shard_map/ppermute | solution.py:28
  31.8 1.9 pad_maximum_fusion.4
  33.7 1.3 collective-permute-start.1
  35.1 1.1 constant_dynamic-update-slice_fusion.7
  36.2 3.8 %collective-permute-start.15 = (f32[4,128,1024]{2,1,0:T(8,128)}, f32[4,128,1024]{2,1,0:T(8,128)}, u32[]{:S(2)}, u32[]{:S(2)}) collective-permute-start(f32[4,128,1024]{2,1,0:T(8,128)} %constant_dynamic-update-slice_fusion.7), channel_id=1, source_target_pairs={{0,16},{1,17},{2,18},{3,19},{4,20},{5,21},{6,22},{7,23},{8,56},{9,... | collective-permute-start | bytes 6291464 | tf_op jit(solution)/shard_map/ppermute | solution.py:28
  39.9 0.0 collective-permute-done.10
  39.9 0.1 collective-permute-start.11
  40.0 2.5 %collective-permute-start.7 = (f32[4,128,1024]{2,1,0:T(8,128)}, f32[4,128,1024]{2,1,0:T(8,128)}, u32[]{:S(2)}, u32[]{:S(2)}) collective-permute-start(f32[4,128,1024]{2,1,0:T(8,128)} %constant_dynamic-update-slice_fusion.7), channel_id=1, source_target_pairs={{0,2},{1,3},{2,4},{3,5},{4,6},{5,7},{6,0},{7,1},{8,14},{9,15},{10,... | collective-permute-start | bytes 6291464 | tf_op jit(solution)/shard_map/ppermute | solution.py:28
  42.6 0.7 constant_dynamic-update-slice_fusion.6
  43.3 11.1 %collective-permute-done.19.refs_11_ = f32[2,128,1024]{2,1,0:T(8,128)S(1)} collective-permute-done((f32[2,128,1024]{2,1,0:T(8,128)}, f32[2,128,1024]{2,1,0:T(8,128)S(1)}, u32[]{:S(2)}, u32[]{:S(2)}) %collective-permute-start.19) | collective-permute-done | bytes 1048608 | tf_op jit(solution)/shard_map/ppermute | solution.py:28
  54.4 0.8 collective-permute-start.20
  55.2 0.2 convert_reduce_fusion
  55.4 2.2 %pad_maximum_fusion.3 = f32[256,1024]{1,0:T(8,128)} fusion(f32[128,1024]{1,0:T(8,128)} %collective-permute-done.1, f32[64,1024]{1,0:T(8,128)} %copy-done.6, f32[64,1024]{1,0:T(8,128)S(1)} %copy-done.5), kind=kLoop, calls=%fused_computation.23 | loop fusion | flops 524288 | bytes 2097152 | tf_op jit(solution)/shard_map/concatenate | solution.py:55
  57.6 3.8 %collective-permute-start.2 = (f32[256,1024]{1,0:T(8,128)}, f32[256,1024]{1,0:T(8,128)}, u32[]{:S(2)}, u32[]{:S(2)}) collective-permute-start(f32[256,1024]{1,0:T(8,128)} %pad_maximum_fusion.3), channel_id=1, source_target_pairs={{0,16},{1,17},{2,18},{3,19},{4,20},{5,21},{6,22},{7,23},{8,56},{9,... | collective-permute-start | bytes 3145736 | tf_op jit(solution)/shard_map/ppermute | solution.py:28
  61.3 0.1 add_multiply_fusion.1
  61.4 0.0 collective-permute-done.11
  61.4 3.1 %pad_maximum_fusion.1 = f32[4,128,1024]{2,1,0:T(8,128)} fusion(f32[2,128,1024]{2,1,0:T(8,128)} %collective-permute-done.11, f32[2,128,1024]{2,1,0:T(8,128)} %collective-permute-done.10), kind=kLoop, calls=%fused_computation.20 | loop fusion | flops 524288 | bytes 4194304 | tf_op jit(solution)/shard_map/concatenate | solution.py:173
  64.5 2.5 %collective-permute-start.12 = (f32[4,128,1024]{2,1,0:T(8,128)}, f32[4,128,1024]{2,1,0:T(8,128)}, u32[]{:S(2)}, u32[]{:S(2)}) collective-permute-start(f32[4,128,1024]{2,1,0:T(8,128)} %pad_maximum_fusion.1), channel_id=1, source_target_pairs={{0,2},{1,3},{2,4},{3,5},{4,6},{5,7},{6,0},{7,1},{8,14},{9,15},{10,... | collective-permute-start | bytes 6291464 | tf_op jit(solution)/shard_map/ppermute | solution.py:28
  67.0 0.1 select_reduce_fusion
  67.2 1.7 pad_maximum_fusion.2
  68.8 0.1 collective-permute-start.23
  69.0 5.5 %collective-permute-done.2 = f32[256,1024]{1,0:T(8,128)} collective-permute-done((f32[256,1024]{1,0:T(8,128)}, f32[256,1024]{1,0:T(8,128)}, u32[]{:S(2)}, u32[]{:S(2)}) %collective-permute-start.2) | collective-permute-done | bytes 1048608 | tf_op jit(solution)/shard_map/ppermute | solution.py:28
  74.4 1.3 collective-permute-start.3
  75.8 1.1 slice.36
  76.9 0.0 collective-permute-done.15.refs_9_
  77.0 2.2 %collective-permute-start.4 = (f32[128,1024]{1,0:T(8,128)S(1)}, f32[128,1024]{1,0:T(8,128)S(1)}, u32[]{:S(2)}, u32[]{:S(2)}) collective-permute-start(f32[128,1024]{1,0:T(8,128)S(1)} %slice.36), channel_id=1, source_target_pairs={{0,16},{1,17},{2,18},{3,19},{4,20},{5,21},{6,22},{7,23},{8,56},{9,... | collective-permute-start | bytes 1572872 | tf_op jit(solution)/shard_map/ppermute | solution.py:28
  79.1 0.1 pad_add_fusion.rows_at
  79.2 2.3 %slice.41 = f32[2,128,1024]{2,1,0:T(8,128)} slice(f32[4,128,1024]{2,1,0:T(8,128)} %collective-permute-done.15.refs_9_), slice={[0:2], [0:128], [0:1024]} | slice | bytes 2097152 | tf_op jit(solution)/shard_map/slice | solution.py:178
  81.6 0.0 collective-permute-start.16
  81.6 3.5 %slice_bitcast_fusion.1 = (f32[2,1,128,1024]{3,2,0,1:T(8,128)}, f32[2,128,1024]{2,1,0:T(8,128)}, f32[2,128,1024]{2,1,0:T(8,128)}) fusion(f32[4,128,1024]{2,1,0:T(8,128)} %collective-permute-done.7), kind=kLoop, calls=%fused_computation.119 | loop fusion | bytes 5242880 | tf_op jit(solution)/shard_map/stack | solution.py:154
  85.1 17.4 %collective-permute-done.4 = f32[128,1024]{1,0:T(8,128)S(1)} collective-permute-done((f32[128,1024]{1,0:T(8,128)S(1)}, f32[128,1024]{1,0:T(8,128)S(1)}, u32[]{:S(2)}, u32[]{:S(2)}) %collective-permute-start.4) | collective-permute-done | bytes 524320 | tf_op jit(solution)/shard_map/ppermute | solution.py:28
  102.4 1.3 collective-permute-start.8
  103.8 0.7 constant_dynamic-update-slice_fusion.5
  104.5 0.0 collective-permute-start.5
  104.5 1.9 constant_dynamic-update-slice_fusion.4
  106.4 2.3 %constant_dynamic-update-slice_fusion.3 = f32[1024,1024]{1,0:T(8,128)} fusion(f32[1024,1024]{1,0:T(8,128)} %constant_dynamic-update-slice_fusion.4, f32[256,1024]{1,0:T(8,128)} %collective-permute-done.2), kind=kLoop, calls=%fused_computation.28 | loop fusion | bytes 2097152
  108.7 1.0 constant_dynamic-update-slice_fusion.2
  109.7 0.8 constant_dynamic-update-slice_fusion.1
  110.5 0.8 constant_dynamic-update-slice_fusion
  111.4 5.0 %gather_fusion = f32[16,64,1024]{2,1,0:T(8,128)} fusion(f32[16,64,1024]{2,1,0:T(8,128)} %bitcast, s32[1024]{0:T(1024)S(1)} %pad_clamp_fusion), kind=kCustom, calls=%fused_computation | custom fusion | bytes 8388672 | tf_op jit(solution)/shard_map/gather | solution.py:81
  116.3 2.5 %collective-permute-start.9 = (f32[2,128,1024]{2,1,0:T(8,128)}, f32[2,128,1024]{2,1,0:T(8,128)}, u32[]{:S(2)}, u32[]{:S(2)}) collective-permute-start(f32[2,128,1024]{2,1,0:T(8,128)} %get-tuple-element.25), channel_id=1, source_target_pairs={{0,2},{1,3},{2,4},{3,5},{4,6},{5,7},{6,0},{7,1},{8,14},{9,15},{10,... | collective-permute-start | bytes 3145736 | tf_op jit(solution)/shard_map/ppermute | solution.py:28
  118.8 3.5 %slice_bitcast_fusion = (f32[2,1,128,1024]{3,2,1,0:T(8,128)}, f32[2,128,1024]{2,1,0:T(8,128)}, f32[2,128,1024]{2,1,0:T(8,128)}) fusion(f32[4,128,1024]{2,1,0:T(8,128)} %collective-permute-done.12), kind=kLoop, calls=%fused_computation.118 | loop fusion | bytes 5242880 | tf_op jit(solution)/shard_map/stack | solution.py:154
  122.3 1.0 copy-done.1
  123.3 0.5 collective-permute-start.13
  123.8 2.6 %collective-permute-start.21 = (f32[2,128,1024]{2,1,0:T(8,128)}, f32[2,128,1024]{2,1,0:T(8,128)}, u32[]{:S(2)}, u32[]{:S(2)}) collective-permute-start(f32[2,128,1024]{2,1,0:T(8,128)} %copy-done.1), channel_id=1, source_target_pairs={{0,64},{1,65},{2,66},{3,67},{4,68},{5,69},{6,70},{7,71},{8,72},{9,... | collective-permute-start | bytes 3145736 | tf_op jit(solution)/shard_map/ppermute | solution.py:28
  126.4 0.4 collective-permute-start.24
  126.8 8.2 %fusion.29 = f32[1024,1024,1]{1,0,2:T(8,128)} fusion(f32[16,64,1024]{2,1,0:T(8,128)S(1)} %copy-done.3), kind=kOutput, calls=%fused_computation.120 | convolution fusion | flops 6442450944 | bytes 8388608 | tf_op jit(solution)/shard_map/ki,kj->ij/dot_general | solution.py:192
  135.0 1.2 collective-permute-start.14
  136.2 2.9 %convolution_bitcast_fusion = f32[2,128,1024]{1,2,0:T(8,128)} fusion(f32[1024,1024,1]{1,0,2:T(8,128)S(1)} %bitcast.60, f32[2,128,1024]{2,1,0:T(8,128)S(1)} %copy-done), kind=kOutput, calls=%fused_computation.22 | convolution fusion | flops 1610612736 | bytes 6291456 | tf_op jit(solution)/shard_map/pak,jk->paj/dot_general | solution.py:191
  139.1 2.5 %copy.15 = f32[2,128,1024]{2,1,0:T(8,128)} copy(f32[2,128,1024]{1,2,0:T(8,128)} %convolution_bitcast_fusion) | data formatting | bytes 2097152
  141.6 8.7 %collective-permute-done.21.refs_13_ = f32[2,128,1024]{2,1,0:T(8,128)} collective-permute-done((f32[2,128,1024]{2,1,0:T(8,128)}, f32[2,128,1024]{2,1,0:T(8,128)}, u32[]{:S(2)}, u32[]{:S(2)}) %collective-permute-start.21) | collective-permute-done | bytes 1048608 | tf_op jit(solution)/shard_map/ppermute | solution.py:28
  150.3 0.9 collective-permute-start.17
  151.2 0.0 collective-permute-start.22
  151.2 0.0 copy-start.11
  151.2 11.1 %fusion = (bf16[2,4,128,1024]{3,2,1,0:T(8,128)(2,1)}, bf16[2,4,128,1024]{3,2,1,0:T(8,128)(2,1)}) fusion(f32[1024,1024,1]{1,0,2:T(8,128)} %fusion.29, f32[2,1,128,1024]{3,2,0,1:T(8,128)} %bitcast.17, f32[2,1,128,1024]{3,2,0,1:T(8,128)} %bitcast.16, f32[2,1,128,1024]{3,2,0,1:T(8,128)} %get-tuple-element.23, f32[2,1,128,1024]{3,2,0,1:T(8,128)S(1)} %bitcast.59), kind=kOutput, calls=%fused_computation.5 | convolution fusion | flops 6449790976 | bytes 12582912 | tf_op jit(solution)/shard_map/pxak,kj->pxaj/dot_general | solution.py:155
  162.3 10.1 %fusion.1 = (bf16[2,4,128,1024]{3,2,1,0:T(8,128)(2,1)}, bf16[2,4,128,1024]{3,2,1,0:T(8,128)(2,1)}) fusion(f32[1024,1024,1]{1,0,2:T(8,128)S(1)} %copy-done.11, f32[2,1,128,1024]{3,2,1,0:T(8,128)} %bitcast.29, f32[2,1,128,1024]{3,2,1,0:T(8,128)} %bitcast.28, f32[2,1,128,1024]{3,2,1,0:T(8,128)S(1)} %copy-done.8, f32[2,1,128,1024]{3,2,1,0:T(8,128)} %bitcast.24), kind=kOutput, calls=%fused_computation.6 | convolution fusion | flops 6449790976 | bytes 12582912 | tf_op jit(solution)/shard_map/pxak,kj->pxaj/dot_general | solution.py:155
  172.5 1.0 copy-done.9
  173.5 35.8 %shard_map.59 = f32[20,1024,128]{2,1,0:T(8,128)} custom-call(s32[20]{0:T(128)S(1)} %get-tuple-element.9.order, s32[20]{0:T(128)S(1)} %get-tuple-element.8.left, s32[20]{0:T(128)S(1)} %fusion.21.buffer, s32[20]{0:T(128)S(1)} %get-tuple-element.12.position, s32[20]{0:T(128)S(1)} %get-tuple-element.6.live, s32[8]{0:T(128)S(1)} %pad_add_fusion.rows_at, ...), custom_call_target="tpu_custom_call" | custom-call | tf_op jit(solution)/shard_map/pallas_call | solution.py:139
  (46 shorter events, 0.2 us)
Async XLA Ops:
  0.6 42.0 %copy-start.5 = (f32[64,1024]{1,0:T(8,128)S(1)}, f32[64,1024]{1,0:T(8,128)}, u32[]{:S(2)}) copy-start(f32[64,1024]{1,0:T(8,128)} %param.4) | copy-start | bytes 786436
  0.6 39.3 %copy-start.10 = (s32[20,2]{0,1:T(2,128)S(1)}, s32[20,2]{0,1:T(2,128)}, u32[]{:S(2)}) copy-start(s32[20,2]{0,1:T(2,128)} %param.7) | copy-start | bytes 484
  0.7 34.4 %collective-permute-start.6 = (f32[2,128,1024]{2,1,0:T(8,128)}, f32[2,128,1024]{2,1,0:T(8,128)S(1)}, u32[]{:S(2)}, u32[]{:S(2)}) collective-permute-start(f32[2,128,1024]{2,1,0:T(8,128)} %refs_5_.1), channel_id=1, source_target_pairs={{0,8},{1,9},{2,10},{3,11},{4,12},{5,13},{6,14},{7,15},{8,0},{9,1},... | collective-permute-start | bytes 3145736 | tf_op jit(solution)/shard_map/ppermute | solution.py:28
  1.4 38.5 %collective-permute-start.10 = (f32[2,128,1024]{2,1,0:T(8,128)}, f32[2,128,1024]{2,1,0:T(8,128)}, u32[]{:S(2)}, u32[]{:S(2)}) collective-permute-start(f32[2,128,1024]{2,1,0:T(8,128)} %refs_5_.1), channel_id=1, source_target_pairs={{0,1},{1,0},{2,3},{3,2},{4,5},{5,4},{6,7},{7,6},{8,9},{9,8},{10,11... | collective-permute-start | bytes 3145736 | tf_op jit(solution)/shard_map/ppermute | solution.py:28
  2.4 29.4 %collective-permute-start = (f32[64,1024]{1,0:T(8,128)}, f32[64,1024]{1,0:T(8,128)S(1)}, u32[]{:S(2)}, u32[]{:S(2)}) collective-permute-start(f32[64,1024]{1,0:T(8,128)} %param.4), channel_id=1, source_target_pairs={{0,64},{1,65},{2,66},{3,67},{4,68},{5,69},{6,70},{7,71},{8,72},{9,... | collective-permute-start | bytes 786440 | tf_op jit(solution)/shard_map/ppermute | solution.py:28
  2.8 51.6 %collective-permute-start.19 = (f32[2,128,1024]{2,1,0:T(8,128)}, f32[2,128,1024]{2,1,0:T(8,128)S(1)}, u32[]{:S(2)}, u32[]{:S(2)}) collective-permute-start(f32[2,128,1024]{2,1,0:T(8,128)} %refs_5_.1), channel_id=1, source_target_pairs={{0,64},{1,65},{2,66},{3,67},{4,68},{5,69},{6,70},{7,71},{8,72},{9,... | collective-permute-start | bytes 3145736 | tf_op jit(solution)/shard_map/ppermute | solution.py:28
  31.8 3.2 %copy-start.6 = (f32[64,1024]{1,0:T(8,128)}, f32[64,1024]{1,0:T(8,128)S(1)}, u32[]{:S(2)}) copy-start(f32[64,1024]{1,0:T(8,128)S(1)} %collective-permute-done) | copy-start | bytes 786436
  33.7 21.6 %collective-permute-start.1 = (f32[128,1024]{1,0:T(8,128)}, f32[128,1024]{1,0:T(8,128)}, u32[]{:S(2)}, u32[]{:S(2)}) collective-permute-start(f32[128,1024]{1,0:T(8,128)} %pad_maximum_fusion.4), channel_id=1, source_target_pairs={{0,8},{1,9},{2,10},{3,11},{4,12},{5,13},{6,14},{7,15},{8,0},{9,1},... | collective-permute-start | bytes 1572872 | tf_op jit(solution)/shard_map/ppermute | solution.py:28
  36.2 40.8 %collective-permute-start.15 = (f32[4,128,1024]{2,1,0:T(8,128)}, f32[4,128,1024]{2,1,0:T(8,128)}, u32[]{:S(2)}, u32[]{:S(2)}) collective-permute-start(f32[4,128,1024]{2,1,0:T(8,128)} %constant_dynamic-update-slice_fusion.7), channel_id=1, source_target_pairs={{0,16},{1,17},{2,18},{3,19},{4,20},{5,21},{6,22},{7,23},{8,56},{9,... | collective-permute-start | bytes 6291464 | tf_op jit(solution)/shard_map/ppermute | solution.py:28
  39.9 21.5 %collective-permute-start.11 = (f32[2,128,1024]{2,1,0:T(8,128)}, f32[2,128,1024]{2,1,0:T(8,128)}, u32[]{:S(2)}, u32[]{:S(2)}) collective-permute-start(f32[2,128,1024]{2,1,0:T(8,128)} %collective-permute-done.10), channel_id=1, source_target_pairs={{0,8},{1,9},{2,10},{3,11},{4,12},{5,13},{6,14},{7,15},{8,0},{9,1},... | collective-permute-start | bytes 3145736 | tf_op jit(solution)/shard_map/ppermute | solution.py:28
  40.0 41.5 %collective-permute-start.7 = (f32[4,128,1024]{2,1,0:T(8,128)}, f32[4,128,1024]{2,1,0:T(8,128)}, u32[]{:S(2)}, u32[]{:S(2)}) collective-permute-start(f32[4,128,1024]{2,1,0:T(8,128)} %constant_dynamic-update-slice_fusion.7), channel_id=1, source_target_pairs={{0,2},{1,3},{2,4},{3,5},{4,6},{5,7},{6,0},{7,1},{8,14},{9,15},{10,... | collective-permute-start | bytes 6291464 | tf_op jit(solution)/shard_map/ppermute | solution.py:28
  54.4 12.7 %collective-permute-start.20 = (f32[2,128,1024]{2,1,0:T(8,128)S(1)}, f32[2,128,1024]{2,1,0:T(8,128)S(1)}, u32[]{:S(2)}, u32[]{:S(2)}) collective-permute-start(f32[2,128,1024]{2,1,0:T(8,128)S(1)} %collective-permute-done.19.refs_11_), channel_id=1, source_target_pairs={{0,8},{1,9},{2,10},{3,11},{4,12},{5,13},{6,14},{7,15},{8,0},{9,1},... | collective-permute-start | bytes 3145736 | tf_op jit(solution)/shard_map/ppermute | solution.py:28
  57.6 16.9 %collective-permute-start.2 = (f32[256,1024]{1,0:T(8,128)}, f32[256,1024]{1,0:T(8,128)}, u32[]{:S(2)}, u32[]{:S(2)}) collective-permute-start(f32[256,1024]{1,0:T(8,128)} %pad_maximum_fusion.3), channel_id=1, source_target_pairs={{0,16},{1,17},{2,18},{3,19},{4,20},{5,21},{6,22},{7,23},{8,56},{9,... | collective-permute-start | bytes 3145736 | tf_op jit(solution)/shard_map/ppermute | solution.py:28
  64.5 54.3 %collective-permute-start.12 = (f32[4,128,1024]{2,1,0:T(8,128)}, f32[4,128,1024]{2,1,0:T(8,128)}, u32[]{:S(2)}, u32[]{:S(2)}) collective-permute-start(f32[4,128,1024]{2,1,0:T(8,128)} %pad_maximum_fusion.1), channel_id=1, source_target_pairs={{0,2},{1,3},{2,4},{3,5},{4,6},{5,7},{6,0},{7,1},{8,14},{9,15},{10,... | collective-permute-start | bytes 6291464 | tf_op jit(solution)/shard_map/ppermute | solution.py:28
  67.2 14.4 %copy-start.4 = (f32[2,128,1024]{2,1,0:T(8,128)}, f32[2,128,1024]{2,1,0:T(8,128)S(1)}, u32[]{:S(2)}) copy-start(f32[2,128,1024]{2,1,0:T(8,128)S(1)} %collective-permute-done.20.refs_12_) | copy-start | bytes 3145732
  68.8 57.6 %collective-permute-start.23 = (f32[4,128,1024]{2,1,0:T(8,128)}, f32[4,128,1024]{2,1,0:T(8,128)}, u32[]{:S(2)}, u32[]{:S(2)}) collective-permute-start(f32[4,128,1024]{2,1,0:T(8,128)} %pad_maximum_fusion.2), channel_id=1, source_target_pairs={{0,16},{1,17},{2,18},{3,19},{4,20},{5,21},{6,22},{7,23},{8,56},{9,... | collective-permute-start | bytes 6291464 | tf_op jit(solution)/shard_map/ppermute | solution.py:28
  74.4 30.0 %collective-permute-start.3 = (f32[256,1024]{1,0:T(8,128)}, f32[256,1024]{1,0:T(8,128)S(1)}, u32[]{:S(2)}, u32[]{:S(2)}) collective-permute-start(f32[256,1024]{1,0:T(8,128)} %collective-permute-done.2), channel_id=1, source_target_pairs={{0,8},{1,9},{2,10},{3,11},{4,12},{5,13},{6,14},{7,15},{8,0},{9,1},... | collective-permute-start | bytes 3145736 | tf_op jit(solution)/shard_map/ppermute | solution.py:28
  75.8 27.9 %copy-start.7 = (f32[64,1024]{1,0:T(8,128)S(1)}, f32[64,1024]{1,0:T(8,128)}, u32[]{:S(2)}) copy-start(f32[64,1024]{1,0:T(8,128)} %copy-done.6) | copy-start | bytes 786436
  77.0 25.5 %collective-permute-start.4 = (f32[128,1024]{1,0:T(8,128)S(1)}, f32[128,1024]{1,0:T(8,128)S(1)}, u32[]{:S(2)}, u32[]{:S(2)}) collective-permute-start(f32[128,1024]{1,0:T(8,128)S(1)} %slice.36), channel_id=1, source_target_pairs={{0,16},{1,17},{2,18},{3,19},{4,20},{5,21},{6,22},{7,23},{8,56},{9,... | collective-permute-start | bytes 1572872 | tf_op jit(solution)/shard_map/ppermute | solution.py:28
  81.6 40.7 %collective-permute-start.16 = (f32[2,128,1024]{2,1,0:T(8,128)}, f32[2,128,1024]{2,1,0:T(8,128)S(1)}, u32[]{:S(2)}, u32[]{:S(2)}) collective-permute-start(f32[2,128,1024]{2,1,0:T(8,128)} %slice.41), channel_id=1, source_target_pairs={{0,16},{1,17},{2,18},{3,19},{4,20},{5,21},{6,22},{7,23},{8,56},{9,... | collective-permute-start | bytes 3145736 | tf_op jit(solution)/shard_map/ppermute | solution.py:28
  102.4 21.4 %collective-permute-start.8 = (f32[2,128,1024]{2,1,0:T(8,128)}, f32[2,128,1024]{2,1,0:T(8,128)}, u32[]{:S(2)}, u32[]{:S(2)}) collective-permute-start(f32[2,128,1024]{2,1,0:T(8,128)} %get-tuple-element.24), channel_id=1, source_target_pairs={{0,8},{1,9},{2,10},{3,11},{4,12},{5,13},{6,14},{7,15},{8,0},{9,1},... | collective-permute-start | bytes 3145736 | tf_op jit(solution)/shard_map/ppermute | solution.py:28
  104.5 6.1 %collective-permute-start.5 = (f32[128,1024]{1,0:T(8,128)S(1)}, f32[128,1024]{1,0:T(8,128)S(1)}, u32[]{:S(2)}, u32[]{:S(2)}) collective-permute-start(f32[128,1024]{1,0:T(8,128)S(1)} %collective-permute-done.4), channel_id=1, source_target_pairs={{0,8},{1,9},{2,10},{3,11},{4,12},{5,13},{6,14},{7,15},{8,0},{9,1},... | collective-permute-start | bytes 1572872 | tf_op jit(solution)/shard_map/ppermute | solution.py:28
  116.3 10.4 %copy-start.3 = (f32[16,64,1024]{2,1,0:T(8,128)S(1)}, f32[16,64,1024]{2,1,0:T(8,128)}, u32[]{:S(2)}) copy-start(f32[16,64,1024]{2,1,0:T(8,128)} %gather_fusion) | copy-start | bytes 12582916
  116.3 18.7 %collective-permute-start.9 = (f32[2,128,1024]{2,1,0:T(8,128)}, f32[2,128,1024]{2,1,0:T(8,128)}, u32[]{:S(2)}, u32[]{:S(2)}) collective-permute-start(f32[2,128,1024]{2,1,0:T(8,128)} %get-tuple-element.25), channel_id=1, source_target_pairs={{0,2},{1,3},{2,4},{3,5},{4,6},{5,7},{6,0},{7,1},{8,14},{9,15},{10,... | collective-permute-start | bytes 3145736 | tf_op jit(solution)/shard_map/ppermute | solution.py:28
  118.8 53.6 %collective-permute-start.18 = (f32[4,128,1024]{2,1,0:T(8,128)}, f32[4,128,1024]{2,1,0:T(8,128)}, u32[]{:S(2)}, u32[]{:S(2)}) collective-permute-start(f32[4,128,1024]{2,1,0:T(8,128)} %collective-permute-done.15.refs_9_), channel_id=1, source_target_pairs={{0,8},{1,9},{2,10},{3,11},{4,12},{5,13},{6,14},{7,15},{8,0},{9,1},... | collective-permute-start | bytes 6291464 | tf_op jit(solution)/shard_map/ppermute | solution.py:28
  122.3 1.0 copy-start.1
  123.3 12.9 %copy-start = (f32[2,128,1024]{2,1,0:T(8,128)S(1)}, f32[2,128,1024]{2,1,0:T(8,128)}, u32[]{:S(2)}) copy-start(f32[2,128,1024]{2,1,0:T(8,128)} %refs_5_.1) | copy-start | bytes 3145732
  123.3 27.9 %collective-permute-start.13 = (f32[2,128,1024]{2,1,0:T(8,128)}, f32[2,128,1024]{2,1,0:T(8,128)}, u32[]{:S(2)}, u32[]{:S(2)}) collective-permute-start(f32[2,128,1024]{2,1,0:T(8,128)} %get-tuple-element.21), channel_id=1, source_target_pairs={{0,8},{1,9},{2,10},{3,11},{4,12},{5,13},{6,14},{7,15},{8,0},{9,1},... | collective-permute-start | bytes 3145736 | tf_op jit(solution)/shard_map/ppermute | solution.py:28
  123.8 26.5 %collective-permute-start.21 = (f32[2,128,1024]{2,1,0:T(8,128)}, f32[2,128,1024]{2,1,0:T(8,128)}, u32[]{:S(2)}, u32[]{:S(2)}) collective-permute-start(f32[2,128,1024]{2,1,0:T(8,128)} %copy-done.1), channel_id=1, source_target_pairs={{0,64},{1,65},{2,66},{3,67},{4,68},{5,69},{6,70},{7,71},{8,72},{9,... | collective-permute-start | bytes 3145736 | tf_op jit(solution)/shard_map/ppermute | solution.py:28
  126.4 46.0 %collective-permute-start.24 = (f32[4,128,1024]{2,1,0:T(8,128)}, f32[4,128,1024]{2,1,0:T(8,128)}, u32[]{:S(2)}, u32[]{:S(2)}) collective-permute-start(f32[4,128,1024]{2,1,0:T(8,128)} %collective-permute-done.23.refs_15_), channel_id=1, source_target_pairs={{0,8},{1,9},{2,10},{3,11},{4,12},{5,13},{6,14},{7,15},{8,0},{9,1},... | collective-permute-start | bytes 6291464 | tf_op jit(solution)/shard_map/ppermute | solution.py:28
  135.0 27.3 %collective-permute-start.14 = (f32[2,128,1024]{2,1,0:T(8,128)}, f32[2,128,1024]{2,1,0:T(8,128)}, u32[]{:S(2)}, u32[]{:S(2)}) collective-permute-start(f32[2,128,1024]{2,1,0:T(8,128)} %get-tuple-element.22), channel_id=1, source_target_pairs={{0,2},{1,3},{2,4},{3,5},{4,6},{5,7},{6,0},{7,1},{8,14},{9,15},{10,... | collective-permute-start | bytes 3145736 | tf_op jit(solution)/shard_map/ppermute | solution.py:28
  150.3 22.1 %collective-permute-start.17 = (f32[2,128,1024]{2,1,0:T(8,128)}, f32[2,128,1024]{2,1,0:T(8,128)S(1)}, u32[]{:S(2)}, u32[]{:S(2)}) collective-permute-start(f32[2,128,1024]{2,1,0:T(8,128)} %copy-done.1), channel_id=1, source_target_pairs={{0,8},{1,9},{2,10},{3,11},{4,12},{5,13},{6,14},{7,15},{8,0},{9,1},... | collective-permute-start | bytes 3145736 | tf_op jit(solution)/shard_map/ppermute | solution.py:28
  151.2 21.3 %collective-permute-start.22 = (f32[2,128,1024]{2,1,0:T(8,128)}, f32[2,128,1024]{2,1,0:T(8,128)S(1)}, u32[]{:S(2)}, u32[]{:S(2)}) collective-permute-start(f32[2,128,1024]{2,1,0:T(8,128)} %collective-permute-done.21.refs_13_), channel_id=1, source_target_pairs={{0,8},{1,9},{2,10},{3,11},{4,12},{5,13},{6,14},{7,15},{8,0},{9,1},... | collective-permute-start | bytes 3145736 | tf_op jit(solution)/shard_map/ppermute | solution.py:28
  151.2 11.1 %copy-start.8 = (f32[2,1,128,1024]{3,2,1,0:T(8,128)S(1)}, f32[2,1,128,1024]{3,2,1,0:T(8,128)}, u32[]{:S(2)}) copy-start(f32[2,1,128,1024]{3,2,1,0:T(8,128)} %get-tuple-element.20) | copy-start | bytes 3145732
  151.2 11.1 %copy-start.11 = (f32[1024,1024,1]{1,0,2:T(8,128)S(1)}, f32[1024,1024,1]{1,0,2:T(8,128)}, u32[]{:S(2)}) copy-start(f32[1024,1024,1]{1,0,2:T(8,128)} %fusion.29) | copy-start | bytes 12582916
  162.3 11.1 %copy-start.2 = (f32[2,128,1024]{2,1,0:T(8,128)S(1)}, f32[2,128,1024]{2,1,0:T(8,128)}, u32[]{:S(2)}) copy-start(f32[2,128,1024]{2,1,0:T(8,128)} %copy-done.1) | copy-start | bytes 3145732
  172.5 1.0 copy-start.9

commit v2 on v0

v2 whole, which is shorter than its diff:
```python
import functools

import jax
import jax.numpy as jnp
from jax import lax
from jax.experimental import pallas as pl
from jax.experimental.pallas import tpu as pltpu
from jax.sharding import PartitionSpec as P

SLOTS = 20
STEPS = 12
ROWS = 128
ORDER = 1024
AXES = ("row", "col")
high = lax.Precision.HIGH


def place(index):
    row, col = divmod(index, 8)
    return col // 2, (row // 8) * 2 + col % 2, (row // 2) % 4, row % 2


def index_of(x, y, z, core):
    return (((y // 2) * 4 + z) * 2 + core) * 8 + x * 2 + y % 2


def send(value, move):
    pairs = [(i, index_of(*move(*place(i)))) for i in range(128)]
    return lax.ppermute(value, AXES, pairs)


def to_sibling(x, y, z, core):
    return x, y, z, 1 - core


def along_z(x, y, z, core):
    return x, y, (z + 1 - 2 * core) % 4, core


def along_x(x, y, z, core):
    return (x + 1 - 2 * core) % 4, y, z, core


def far_y(x, y, z, core):
    return x, (y + 2) % 4, z, core


def near_y(x, y, z, core):
    return x, y ^ 1, z, core


def after(value, *first):
    return lax.optimization_barrier((value,) + first)[0]


def turn_z(by):
    return lambda x, y, z, core: (x, y, (z + by) % 4, core)


def solve(panel, lower, upper, z):
    half = ORDER // 2
    first = jnp.einsum("pak,jk->paj", panel[:, :, :half], upper, precision=high)
    second = jnp.einsum("pak,jk->paj", panel, lower, precision=high)

    def turned(cols):
        twice = jnp.concatenate([cols, cols], 2)
        return lax.dynamic_slice_in_dim(twice, (half - z * ROWS) % half, half, 2)

    return jnp.concatenate([turned(first), turned(second)], 2)


def square_of(lower, upper):
    half = ORDER // 2
    whole = jnp.einsum("ki,kj->ij", lower, lower, precision=high)
    corner = jnp.einsum("ki,kj->ij", upper, upper, precision=high)
    return whole.at[:half, :half].add(corner)


def update_kernel(counts, slots, left, buffer, position, kind, meta, *refs):
    blocks, n_sources = counts
    trails, refs = refs[:2], refs[2:]
    lefts, refs = refs[: 2 * len(blocks)], refs[2 * len(blocks) :]
    sources, refs = refs[:n_sources], refs[n_sources:]
    out, slab, sems, done, done_sems = refs
    step = pl.program_id(0)
    half = step % 2

    def fetch(at):
        for which, source in enumerate(sources):
            for q in range(2):
                @pl.when(buffer[2 * at + q] == which)
                def _():
                    pltpu.make_async_copy(
                        source.at[position[2 * at + q]], slab.at[at % 2, q], sems.at[at % 2, q]
                    ).start()

    def written(at, q):
        return pltpu.make_async_copy(
            done.at[at % 2, q], out.at[slots[2 * at + q]], done_sems.at[at % 2, q]
        )

    @pl.when(jnp.logical_and(step == 0, kind[0] == 2))
    def _():
        fetch(0)

    following = jnp.minimum(step + 1, STEPS - 1)

    @pl.when(jnp.logical_and(step + 1 < STEPS, kind[2 * following] == 2))
    def _():
        fetch(following)

    before = jnp.maximum(step - 2, 0)
    for q in range(2):
        @pl.when(jnp.logical_and(step >= 2, kind[2 * before + q] > 0))
        def _():
            written(before, q).wait()

    @pl.when(kind[2 * step] == 2)
    def _():
        tops, rests = [], []
        for q in range(2):
            pltpu.make_async_copy(sources[0].at[0], slab.at[half, q], sems.at[half, q]).wait()
            right = slab[half, q]
            top = right.astype(jnp.bfloat16)
            tops.append(top)
            rests.append((right - top.astype(jnp.float32)).astype(jnp.bfloat16))
        top, rest = jnp.concatenate(tops, 0), jnp.concatenate(rests, 0)
        first = 0
        for at, size in enumerate(blocks):
            hi, lo = lefts[2 * at][0], lefts[2 * at + 1][0]
            term = product(hi, top) + product(hi, rest) + product(lo, top)
            for j in range(size):
                lane = pl.ds(pl.multiple_of(meta[first + j], ROWS), ROWS)
                rows = slice(j * ROWS, (j + 1) * ROWS)
                for q in range(2):
                    done[half, q, lane, :] = trails[q][0, lane, :] - term[rows, q * ROWS : (q + 1) * ROWS]
            first += size

    @pl.when(kind[2 * step] == 1)
    def _():
        for q in range(2):
            done[half, q] = trails[q][0]

    for q in range(2):
        @pl.when(kind[2 * step + q] > 0)
        def _():
            written(step, q).start()

    @pl.when(step == STEPS - 1)
    def _():
        for at in (STEPS - 2, STEPS - 1):
            for q in range(2):
                @pl.when(kind[2 * at + q] > 0)
                def _():
                    written(at, q).wait()


def product(a, b):
    return lax.dot_general(a, b, (((1,), (1,)), ((), ())), preferred_element_type=jnp.float32)


def update(trailing, blocks, lefts, sources, tables):
    def slot(q):
        return lambda step, slots, *_: (slots[2 * step + q], 0, 0)

    def tile(step, slots, left, *_):
        return left[step], 0, 0

    left_specs = [pl.BlockSpec((1, p.shape[1], ORDER), tile) for p in lefts]
    hbm = pl.BlockSpec(memory_space=pl.ANY)
    return pl.pallas_call(
        functools.partial(update_kernel, (blocks, len(sources))),
        grid_spec=pltpu.PrefetchScalarGridSpec(
            num_scalar_prefetch=len(tables),
            grid=(STEPS,),
            in_specs=[pl.BlockSpec((1, ORDER, ROWS), slot(q)) for q in range(2)]
            + left_specs
            + [hbm] * len(sources),
            out_specs=hbm,
            scratch_shapes=[
                pltpu.VMEM((2, 2, ROWS, ORDER), jnp.float32),
                pltpu.SemaphoreType.DMA((2, 2)),
                pltpu.VMEM((2, 2, ORDER, ROWS), jnp.float32),
                pltpu.SemaphoreType.DMA((2, 2)),
            ],
        ),
        out_shape=jax.ShapeDtypeStruct(trailing.shape, trailing.dtype),
        compiler_params=pltpu.CompilerParams(vmem_limit_bytes=56 << 20),
    )(*tables, trailing, trailing, *lefts, *sources)


def split(product):
    top = lax.reduce_precision(product, 8, 7)
    flat = (2, product.shape[1] * ROWS, ORDER)
    return top.astype(jnp.bfloat16).reshape(flat), (product - top).astype(jnp.bfloat16).reshape(flat)


def times(blocks, square):
    return split(jnp.einsum("pxak,kj->pxaj", jnp.stack(blocks, 1), square, precision=high))


def per_device(pivot_inverse, panel, trailing, tile_list):
    row, col = lax.axis_index("row"), lax.axis_index("col")
    far, z, core = row // 8, (row // 2) % 4, row % 2
    x, near = col // 2, col % 2
    swap = functools.partial(send, move=to_sibling)

    toward = jnp.where(core == 0, -1, 1)
    places = jnp.stack([x, (x + toward) % 4, (x - toward) % 4, (x + 2) % 4]) * 2
    places = jnp.concatenate([places + near, places + 1 - near]) * ROWS
    left, right = tile_list[:, 0], tile_list[:, 1]
    live = right >= 0
    right = jnp.maximum(right, 0)
    inner, owner = right % 2, right // 2
    owner_far, owner_z, owner_core = owner // 8, (owner // 2) % 4, owner % 2
    dz = (owner_z - z) % 4
    other_core = (owner_core != core).astype(jnp.int32)
    ahead = jnp.where(core == 0, dz == 3, dz == 1)
    here = jnp.where(dz % 2 == 0, dz + other_core, jnp.where(ahead, 4 + other_core, 7 - other_core))
    there = jnp.where(dz % 2 == 0, 8 + dz + other_core, jnp.where(dz == 3, 12, 13) + 2 * other_core)
    buffer = jnp.where(owner_far == far, here, there)
    group = jnp.where(live, left, 2)
    slot = jnp.arange(SLOTS, dtype=jnp.int32)
    ahead_of = (group[None, :] == group[:, None]) & (slot[None, :] < slot[:, None])
    rank = jnp.sum(ahead_of.astype(jnp.int32), 1)
    pairs = [(jnp.sum((group == g).astype(jnp.int32)) + 1) // 2 for g in range(3)]
    start = jnp.where(group == 0, 0, jnp.where(group == 1, pairs[0], pairs[0] + pairs[1]))
    at = 2 * start + rank
    spots = jnp.arange(2 * STEPS, dtype=jnp.int32)
    pick = (at[None, :] == spots[:, None]).astype(jnp.int32)
    mate = (at[None, :] == (spots ^ 1)[:, None]).astype(jnp.int32)
    rows = jnp.stack([slot, buffer, inner, jnp.where(live, 2, 1)]).astype(jnp.int32)
    mine_rows = jnp.sum(rows[:, None, :] * pick[None], 2)
    mate_rows = jnp.sum(rows[:, None, :] * mate[None], 2)
    filled = jnp.sum(pick, 1)
    chosen = jnp.where(filled[None] > 0, mine_rows, mate_rows)
    kind = jnp.where(filled > 0, chosen[3], 0)
    left_of = jnp.where(jnp.arange(STEPS, dtype=jnp.int32) < pairs[0], 0, 1).astype(jnp.int32)
    tables = [chosen[0], left_of, chosen[1], chosen[2], kind, places.astype(jnp.int32)]

    half = ORDER // 2

    sib = swap(panel)
    other = send(pivot_inverse, far_y)
    near_own = send(after(panel, other), near_y)
    z1a = send(panel, along_z)
    upper = jnp.where(far == 0, pivot_inverse, other)[:, :half]
    lower = jnp.where(far == 0, other, pivot_inverse)
    mine = jnp.concatenate([lower, upper], 1)
    chip = jnp.concatenate([panel, sib], 0)
    x1 = send(chip, along_x)
    z1b = send(after(sib, z1a), along_z)
    from_down = send(mine, turn_z(1))
    from_up = send(mine, turn_z(-1))

    done = (x1, z1a, z1b, near_own, from_down, from_up, *tables)
    z2 = send(after(z1a, *done), along_z)
    across = send(after(mine, *done), turn_z(2))
    x2n = send(after(jnp.concatenate([x1[:2], near_own], 0), *done), along_x)
    far_own = send(after(panel, *done), far_y)
    near_sib = swap(near_own)
    sx1, sz1a, sz1b = swap(x1[2:]), swap(z1a), swap(z1b)
    x2, nx1a = x2n[:2], x2n[2:]

    done = (z2, across, x2n, far_own, near_sib, sx1, sz1a, sz1b)
    quarters = after(jnp.stack([mine, from_up, across, from_down], 0), *done)
    theirs = swap(quarters)
    nx12 = send(after(jnp.concatenate([near_sib, nx1a], 0), *done), along_x)
    fz_down = send(after(far_own, *done), turn_z(1))
    fz_up = send(after(far_own, *done), turn_z(-1))
    fz2 = send(after(z2, *done), far_y)
    sz2, far_sib = swap(after(z2, theirs)), swap(after(far_own, theirs))
    nx1b, nx2 = nx12[:2], nx12[2:]

    first = jnp.where(core == 0, quarters, theirs)
    second = jnp.where(core == 0, theirs, quarters)
    whole = jnp.stack([first, second], 1).reshape(half, ORDER + half)
    lower, upper = whole[:, :ORDER], whole[:, ORDER:]
    square = square_of(lower, upper)
    own_left = times([panel, x1[:2], sx1, x2], square)
    near_first = times([near_own, nx1a], square)
    solved = solve(panel, lower, upper, z)
    nsx1 = swap(after(nx1b, solved, *own_left, *near_first))
    near_second = times([nsx1, nx2], square)
    sfz_down, sfz_up, sfz2 = swap(after(fz_down, solved, *own_left, *near_first)), swap(fz_up), swap(fz2)

    sources = [panel, sib, z2, sz2, z1a, z1b, sz1a, sz1b]
    sources += [far_own, far_sib, fz2, sfz2, fz_down, fz_up, sfz_down, sfz_up]
    lefts = own_left + near_first + near_second
    return solved, update(trailing, (4, 2, 2), lefts, sources, tables)


def solution(mesh):
    placed = (P("row", None), P("row", "col", None), P("row", None, "col"), P("row", None))
    return jax.shard_map(
        per_device,
        mesh=mesh,
        in_specs=placed,
        out_specs=(P("row", "col", None), P("row", None, "col")),
        check_vma=False,
    )
```

time: 583 us -> 156 us (0.27)
  waiting for transfers between devices: 342 us -> 43.8 us
  matrix products: 113 us -> 28 us
  loops' own time: 58.7 us -> 0 us
  local copies, waits for them, and re-layouts: 41.6 us -> 8.87 us
  Pallas kernels: 0 us -> 30.6 us
  starting transfers between devices: 0.12 us -> 30.4 us
  between operations: 13.8 us -> 2.59 us
    all_gather x3 -> x0, waiting for transfers between devices: 341 us -> none  [the longest x1 166 us: per_device(): whole_tiles = lax.all_gather(solved, 'col', axis=1, tiled=True)]
    dot_general x21 -> x7, matrix products: 113 us -> 28 us  [the longest x3 21.2 us: times(): jnp.einsum('pxak,kj->pxaj', jnp.stack(blocks, 1), square, precision=high)]
    another operation x21 -> x0, loops' own time: 58.7 us -> none  [the longest x20 47 us: owner_slot(): lax.cond(listed[1] >= 0, lambda: slot_term(whole_tiles[listed[0]], slices...]
    ppermute x0 -> x27, waiting for transfers between devices: none -> 43.8 us  [send(): return lax.ppermute(value, AXES, pairs)]
    pallas_call x0 -> x1, Pallas kernels: none -> 30.6 us  [update(): pl.pallas_call(functools.partial(update_kernel, (blocks, len(sources))),...]
    ppermute x0 -> x27, starting transfers between devices: none -> 30.4 us  [send(): return lax.ppermute(value, AXES, pairs)]
    slice x40 -> x2, local copies, waits for them, and re-layouts: 24.1 us -> 1.95 us  [the longest x1 1.82 us: per_device(): x2, nx1a = (x2n[:2], x2n[2:])]
    dynamic_update_slice x20 -> x0, local copies, waits for them, and re-layouts: 16.7 us -> none  [per_device(): updates = lax.map(owner_slot, tile_list)]
  transfers between devices with their start and end apart: 3 -> 27, of which waited for: 3 -> 5; matrix products, arithmetic and copies ran while one was open for 0% -> 30% of each run, Pallas kernels for 0% -> 0%
where the time goes in v2:
time: 156 us; the launch traced here: 155 us
  waiting for transfers between devices  43.8 us (28%)
  Pallas kernels  30.6 us (20%)
  starting transfers between devices  30.4 us (19%)
  matrix products  28 us (18%)
  other arithmetic  11.1 us (7%)
  local copies, waits for them, and re-layouts  8.87 us (6%)
  between operations  2.59 us (2%)
    ppermute x27, waiting for transfers between devices, send(): return lax.ppermute(value, AXES, pairs)  43.8 us
    pallas_call x1, Pallas kernels, update(): pl.pallas_call(functools.partial(update_kernel, (blocks, len(sources))),...  30.6 us
    ppermute x27, starting transfers between devices, send(): return lax.ppermute(value, AXES, pairs)  30.4 us
    dot_general x3, matrix products, times(): jnp.einsum('pxak,kj->pxaj', jnp.stack(blocks, 1), square, precision=high)  21.2 us
    dot_general x1, matrix products, square_of(): whole = jnp.einsum('ki,kj->ij', lower, lower, precision=high)  3.84 us
    unnamed x31, local copies, waits for them, and re-layouts  3.22 us
    concatenate x1, other arithmetic, per_device(): chip = jnp.concatenate([panel, sib], 0)  3.14 us
  transfers between devices with their start and end apart: 27, of which 5 were waited for; matrix products, arithmetic and copies ran while one was open for 30% of the time, Pallas kernels for 0%

profile of v2, /device:TPU:17, one launch (start us, length us, event | category | flops | bytes accessed | tf_op | source)
XLA Modules:
  0.0 155.4 jit_solution(2707523056157739874)
XLA Ops:
  0.6 3.8 %collective-permute-start.4 = (f32[2,128,1024]{2,1,0:T(8,128)}, f32[2,128,1024]{2,1,0:T(8,128)}, u32[]{:S(2)}, u32[]{:S(2)}) collective-permute-start(f32[2,128,1024]{2,1,0:T(8,128)} %refs_8_.1), channel_id=1, source_target_pairs={{0,16},{1,17},{2,18},{3,19},{4,20},{5,21},{6,22},{7,23},{8,56},{9,... | collective-permute-start | bytes 3145736 | tf_op jit(solution)/shard_map/ppermute | solution.py:29
  4.5 1.4 fusion.36
  7.2 0.2 convert_reduce_fusion
  7.5 0.1 broadcast_add_fusion
  7.6 0.1 fusion.29
  7.7 0.7 fusion.32
  8.4 0.7 compare_select_fusion.7
  9.1 3.1 %pad_maximum_fusion.2 = f32[4,128,1024]{2,1,0:T(8,128)} fusion(f32[2,128,1024]{2,1,0:T(8,128)S(1)} %collective-permute-done.2.refs_9_, f32[2,128,1024]{2,1,0:T(8,128)} %refs_8_.1), kind=kLoop, calls=%fused_computation.18 | loop fusion | flops 524288 | bytes 4194304 | tf_op jit(solution)/shard_map/concatenate | solution.py:250
  12.3 2.5 %collective-permute-start.3 = (f32[4,128,1024]{2,1,0:T(8,128)}, f32[4,128,1024]{2,1,0:T(8,128)}, u32[]{:S(2)}, u32[]{:S(2)}) collective-permute-start(f32[4,128,1024]{2,1,0:T(8,128)} %pad_maximum_fusion.2), channel_id=1, source_target_pairs={{0,2},{1,3},{2,4},{3,5},{4,6},{5,7},{6,0},{7,1},{8,14},{9,15},{10,... | collective-permute-start | bytes 6291464 | tf_op jit(solution)/shard_map/ppermute | solution.py:29
  14.8 0.1 fusion.28
  14.8 0.1 copy.11
  14.9 0.1 multiply_reduce_fusion
  15.1 0.5 compare_select_fusion.6.left
  15.6 0.5 bitcast_select_fusion.kind
  16.1 1.9 %collective-permute-start.6 = (f32[2,128,1024]{2,1,0:T(8,128)S(1)}, f32[2,128,1024]{2,1,0:T(8,128)S(1)}, u32[]{:S(2)}, u32[]{:S(2)}) collective-permute-start(f32[2,128,1024]{2,1,0:T(8,128)S(1)} %copy-done.1), channel_id=1, source_target_pairs={{0,1},{1,0},{2,3},{3,2},{4,5},{5,4},{6,7},{7,6},{8,9},{9,8},{10,11... | collective-permute-start | bytes 3145736 | tf_op jit(solution)/shard_map/ppermute | solution.py:29
  18.0 0.7 add_multiply_fusion.1.meta
  18.7 0.6 slice_bitcast_fusion.2
  19.3 0.8 collective-permute-start.5
  20.2 0.8 collective-permute-start.7
  21.0 2.0 %collective-permute-start.1 = (f32[64,1536]{1,0:T(8,128)S(1)}, f32[64,1536]{1,0:T(8,128)S(1)}, u32[]{:S(2)}, u32[]{:S(2)}) collective-permute-start(f32[64,1536]{1,0:T(8,128)S(1)} %get-tuple-element.30), channel_id=1, source_target_pairs={{0,48},{1,49},{2,50},{3,51},{4,52},{5,53},{6,54},{7,55},{8,56},{9,... | collective-permute-start | bytes 1179656 | tf_op jit(solution)/shard_map/ppermute | solution.py:29
  23.0 18.8 %collective-permute-done.6 = f32[2,128,1024]{2,1,0:T(8,128)S(1)} collective-permute-done((f32[2,128,1024]{2,1,0:T(8,128)S(1)}, f32[2,128,1024]{2,1,0:T(8,128)S(1)}, u32[]{:S(2)}, u32[]{:S(2)}) %collective-permute-start.6) | collective-permute-done | bytes 1048608 | tf_op jit(solution)/shard_map/ppermute | solution.py:29
  41.7 0.4 collective-permute-start.14
  42.1 0.1 collective-permute-start.12
  42.3 2.8 %slice_bitcast_fusion.6 = (f32[2,1,128,1024]{3,2,0,1:T(8,128)}, f32[2,128,1024]{2,1,0:T(8,128)S(1)}, f32[2,128,1024]{2,1,0:T(8,128)S(1)}) fusion(f32[4,128,1024]{2,1,0:T(8,128)} %collective-permute-done.3), kind=kLoop, calls=%fused_computation.121 | loop fusion | bytes 5242880 | tf_op jit(solution)/shard_map/stack | solution.py:199
  45.1 0.2 pad_maximum_fusion.3
  45.4 0.6 collective-permute-start.10
  46.0 2.1 %collective-permute-start.8 = (f32[64,1536]{1,0:T(8,128)S(1)}, f32[64,1536]{1,0:T(8,128)S(1)}, u32[]{:S(2)}, u32[]{:S(2)}) collective-permute-start(f32[64,1536]{1,0:T(8,128)S(1)} %get-tuple-element.30), channel_id=1, source_target_pairs={{0,32},{1,33},{2,34},{3,35},{4,36},{5,37},{6,38},{7,39},{8,40},{9,... | collective-permute-start | bytes 1179656 | tf_op jit(solution)/shard_map/ppermute | solution.py:29
  48.1 0.8 collective-permute-start.9
  48.9 2.5 %collective-permute-start.11 = (f32[2,128,1024]{2,1,0:T(8,128)S(1)}, f32[2,128,1024]{2,1,0:T(8,128)}, u32[]{:S(2)}, u32[]{:S(2)}) collective-permute-start(f32[2,128,1024]{2,1,0:T(8,128)S(1)} %copy-done.1), channel_id=1, source_target_pairs={{0,64},{1,65},{2,66},{3,67},{4,68},{5,69},{6,70},{7,71},{8,72},{9,... | collective-permute-start | bytes 3145736 | tf_op jit(solution)/shard_map/ppermute | solution.py:29
  51.4 7.0 %collective-permute-done.8 = f32[64,1536]{1,0:T(8,128)S(1)} collective-permute-done((f32[64,1536]{1,0:T(8,128)S(1)}, f32[64,1536]{1,0:T(8,128)S(1)}, u32[]{:S(2)}, u32[]{:S(2)}) %collective-permute-start.8) | collective-permute-done | bytes 393248 | tf_op jit(solution)/shard_map/ppermute | solution.py:29
  58.3 0.8 collective-permute-start.13
  59.1 0.1 pad_maximum_fusion.7
  59.2 8.8 %collective-permute-done.9.refs_10_ = f32[2,128,1024]{2,1,0:T(8,128)} collective-permute-done((f32[2,128,1024]{2,1,0:T(8,128)}, f32[2,128,1024]{2,1,0:T(8,128)}, u32[]{:S(2)}, u32[]{:S(2)}) %collective-permute-start.9) | collective-permute-done | bytes 1048608 | tf_op jit(solution)/shard_map/ppermute | solution.py:29
  68.1 7.4 %collective-permute-done.11.refs_16_ = f32[2,128,1024]{2,1,0:T(8,128)} collective-permute-done((f32[2,128,1024]{2,1,0:T(8,128)S(1)}, f32[2,128,1024]{2,1,0:T(8,128)}, u32[]{:S(2)}, u32[]{:S(2)}) %collective-permute-start.11) | collective-permute-done | bytes 1048608 | tf_op jit(solution)/shard_map/ppermute | solution.py:29
  75.5 0.9 copy-done.13
  76.4 0.7 collective-permute-start.16
  77.1 0.5 collective-permute-start.24
  77.6 0.9 collective-permute-start.23
  78.5 2.5 %collective-permute-start.21 = (f32[2,128,1024]{2,1,0:T(8,128)}, f32[2,128,1024]{2,1,0:T(8,128)}, u32[]{:S(2)}, u32[]{:S(2)}) collective-permute-start(f32[2,128,1024]{2,1,0:T(8,128)} %collective-permute-done.9.refs_10_), channel_id=1, source_target_pairs={{0,64},{1,65},{2,66},{3,67},{4,68},{5,69},{6,70},{7,71},{8,72},{9,... | collective-permute-start | bytes 3145736 | tf_op jit(solution)/shard_map/ppermute | solution.py:29
  81.0 1.8 %fusion.46 = (f32[2,128,1024]{2,1,0:T(8,128)S(1)}, f32[2,1,128,1024]{3,2,0,1:T(8,128)S(1)}, f32[2,1,128,1024]{3,2,0,1:T(8,128)S(1)}) fusion(f32[4,128,1024]{2,1,0:T(8,128)} %collective-permute-done.10), kind=kLoop, calls=%fused_computation.124 | loop fusion | bytes 5242880 | tf_op jit(solution)/shard_map/slice | solution.py:263
  82.9 0.2 pad_maximum_fusion.5
  83.1 2.6 %collective-permute-start.17 = (f32[4,128,1024]{2,1,0:T(8,128)S(1)}, f32[4,128,1024]{2,1,0:T(8,128)S(1)}, u32[]{:S(2)}, u32[]{:S(2)}) collective-permute-start(f32[4,128,1024]{2,1,0:T(8,128)S(1)} %pad_maximum_fusion.5), channel_id=1, source_target_pairs={{0,2},{1,3},{2,4},{3,5},{4,6},{5,7},{6,0},{7,1},{8,14},{9,15},{10,... | collective-permute-start | bytes 6291464 | tf_op jit(solution)/shard_map/ppermute | solution.py:29
  85.7 1.7 %select_bitcast_fusion.1 = (f32[4,1,64,1536]{3,2,0,1:T(8,128)S(1)}, f32[4,1,64,1536]{3,2,0,1:T(8,128)S(1)}) fusion(f32[4,64,1536]{2,1,0:T(8,128)S(1)} %pad_maximum_fusion.7, f32[4,64,1536]{2,1,0:T(8,128)} %collective-permute-done.16, pred[]{:T(512)S(6)} %eq.132), kind=kLoop, calls=%fused_computation.32 | loop fusion | flops 786432 | bytes 6291457 | tf_op jit(solution)/shard_map/stack | solution.py:277
  87.4 0.2 pad_maximum_fusion.1
  87.6 0.2 copy.12
  87.8 1.0 fusion.18
  88.9 0.6 convolution_bitcast_fusion
  89.5 0.3 fusion.24
  89.9 3.8 %fusion.14 = f32[1024,1024]{1,0:T(8,128)S(1)} fusion(f32[512,1536]{1,0:T(8,128)S(1)} %bitcast.90), kind=kOutput, calls=%fused_computation.27 | convolution fusion | flops 3221225472 | bytes 6291456 | tf_op jit(solution)/shard_map/ki,kj->ij/dot_general | solution.py:74
  93.7 1.2 fusion.17
  95.0 5.2 %fusion.8 = (bf16[2,2,128,1024]{3,2,1,0:T(8,128)(2,1)}, bf16[2,2,128,1024]{3,2,1,0:T(8,128)(2,1)}) fusion(f32[1024,1024]{1,0:T(8,128)S(1)} %fusion.17, f32[2,1,128,1024]{3,2,0,1:T(8,128)S(1)} %get-tuple-element.62, f32[2,1,128,1024]{3,2,0,1:T(8,128)S(1)} %bitcast.97), kind=kOutput, calls=%fused_computation.16 | convolution fusion | flops 3223846912 | bytes 8388608 | tf_op jit(solution)/shard_map/pxak,kj->pxaj/dot_general | solution.py:199
  100.2 8.6 %fusion = (bf16[2,4,128,1024]{3,2,1,0:T(8,128)(2,1)}, bf16[2,4,128,1024]{3,2,1,0:T(8,128)(2,1)}) fusion(f32[1024,1024]{1,0:T(8,128)S(1)} %fusion.17, f32[2,1,128,1024]{3,2,0,1:T(8,128)S(1)} %get-tuple-element.63, f32[2,1,128,1024]{3,2,0,1:T(8,128)S(1)} %bitcast.103, f32[2,1,128,1024]{3,2,0,1:T(8,128)S(1)} %copy-done.8, f32[2,1,128,1024]{3,2,0,1:T(8,128)S(1)} %bitcast.92), kind=kOutput, calls=%fused_computation.2 | convolution fusion | flops 6449790976 | bytes 12582912 | tf_op jit(solution)/shard_map/pxak,kj->pxaj/dot_general | solution.py:199
  108.8 0.1 fusion.45
  109.0 2.7 %collective-permute-start.18 = (f32[2,128,1024]{2,1,0:T(8,128)S(1)}, f32[2,128,1024]{2,1,0:T(8,128)}, u32[]{:S(2)}, u32[]{:S(2)}) collective-permute-start(f32[2,128,1024]{2,1,0:T(8,128)S(1)} %get-tuple-element.36), channel_id=1, source_target_pairs={{0,8},{1,9},{2,10},{3,11},{4,12},{5,13},{6,14},{7,15},{8,0},{9,1},... | collective-permute-start | bytes 3145736 | tf_op jit(solution)/shard_map/ppermute | solution.py:29
  111.7 0.1 collective-permute-start.26
  111.8 0.4 collective-permute-start.22
  112.2 0.1 collective-permute-start.20
  112.3 0.4 collective-permute-start.19
  112.7 1.8 %collective-permute-done.18 = f32[2,128,1024]{2,1,0:T(8,128)} collective-permute-done((f32[2,128,1024]{2,1,0:T(8,128)S(1)}, f32[2,128,1024]{2,1,0:T(8,128)}, u32[]{:S(2)}, u32[]{:S(2)}) %collective-permute-start.18) | collective-permute-done | bytes 1048608 | tf_op jit(solution)/shard_map/ppermute | solution.py:29
  114.5 0.4 collective-permute-start.25
  114.9 1.3 copy.16
  116.2 7.4 %fusion.9 = (bf16[2,2,128,1024]{3,2,1,0:T(8,128)(2,1)}, bf16[2,2,128,1024]{3,2,1,0:T(8,128)(2,1)}) fusion(f32[1024,1024]{1,0:T(8,128)} %copy-done, f32[2,1,128,1024]{3,2,0,1:T(8,128)S(1)} %get-tuple-element.60, f32[2,1,128,1024]{3,2,0,1:T(8,128)} %bitcast.37), kind=kOutput, calls=%fused_computation.17 | convolution fusion | flops 3223846912 | bytes 8388608 | tf_op jit(solution)/shard_map/pxak,kj->pxaj/dot_general | solution.py:199
  123.7 0.9 copy-done.9
  124.6 30.6 %shard_map.59 = f32[20,1024,128]{2,1,0:T(8,128)} custom-call(s32[24]{0:T(128)} %get-tuple-element.73.slots, s32[12]{0:T(128)} %compare_select_fusion.6.left, s32[24]{0:T(128)} %get-tuple-element.72.buffer, s32[24]{0:T(128)} %get-tuple-element.71.position, s32[24]{0:T(128)} %bitcast_select_fusion.kind, s32[8]{0:T(128)} %add_multiply_fusion.1.meta, ...), custom_call_target="tpu_custom_call" | custom-call | tf_op jit(solution)/shard_map/pallas_call | solution.py:171
  (64 shorter events, 0.4 us)
Async XLA Ops:
  0.6 18.7 %collective-permute-start.4 = (f32[2,128,1024]{2,1,0:T(8,128)}, f32[2,128,1024]{2,1,0:T(8,128)}, u32[]{:S(2)}, u32[]{:S(2)}) collective-permute-start(f32[2,128,1024]{2,1,0:T(8,128)} %refs_8_.1), channel_id=1, source_target_pairs={{0,16},{1,17},{2,18},{3,19},{4,20},{5,21},{6,22},{7,23},{8,56},{9,... | collective-permute-start | bytes 3145736 | tf_op jit(solution)/shard_map/ppermute | solution.py:29
  4.5 4.7 %collective-permute-start.2 = (f32[2,128,1024]{2,1,0:T(8,128)}, f32[2,128,1024]{2,1,0:T(8,128)S(1)}, u32[]{:S(2)}, u32[]{:S(2)}) collective-permute-start(f32[2,128,1024]{2,1,0:T(8,128)} %refs_8_.1), channel_id=1, source_target_pairs={{0,8},{1,9},{2,10},{3,11},{4,12},{5,13},{6,14},{7,15},{8,0},{9,1},... | collective-permute-start | bytes 3145736 | tf_op jit(solution)/shard_map/ppermute | solution.py:29
  4.5 11.7 %collective-permute-start = (f32[64,1024]{1,0:T(8,128)}, f32[64,1024]{1,0:T(8,128)S(1)}, u32[]{:S(2)}, u32[]{:S(2)}) collective-permute-start(f32[64,1024]{1,0:T(8,128)} %param.6), channel_id=1, source_target_pairs={{0,64},{1,65},{2,66},{3,67},{4,68},{5,69},{6,70},{7,71},{8,72},{9,... | collective-permute-start | bytes 786440 | tf_op jit(solution)/shard_map/ppermute | solution.py:29
  9.1 7.1 %copy-start.1 = (f32[2,128,1024]{2,1,0:T(8,128)S(1)}, f32[2,128,1024]{2,1,0:T(8,128)}, u32[]{:S(2)}) copy-start(f32[2,128,1024]{2,1,0:T(8,128)} %refs_8_.1) | copy-start | bytes 3145732
  9.1 11.0 %copy-start.12 = (f32[64,1024]{1,0:T(8,128)S(1)}, f32[64,1024]{1,0:T(8,128)}, u32[]{:S(2)}) copy-start(f32[64,1024]{1,0:T(8,128)} %param.6) | copy-start | bytes 786436
  9.1 10.2 %copy-start.2 = (f32[2,128,1024]{2,1,0:T(8,128)}, f32[2,128,1024]{2,1,0:T(8,128)S(1)}, u32[]{:S(2)}) copy-start(f32[2,128,1024]{2,1,0:T(8,128)S(1)} %collective-permute-done.2.refs_9_) | copy-start | bytes 3145732
  12.3 29.9 %collective-permute-start.3 = (f32[4,128,1024]{2,1,0:T(8,128)}, f32[4,128,1024]{2,1,0:T(8,128)}, u32[]{:S(2)}, u32[]{:S(2)}) collective-permute-start(f32[4,128,1024]{2,1,0:T(8,128)} %pad_maximum_fusion.2), channel_id=1, source_target_pairs={{0,2},{1,3},{2,4},{3,5},{4,6},{5,7},{6,0},{7,1},{8,14},{9,15},{10,... | collective-permute-start | bytes 6291464 | tf_op jit(solution)/shard_map/ppermute | solution.py:29
  16.1 25.6 %collective-permute-start.6 = (f32[2,128,1024]{2,1,0:T(8,128)S(1)}, f32[2,128,1024]{2,1,0:T(8,128)S(1)}, u32[]{:S(2)}, u32[]{:S(2)}) collective-permute-start(f32[2,128,1024]{2,1,0:T(8,128)S(1)} %copy-done.1), channel_id=1, source_target_pairs={{0,1},{1,0},{2,3},{3,2},{4,5},{5,4},{6,7},{7,6},{8,9},{9,8},{10,11... | collective-permute-start | bytes 3145736 | tf_op jit(solution)/shard_map/ppermute | solution.py:29
  19.3 26.0 %collective-permute-start.5 = (f32[2,128,1024]{2,1,0:T(8,128)S(1)}, f32[2,128,1024]{2,1,0:T(8,128)S(1)}, u32[]{:S(2)}, u32[]{:S(2)}) collective-permute-start(f32[2,128,1024]{2,1,0:T(8,128)S(1)} %collective-permute-done.2.refs_9_), channel_id=1, source_target_pairs={{0,16},{1,17},{2,18},{3,19},{4,20},{5,21},{6,22},{7,23},{8,56},{9,... | collective-permute-start | bytes 3145736 | tf_op jit(solution)/shard_map/ppermute | solution.py:29
  20.2 25.1 %collective-permute-start.7 = (f32[64,1536]{1,0:T(8,128)S(1)}, f32[64,1536]{1,0:T(8,128)S(1)}, u32[]{:S(2)}, u32[]{:S(2)}) collective-permute-start(f32[64,1536]{1,0:T(8,128)S(1)} %get-tuple-element.30), channel_id=1, source_target_pairs={{0,16},{1,17},{2,18},{3,19},{4,20},{5,21},{6,22},{7,23},{8,24},{9,... | collective-permute-start | bytes 1179656 | tf_op jit(solution)/shard_map/ppermute | solution.py:29
  21.0 24.4 %collective-permute-start.1 = (f32[64,1536]{1,0:T(8,128)S(1)}, f32[64,1536]{1,0:T(8,128)S(1)}, u32[]{:S(2)}, u32[]{:S(2)}) collective-permute-start(f32[64,1536]{1,0:T(8,128)S(1)} %get-tuple-element.30), channel_id=1, source_target_pairs={{0,48},{1,49},{2,50},{3,51},{4,52},{5,53},{6,54},{7,55},{8,56},{9,... | collective-permute-start | bytes 1179656 | tf_op jit(solution)/shard_map/ppermute | solution.py:29
  41.7 3.3 %copy-start.3 = (f32[2,128,1024]{2,1,0:T(8,128)}, f32[2,128,1024]{2,1,0:T(8,128)S(1)}, u32[]{:S(2)}) copy-start(f32[2,128,1024]{2,1,0:T(8,128)S(1)} %collective-permute-done.6) | copy-start | bytes 3145732
  41.7 6.4 %collective-permute-start.14 = (f32[2,128,1024]{2,1,0:T(8,128)}, f32[2,128,1024]{2,1,0:T(8,128)S(1)}, u32[]{:S(2)}, u32[]{:S(2)}) collective-permute-start(f32[2,128,1024]{2,1,0:T(8,128)} %collective-permute-done.4.refs_12_), channel_id=1, source_target_pairs={{0,8},{1,9},{2,10},{3,11},{4,12},{5,13},{6,14},{7,15},{8,0},{9,1},... | collective-permute-start | bytes 3145736 | tf_op jit(solution)/shard_map/ppermute | solution.py:29
  42.1 6.8 %collective-permute-start.12 = (f32[2,128,1024]{2,1,0:T(8,128)S(1)}, f32[2,128,1024]{2,1,0:T(8,128)S(1)}, u32[]{:S(2)}, u32[]{:S(2)}) collective-permute-start(f32[2,128,1024]{2,1,0:T(8,128)S(1)} %collective-permute-done.6), channel_id=1, source_target_pairs={{0,8},{1,9},{2,10},{3,11},{4,12},{5,13},{6,14},{7,15},{8,0},{9,1},... | collective-permute-start | bytes 3145736 | tf_op jit(solution)/shard_map/ppermute | solution.py:29
  45.3 30.1 %copy-start.5 = (f32[2,128,1024]{2,1,0:T(8,128)}, f32[2,128,1024]{2,1,0:T(8,128)S(1)}, u32[]{:S(2)}) copy-start(f32[2,128,1024]{2,1,0:T(8,128)S(1)} %collective-permute-done.5.refs_13_) | copy-start | bytes 3145732
  45.4 30.1 %collective-permute-start.10 = (f32[4,128,1024]{2,1,0:T(8,128)S(1)}, f32[4,128,1024]{2,1,0:T(8,128)}, u32[]{:S(2)}, u32[]{:S(2)}) collective-permute-start(f32[4,128,1024]{2,1,0:T(8,128)S(1)} %pad_maximum_fusion.3), channel_id=1, source_target_pairs={{0,2},{1,3},{2,4},{3,5},{4,6},{5,7},{6,0},{7,1},{8,14},{9,15},{10,... | collective-permute-start | bytes 6291464 | tf_op jit(solution)/shard_map/ppermute | solution.py:29
  46.0 12.4 %collective-permute-start.8 = (f32[64,1536]{1,0:T(8,128)S(1)}, f32[64,1536]{1,0:T(8,128)S(1)}, u32[]{:S(2)}, u32[]{:S(2)}) collective-permute-start(f32[64,1536]{1,0:T(8,128)S(1)} %get-tuple-element.30), channel_id=1, source_target_pairs={{0,32},{1,33},{2,34},{3,35},{4,36},{5,37},{6,38},{7,39},{8,40},{9,... | collective-permute-start | bytes 1179656 | tf_op jit(solution)/shard_map/ppermute | solution.py:29
  48.1 11.1 %collective-permute-start.15 = (f32[2,128,1024]{2,1,0:T(8,128)S(1)}, f32[2,128,1024]{2,1,0:T(8,128)S(1)}, u32[]{:S(2)}, u32[]{:S(2)}) collective-permute-start(f32[2,128,1024]{2,1,0:T(8,128)S(1)} %collective-permute-done.5.refs_13_), channel_id=1, source_target_pairs={{0,8},{1,9},{2,10},{3,11},{4,12},{5,13},{6,14},{7,15},{8,0},{9,1},... | collective-permute-start | bytes 3145736 | tf_op jit(solution)/shard_map/ppermute | solution.py:29
  48.1 27.3 %copy-start.6 = (f32[2,128,1024]{2,1,0:T(8,128)}, f32[2,128,1024]{2,1,0:T(8,128)S(1)}, u32[]{:S(2)}) copy-start(f32[2,128,1024]{2,1,0:T(8,128)S(1)} %collective-permute-done.14.refs_14_) | copy-start | bytes 3145732
  48.1 19.9 %collective-permute-start.9 = (f32[2,128,1024]{2,1,0:T(8,128)}, f32[2,128,1024]{2,1,0:T(8,128)}, u32[]{:S(2)}, u32[]{:S(2)}) collective-permute-start(f32[2,128,1024]{2,1,0:T(8,128)} %collective-permute-done.4.refs_12_), channel_id=1, source_target_pairs={{0,16},{1,17},{2,18},{3,19},{4,20},{5,21},{6,22},{7,23},{8,56},{9,... | collective-permute-start | bytes 3145736 | tf_op jit(solution)/shard_map/ppermute | solution.py:29
  48.9 26.6 %copy-start.10 = (f32[2,128,1024]{2,1,0:T(8,128)}, f32[2,128,1024]{2,1,0:T(8,128)S(1)}, u32[]{:S(2)}) copy-start(f32[2,128,1024]{2,1,0:T(8,128)S(1)} %collective-permute-done.12) | copy-start | bytes 3145732
  48.9 26.5 %collective-permute-start.11 = (f32[2,128,1024]{2,1,0:T(8,128)S(1)}, f32[2,128,1024]{2,1,0:T(8,128)}, u32[]{:S(2)}, u32[]{:S(2)}) collective-permute-start(f32[2,128,1024]{2,1,0:T(8,128)S(1)} %copy-done.1), channel_id=1, source_target_pairs={{0,64},{1,65},{2,66},{3,67},{4,68},{5,69},{6,70},{7,71},{8,72},{9,... | collective-permute-start | bytes 3145736 | tf_op jit(solution)/shard_map/ppermute | solution.py:29
  58.3 17.1 %collective-permute-start.13 = (f32[2,128,1024]{2,1,0:T(8,128)S(1)}, f32[2,128,1024]{2,1,0:T(8,128)S(1)}, u32[]{:S(2)}, u32[]{:S(2)}) collective-permute-start(f32[2,128,1024]{2,1,0:T(8,128)S(1)} %get-tuple-element.67), channel_id=1, source_target_pairs={{0,8},{1,9},{2,10},{3,11},{4,12},{5,13},{6,14},{7,15},{8,0},{9,1},... | collective-permute-start | bytes 3145736 | tf_op jit(solution)/shard_map/ppermute | solution.py:29
  59.2 16.2 %copy-start.7 = (f32[2,128,1024]{2,1,0:T(8,128)}, f32[2,128,1024]{2,1,0:T(8,128)S(1)}, u32[]{:S(2)}) copy-start(f32[2,128,1024]{2,1,0:T(8,128)S(1)} %collective-permute-done.15.refs_15_) | copy-start | bytes 3145732
  75.4 1.0 copy-start.13
  76.4 9.3 %collective-permute-start.16 = (f32[4,64,1536]{2,1,0:T(8,128)S(1)}, f32[4,64,1536]{2,1,0:T(8,128)}, u32[]{:S(2)}, u32[]{:S(2)}) collective-permute-start(f32[4,64,1536]{2,1,0:T(8,128)S(1)} %pad_maximum_fusion.7), channel_id=1, source_target_pairs={{0,8},{1,9},{2,10},{3,11},{4,12},{5,13},{6,14},{7,15},{8,0},{9,1},... | collective-permute-start | bytes 4718600 | tf_op jit(solution)/shard_map/ppermute | solution.py:29
  77.1 5.8 %copy-start.11 = (f32[2,128,1024]{2,1,0:T(8,128)S(1)}, f32[2,128,1024]{2,1,0:T(8,128)}, u32[]{:S(2)}) copy-start(f32[2,128,1024]{2,1,0:T(8,128)} %copy-done.10) | copy-start | bytes 3145732
  77.1 34.6 %collective-permute-start.24 = (f32[2,128,1024]{2,1,0:T(8,128)}, f32[2,128,1024]{2,1,0:T(8,128)}, u32[]{:S(2)}, u32[]{:S(2)}) collective-permute-start(f32[2,128,1024]{2,1,0:T(8,128)} %collective-permute-done.11.refs_16_), channel_id=1, source_target_pairs={{0,48},{1,49},{2,50},{3,51},{4,52},{5,53},{6,54},{7,55},{8,56},{9,... | collective-permute-start | bytes 3145736 | tf_op jit(solution)/shard_map/ppermute | solution.py:29
  77.6 34.7 %collective-permute-start.23 = (f32[2,128,1024]{2,1,0:T(8,128)}, f32[2,128,1024]{2,1,0:T(8,128)}, u32[]{:S(2)}, u32[]{:S(2)}) collective-permute-start(f32[2,128,1024]{2,1,0:T(8,128)} %collective-permute-done.11.refs_16_), channel_id=1, source_target_pairs={{0,16},{1,17},{2,18},{3,19},{4,20},{5,21},{6,22},{7,23},{8,24},{9,... | collective-permute-start | bytes 3145736 | tf_op jit(solution)/shard_map/ppermute | solution.py:29
  78.5 33.2 %collective-permute-start.21 = (f32[2,128,1024]{2,1,0:T(8,128)}, f32[2,128,1024]{2,1,0:T(8,128)}, u32[]{:S(2)}, u32[]{:S(2)}) collective-permute-start(f32[2,128,1024]{2,1,0:T(8,128)} %collective-permute-done.9.refs_10_), channel_id=1, source_target_pairs={{0,64},{1,65},{2,66},{3,67},{4,68},{5,69},{6,70},{7,71},{8,72},{9,... | collective-permute-start | bytes 3145736 | tf_op jit(solution)/shard_map/ppermute | solution.py:29
  83.1 25.7 %collective-permute-start.17 = (f32[4,128,1024]{2,1,0:T(8,128)S(1)}, f32[4,128,1024]{2,1,0:T(8,128)S(1)}, u32[]{:S(2)}, u32[]{:S(2)}) collective-permute-start(f32[4,128,1024]{2,1,0:T(8,128)S(1)} %pad_maximum_fusion.5), channel_id=1, source_target_pairs={{0,2},{1,3},{2,4},{3,5},{4,6},{5,7},{6,0},{7,1},{8,14},{9,15},{10,... | collective-permute-start | bytes 6291464 | tf_op jit(solution)/shard_map/ppermute | solution.py:29
  93.7 1.3 copy-start.4
  95.0 5.2 %copy-start = (f32[1024,1024]{1,0:T(8,128)}, f32[1024,1024]{1,0:T(8,128)S(1)}, u32[]{:S(2)}) copy-start(f32[1024,1024]{1,0:T(8,128)S(1)} %fusion.17) | copy-start | bytes 12582916
  95.0 5.2 %copy-start.8 = (f32[2,1,128,1024]{3,2,0,1:T(8,128)S(1)}, f32[2,1,128,1024]{3,2,0,1:T(8,128)}, u32[]{:S(2)}) copy-start(f32[2,1,128,1024]{3,2,0,1:T(8,128)} %get-tuple-element.66) | copy-start | bytes 3145732
  95.0 5.2 %copy-start.14 = (f32[2,128,1024]{2,1,0:T(8,128)S(1)}, f32[2,128,1024]{2,1,0:T(8,128)}, u32[]{:S(2)}) copy-start(f32[2,128,1024]{2,1,0:T(8,128)} %copy-done.13) | copy-start | bytes 3145732
  109.0 5.6 %collective-permute-start.18 = (f32[2,128,1024]{2,1,0:T(8,128)S(1)}, f32[2,128,1024]{2,1,0:T(8,128)}, u32[]{:S(2)}, u32[]{:S(2)}) collective-permute-start(f32[2,128,1024]{2,1,0:T(8,128)S(1)} %get-tuple-element.36), channel_id=1, source_target_pairs={{0,8},{1,9},{2,10},{3,11},{4,12},{5,13},{6,14},{7,15},{8,0},{9,1},... | collective-permute-start | bytes 3145736 | tf_op jit(solution)/shard_map/ppermute | solution.py:29
  111.7 12.0 %collective-permute-start.26 = (f32[2,128,1024]{2,1,0:T(8,128)}, f32[2,128,1024]{2,1,0:T(8,128)S(1)}, u32[]{:S(2)}, u32[]{:S(2)}) collective-permute-start(f32[2,128,1024]{2,1,0:T(8,128)} %collective-permute-done.24.refs_21_), channel_id=1, source_target_pairs={{0,8},{1,9},{2,10},{3,11},{4,12},{5,13},{6,14},{7,15},{8,0},{9,1},... | collective-permute-start | bytes 3145736 | tf_op jit(solution)/shard_map/ppermute | solution.py:29
  111.8 11.9 %collective-permute-start.22 = (f32[2,128,1024]{2,1,0:T(8,128)}, f32[2,128,1024]{2,1,0:T(8,128)}, u32[]{:S(2)}, u32[]{:S(2)}) collective-permute-start(f32[2,128,1024]{2,1,0:T(8,128)} %collective-permute-done.21.refs_18_), channel_id=1, source_target_pairs={{0,8},{1,9},{2,10},{3,11},{4,12},{5,13},{6,14},{7,15},{8,0},{9,1},... | collective-permute-start | bytes 3145736 | tf_op jit(solution)/shard_map/ppermute | solution.py:29
  112.2 11.5 %collective-permute-start.20 = (f32[2,128,1024]{2,1,0:T(8,128)}, f32[2,128,1024]{2,1,0:T(8,128)}, u32[]{:S(2)}, u32[]{:S(2)}) collective-permute-start(f32[2,128,1024]{2,1,0:T(8,128)} %collective-permute-done.11.refs_16_), channel_id=1, source_target_pairs={{0,8},{1,9},{2,10},{3,11},{4,12},{5,13},{6,14},{7,15},{8,0},{9,1},... | collective-permute-start | bytes 3145736 | tf_op jit(solution)/shard_map/ppermute | solution.py:29
  112.3 11.4 %collective-permute-start.19 = (f32[2,128,1024]{2,1,0:T(8,128)}, f32[2,128,1024]{2,1,0:T(8,128)}, u32[]{:S(2)}, u32[]{:S(2)}) collective-permute-start(f32[2,128,1024]{2,1,0:T(8,128)} %collective-permute-done.9.refs_10_), channel_id=1, source_target_pairs={{0,8},{1,9},{2,10},{3,11},{4,12},{5,13},{6,14},{7,15},{8,0},{9,1},... | collective-permute-start | bytes 3145736 | tf_op jit(solution)/shard_map/ppermute | solution.py:29
  114.5 9.2 %collective-permute-start.25 = (f32[2,128,1024]{2,1,0:T(8,128)}, f32[2,128,1024]{2,1,0:T(8,128)}, u32[]{:S(2)}, u32[]{:S(2)}) collective-permute-start(f32[2,128,1024]{2,1,0:T(8,128)} %collective-permute-done.23.refs_20_), channel_id=1, source_target_pairs={{0,8},{1,9},{2,10},{3,11},{4,12},{5,13},{6,14},{7,15},{8,0},{9,1},... | collective-permute-start | bytes 3145736 | tf_op jit(solution)/shard_map/ppermute | solution.py:29
  123.7 1.0 copy-start.9

commit v3 on v2

--- a/solution.py
+++ b/solution.py
@@ -258,17 +258,19 @@
     across = send(after(mine, *done), turn_z(2))
     x2n = send(after(jnp.concatenate([x1[:2], near_own], 0), *done), along_x)
     far_own = send(after(panel, *done), far_y)
-    near_sib = swap(near_own)
-    sx1, sz1a, sz1b = swap(x1[2:]), swap(z1a), swap(z1b)
+    quarters = jnp.stack([mine, from_up, across, from_down], 0)
+    both_sib = swap(after(jnp.concatenate([near_own, x1[2:]], 0), *done))
+    near_sib, sx1 = both_sib[:2], both_sib[2:]
     x2, nx1a = x2n[:2], x2n[2:]
 
-    done = (z2, across, x2n, far_own, near_sib, sx1, sz1a, sz1b)
-    quarters = after(jnp.stack([mine, from_up, across, from_down], 0), *done)
-    theirs = swap(quarters)
-    nx12 = send(after(jnp.concatenate([near_sib, nx1a], 0), *done), along_x)
-    fz_down = send(after(far_own, *done), turn_z(1))
-    fz_up = send(after(far_own, *done), turn_z(-1))
-    fz2 = send(after(z2, *done), far_y)
+    done = (z2, across, x2n, far_own, both_sib)
+    near_pair = after(jnp.concatenate([near_sib, nx1a], 0), *done)
+    nx12 = send(near_pair, along_x)
+    theirs = swap(after(quarters, near_pair))
+    sz1a, sz1b = swap(after(z1a, theirs)), swap(after(z1b, theirs))
+    fz_down = send(after(far_own, near_pair), turn_z(1))
+    fz_up = send(after(far_own, near_pair), turn_z(-1))
+    fz2 = send(after(z2, near_pair), far_y)
     sz2, far_sib = swap(after(z2, theirs)), swap(after(far_own, theirs))
     nx1b, nx2 = nx12[:2], nx12[2:]
 
@@ -280,9 +282,10 @@
     own_left = times([panel, x1[:2], sx1, x2], square)
     near_first = times([near_own, nx1a], square)
     solved = solve(panel, lower, upper, z)
-    nsx1 = swap(after(nx1b, solved, *own_left, *near_first))
+    ready = (solved, *own_left, *near_first)
+    nsx1 = swap(after(nx1b, *ready))
     near_second = times([nsx1, nx2], square)
-    sfz_down, sfz_up, sfz2 = swap(after(fz_down, solved, *own_left, *near_first)), swap(fz_up), swap(fz2)
+    sfz_down, sfz_up, sfz2 = [swap(after(part, *ready)) for part in (fz_down, fz_up, fz2)]
 
     sources = [panel, sib, z2, sz2, z1a, z1b, sz1a, sz1b]
     sources += [far_own, far_sib, fz2, sfz2, fz_down, fz_up, sfz_down, sfz_up]

time: 156 us -> 156 us (level)
  waiting for transfers between devices: 43.8 us -> 37.7 us
  local copies, waits for them, and re-layouts: 8.87 us -> 13.4 us
  other arithmetic: 11.1 us -> 15.4 us
  starting transfers between devices: 30.4 us -> 27.8 us
    ppermute x27 -> x26, waiting for transfers between devices: 43.8 us -> 37.7 us  [send(): return lax.ppermute(value, AXES, pairs)]
    unnamed x31 -> x39, local copies, waits for them, and re-layouts: 3.22 us -> 6.91 us
    ppermute x27 -> x26, starting transfers between devices: 30.4 us -> 27.8 us  [send(): return lax.ppermute(value, AXES, pairs)]
    another operation x1 -> x3, local copies, waits for them, and re-layouts: 2.8 us -> 5.27 us  [times(): jnp.stack(blocks, 1)]
    slice x1 -> x0, local copies, waits for them, and re-layouts: 1.82 us -> none  [per_device(): x2, nx1a = (x2n[:2], x2n[2:])]
    concatenate x2, other arithmetic: 0.48 us -> 2.15 us  [the longest x1 1.52 us: per_device(): near_pair = after(jnp.concatenate([near_sib, nx1a], 0), *done)]
  transfers between devices with their start and end apart: 27 -> 26, of which waited for: 5 -> 7; matrix products, arithmetic and copies ran while one was open for 30% -> 33% of each run, Pallas kernels for 0% -> 0%
where the time goes in v3:
time: 156 us; the launch traced here: 155 us
  waiting for transfers between devices  37.7 us (24%)
  Pallas kernels  30.4 us (19%)
  starting transfers between devices  27.8 us (18%)
  matrix products  27.6 us (18%)
  other arithmetic  15.4 us (10%)
  local copies, waits for them, and re-layouts  13.4 us (9%)
  between operations  2.54 us (2%)
    ppermute x26, waiting for transfers between devices, send(): return lax.ppermute(value, AXES, pairs)  37.7 us
    pallas_call x1, Pallas kernels, update(): pl.pallas_call(functools.partial(update_kernel, (blocks, len(sources))),...  30.4 us
    ppermute x26, starting transfers between devices, send(): return lax.ppermute(value, AXES, pairs)  27.8 us
    dot_general x3, matrix products, times(): jnp.einsum('pxak,kj->pxaj', jnp.stack(blocks, 1), square, precision=high)  21 us
    unnamed x39, local copies, waits for them, and re-layouts  6.91 us
    another operation x3, local copies, waits for them, and re-layouts, times(): jnp.stack(blocks, 1)  5.27 us
    dot_general x1, matrix products, square_of(): whole = jnp.einsum('ki,kj->ij', lower, lower, precision=high)  3.75 us
    concatenate x1, other arithmetic, per_device(): chip = jnp.concatenate([panel, sib], 0)  3.2 us
  transfers between devices with their start and end apart: 26, of which 7 were waited for; matrix products, arithmetic and copies ran while one was open for 33% of the time, Pallas kernels for 0%

profile of v3, /device:TPU:17, one launch (start us, length us, event | category | flops | bytes accessed | tf_op | source)
XLA Modules:
  0.0 154.9 jit_solution(6780065845474362955)
XLA Ops:
  0.6 3.8 %collective-permute-start.4 = (f32[2,128,1024]{2,1,0:T(8,128)}, f32[2,128,1024]{2,1,0:T(8,128)}, u32[]{:S(2)}, u32[]{:S(2)}) collective-permute-start(f32[2,128,1024]{2,1,0:T(8,128)} %refs_8_.1), channel_id=1, source_target_pairs={{0,16},{1,17},{2,18},{3,19},{4,20},{5,21},{6,22},{7,23},{8,56},{9,... | collective-permute-start | bytes 3145736 | tf_op jit(solution)/shard_map/ppermute | solution.py:29
  4.5 1.4 fusion.36
  7.2 0.2 convert_reduce_fusion
  7.7 0.7 fusion.32
  8.4 0.7 compare_select_fusion.7
  9.1 3.2 %pad_maximum_fusion.2 = f32[4,128,1024]{2,1,0:T(8,128)} fusion(f32[2,128,1024]{2,1,0:T(8,128)S(1)} %collective-permute-done.2.refs_9_, f32[2,128,1024]{2,1,0:T(8,128)} %refs_8_.1), kind=kLoop, calls=%fused_computation.18 | loop fusion | flops 524288 | bytes 4194304 | tf_op jit(solution)/shard_map/concatenate | solution.py:250
  12.3 2.5 %collective-permute-start.3 = (f32[4,128,1024]{2,1,0:T(8,128)}, f32[4,128,1024]{2,1,0:T(8,128)}, u32[]{:S(2)}, u32[]{:S(2)}) collective-permute-start(f32[4,128,1024]{2,1,0:T(8,128)} %pad_maximum_fusion.2), channel_id=1, source_target_pairs={{0,2},{1,3},{2,4},{3,5},{4,6},{5,7},{6,0},{7,1},{8,14},{9,15},{10,... | collective-permute-start | bytes 6291464 | tf_op jit(solution)/shard_map/ppermute | solution.py:29
  15.1 0.5 bitcast_select_fusion.kind
  15.6 0.5 compare_select_fusion.6.left
  16.2 0.6 slice_bitcast_fusion.3
  16.8 1.9 %collective-permute-start.6 = (f32[2,128,1024]{2,1,0:T(8,128)S(1)}, f32[2,128,1024]{2,1,0:T(8,128)S(1)}, u32[]{:S(2)}, u32[]{:S(2)}) collective-permute-start(f32[2,128,1024]{2,1,0:T(8,128)S(1)} %copy-done.1), channel_id=1, source_target_pairs={{0,1},{1,0},{2,3},{3,2},{4,5},{5,4},{6,7},{7,6},{8,9},{9,8},{10,11... | collective-permute-start | bytes 3145736 | tf_op jit(solution)/shard_map/ppermute | solution.py:29
  18.7 0.6 add_multiply_fusion.1.meta
  19.3 0.8 collective-permute-start.5
  20.1 0.9 slice_select_fusion
  21.1 0.8 collective-permute-start.7
  21.9 2.0 %collective-permute-start.1 = (f32[64,1536]{1,0:T(8,128)S(1)}, f32[64,1536]{1,0:T(8,128)S(1)}, u32[]{:S(2)}, u32[]{:S(2)}) collective-permute-start(f32[64,1536]{1,0:T(8,128)S(1)} %get-tuple-element.35), channel_id=1, source_target_pairs={{0,48},{1,49},{2,50},{3,51},{4,52},{5,53},{6,54},{7,55},{8,56},{9,... | collective-permute-start | bytes 1179656 | tf_op jit(solution)/shard_map/ppermute | solution.py:29
  23.9 14.3 %collective-permute-done.3 = f32[4,128,1024]{2,1,0:T(8,128)} collective-permute-done((f32[4,128,1024]{2,1,0:T(8,128)}, f32[4,128,1024]{2,1,0:T(8,128)}, u32[]{:S(2)}, u32[]{:S(2)}) %collective-permute-start.3) | collective-permute-done | bytes 2097184 | tf_op jit(solution)/shard_map/ppermute | solution.py:29
  38.1 2.8 %slice_bitcast_fusion.7 = (f32[2,1,128,1024]{3,2,0,1:T(8,128)}, f32[2,128,1024]{2,1,0:T(8,128)S(1)}, f32[2,128,1024]{2,1,0:T(8,128)S(1)}) fusion(f32[4,128,1024]{2,1,0:T(8,128)} %collective-permute-done.3), kind=kLoop, calls=%fused_computation.123 | loop fusion | bytes 5242880 | tf_op jit(solution)/shard_map/stack | solution.py:199
  40.9 1.5 collective-permute-done.6
  42.4 0.6 pad_maximum_fusion.3
  43.1 1.2 collective-permute-start.9
  44.3 1.3 collective-permute-start.10
  45.6 1.6 %collective-permute-start.8 = (f32[64,1536]{1,0:T(8,128)S(1)}, f32[64,1536]{1,0:T(8,128)S(1)}, u32[]{:S(2)}, u32[]{:S(2)}) collective-permute-start(f32[64,1536]{1,0:T(8,128)S(1)} %get-tuple-element.35), channel_id=1, source_target_pairs={{0,32},{1,33},{2,34},{3,35},{4,36},{5,37},{6,38},{7,39},{8,40},{9,... | collective-permute-start | bytes 1179656 | tf_op jit(solution)/shard_map/ppermute | solution.py:29
  47.2 2.9 %collective-permute-start.12 = (f32[2,128,1024]{2,1,0:T(8,128)S(1)}, f32[2,128,1024]{2,1,0:T(8,128)S(1)}, u32[]{:S(2)}, u32[]{:S(2)}) collective-permute-start(f32[2,128,1024]{2,1,0:T(8,128)S(1)} %copy-done.1), channel_id=1, source_target_pairs={{0,64},{1,65},{2,66},{3,67},{4,68},{5,69},{6,70},{7,71},{8,72},{9,... | collective-permute-start | bytes 3145736 | tf_op jit(solution)/shard_map/ppermute | solution.py:29
  50.1 0.7 collective-permute-start.11
  50.8 7.1 %collective-permute-done.8 = f32[64,1536]{1,0:T(8,128)S(1)} collective-permute-done((f32[64,1536]{1,0:T(8,128)S(1)}, f32[64,1536]{1,0:T(8,128)S(1)}, u32[]{:S(2)}, u32[]{:S(2)}) %collective-permute-start.8) | collective-permute-done | bytes 393248 | tf_op jit(solution)/shard_map/ppermute | solution.py:29
  57.9 1.3 pad_maximum_fusion.8
  59.2 1.2 slice_bitcast_fusion.2
  60.4 9.0 %collective-permute-done.10 = f32[4,128,1024]{2,1,0:T(8,128)S(1)} collective-permute-done((f32[4,128,1024]{2,1,0:T(8,128)S(1)}, f32[4,128,1024]{2,1,0:T(8,128)S(1)}, u32[]{:S(2)}, u32[]{:S(2)}) %collective-permute-start.10) | collective-permute-done | bytes 2097184 | tf_op jit(solution)/shard_map/ppermute | solution.py:29
  69.5 1.3 slice_bitcast_fusion.6
  70.7 1.5 pad_maximum_fusion.5
  72.3 1.3 collective-permute-done.12.refs_16_
  73.5 1.0 copy-done.8
  74.5 1.0 copy-done.10
  75.5 0.9 collective-permute-start.13
  76.4 0.4 collective-permute-start.23
  76.7 1.1 collective-permute-start.22
  77.8 0.4 collective-permute-start.14
  78.2 2.9 %collective-permute-start.20 = (f32[2,128,1024]{2,1,0:T(8,128)}, f32[2,128,1024]{2,1,0:T(8,128)}, u32[]{:S(2)}, u32[]{:S(2)}) collective-permute-start(f32[2,128,1024]{2,1,0:T(8,128)} %copy-done.10), channel_id=1, source_target_pairs={{0,64},{1,65},{2,66},{3,67},{4,68},{5,69},{6,70},{7,71},{8,72},{9,... | collective-permute-start | bytes 3145736 | tf_op jit(solution)/shard_map/ppermute | solution.py:29
  81.2 2.0 %select_bitcast_fusion.1 = (f32[4,1,64,1536]{3,2,0,1:T(8,128)S(1)}, f32[4,1,64,1536]{3,2,0,1:T(8,128)S(1)}) fusion(f32[4,64,1536]{2,1,0:T(8,128)} %collective-permute-done.13, pred[]{:T(512)S(6)} %eq.132, f32[1,64,1536]{2,1,0:T(8,128)} %bitcast.102, f32[1,64,1536]{2,1,0:T(8,128)} %bitcast.106, f32[1,64,1536]{2,1,0:T(8,128)} %bitcast.104, ...), kind=kLoop, calls=%fused_computation.33 | loop fusion | flops 1966080 | bytes 6291457 | tf_op jit(solution)/shard_map/stack | solution.py:279
  83.2 0.3 pad_maximum_fusion.1
  83.5 0.3 copy.12
  83.9 1.0 fusion.18
  84.9 0.6 convolution_bitcast_fusion
  85.5 1.1 collective-permute-start.19
  86.6 0.3 fusion.24
  86.9 3.8 %fusion.14 = f32[1024,1024]{1,0:T(8,128)S(1)} fusion(f32[512,1536]{1,0:T(8,128)S(1)} %bitcast.91), kind=kOutput, calls=%fused_computation.28 | convolution fusion | flops 3221225472 | bytes 6291456 | tf_op jit(solution)/shard_map/ki,kj->ij/dot_general | solution.py:74
  90.6 1.2 fusion.17
  91.9 4.9 %fusion.8 = (bf16[2,2,128,1024]{3,2,1,0:T(8,128)(2,1)}, bf16[2,2,128,1024]{3,2,1,0:T(8,128)(2,1)}) fusion(f32[1024,1024]{1,0:T(8,128)S(1)} %fusion.17, f32[2,1,128,1024]{3,2,0,1:T(8,128)S(1)} %get-tuple-element.73, f32[2,1,128,1024]{3,2,0,1:T(8,128)S(1)} %bitcast.94), kind=kOutput, calls=%fused_computation.16 | convolution fusion | flops 3223846912 | bytes 8388608 | tf_op jit(solution)/shard_map/pxak,kj->pxaj/dot_general | solution.py:199
  96.9 1.1 copy-done.12
  98.0 0.3 copy-done.14
  98.3 8.6 %fusion = (bf16[2,4,128,1024]{3,2,1,0:T(8,128)(2,1)}, bf16[2,4,128,1024]{3,2,1,0:T(8,128)(2,1)}) fusion(f32[1024,1024]{1,0:T(8,128)S(1)} %fusion.17, f32[2,1,128,1024]{3,2,0,1:T(8,128)S(1)} %copy-done.14, f32[2,1,128,1024]{3,2,0,1:T(8,128)S(1)} %copy-done.16, f32[2,1,128,1024]{3,2,0,1:T(8,128)S(1)} %copy-done.12, f32[2,1,128,1024]{3,2,0,1:T(8,128)S(1)} %bitcast.93), kind=kOutput, calls=%fused_computation.2 | convolution fusion | flops 6449790976 | bytes 12582912 | tf_op jit(solution)/shard_map/pxak,kj->pxaj/dot_general | solution.py:199
  107.1 0.2 fusion.45
  107.3 0.6 collective-permute-start.15
  107.9 0.2 copy-done.7
  108.2 0.2 collective-permute-start.18
  108.4 0.3 collective-permute-start.21
  108.7 1.0 collective-permute-done.16.refs_11_
  109.8 0.9 copy-done.15
  110.7 3.5 %collective-permute-done.15 = f32[2,128,1024]{2,1,0:T(8,128)S(1)} collective-permute-done((f32[2,128,1024]{2,1,0:T(8,128)S(1)}, f32[2,128,1024]{2,1,0:T(8,128)S(1)}, u32[]{:S(2)}, u32[]{:S(2)}) %collective-permute-start.15) | collective-permute-done | bytes 1048608 | tf_op jit(solution)/shard_map/ppermute | solution.py:29
  114.2 1.0 copy-done.17
  115.4 1.3 copy.16
  116.7 7.5 %fusion.9 = (bf16[2,2,128,1024]{3,2,1,0:T(8,128)(2,1)}, bf16[2,2,128,1024]{3,2,1,0:T(8,128)(2,1)}) fusion(f32[1024,1024]{1,0:T(8,128)} %copy-done, f32[2,1,128,1024]{3,2,0,1:T(8,128)S(1)} %get-tuple-element.70, f32[2,1,128,1024]{3,2,0,1:T(8,128)} %bitcast.107), kind=kOutput, calls=%fused_computation.17 | convolution fusion | flops 3223846912 | bytes 8388608 | tf_op jit(solution)/shard_map/pxak,kj->pxaj/dot_general | solution.py:199
  124.2 30.4 %shard_map.59 = f32[20,1024,128]{2,1,0:T(8,128)} custom-call(s32[24]{0:T(128)} %get-tuple-element.87.slots, s32[12]{0:T(128)} %compare_select_fusion.6.left, s32[24]{0:T(128)} %get-tuple-element.86.buffer, s32[24]{0:T(128)} %get-tuple-element.85.position, s32[24]{0:T(128)} %bitcast_select_fusion.kind, s32[8]{0:T(128)} %add_multiply_fusion.1.meta, ...), custom_call_target="tpu_custom_call" | custom-call | tf_op jit(solution)/shard_map/pallas_call | solution.py:171
  (71 shorter events, 1.3 us)
Async XLA Ops:
  0.6 18.7 %collective-permute-start.4 = (f32[2,128,1024]{2,1,0:T(8,128)}, f32[2,128,1024]{2,1,0:T(8,128)}, u32[]{:S(2)}, u32[]{:S(2)}) collective-permute-start(f32[2,128,1024]{2,1,0:T(8,128)} %refs_8_.1), channel_id=1, source_target_pairs={{0,16},{1,17},{2,18},{3,19},{4,20},{5,21},{6,22},{7,23},{8,56},{9,... | collective-permute-start | bytes 3145736 | tf_op jit(solution)/shard_map/ppermute | solution.py:29
  4.5 4.7 %collective-permute-start.2 = (f32[2,128,1024]{2,1,0:T(8,128)}, f32[2,128,1024]{2,1,0:T(8,128)S(1)}, u32[]{:S(2)}, u32[]{:S(2)}) collective-permute-start(f32[2,128,1024]{2,1,0:T(8,128)} %refs_8_.1), channel_id=1, source_target_pairs={{0,8},{1,9},{2,10},{3,11},{4,12},{5,13},{6,14},{7,15},{8,0},{9,1},... | collective-permute-start | bytes 3145736 | tf_op jit(solution)/shard_map/ppermute | solution.py:29
  4.5 12.3 %collective-permute-start = (f32[64,1024]{1,0:T(8,128)}, f32[64,1024]{1,0:T(8,128)}, u32[]{:S(2)}, u32[]{:S(2)}) collective-permute-start(f32[64,1024]{1,0:T(8,128)} %param.6), channel_id=1, source_target_pairs={{0,64},{1,65},{2,66},{3,67},{4,68},{5,69},{6,70},{7,71},{8,72},{9,... | collective-permute-start | bytes 786440 | tf_op jit(solution)/shard_map/ppermute | solution.py:29
  9.1 7.7 %copy-start.1 = (f32[2,128,1024]{2,1,0:T(8,128)S(1)}, f32[2,128,1024]{2,1,0:T(8,128)}, u32[]{:S(2)}) copy-start(f32[2,128,1024]{2,1,0:T(8,128)} %refs_8_.1) | copy-start | bytes 3145732
  9.1 11.0 %copy-start.18 = (f32[64,1024]{1,0:T(8,128)S(1)}, f32[64,1024]{1,0:T(8,128)}, u32[]{:S(2)}) copy-start(f32[64,1024]{1,0:T(8,128)} %param.6) | copy-start | bytes 786436
  9.1 10.2 %copy-start.2 = (f32[2,128,1024]{2,1,0:T(8,128)}, f32[2,128,1024]{2,1,0:T(8,128)S(1)}, u32[]{:S(2)}) copy-start(f32[2,128,1024]{2,1,0:T(8,128)S(1)} %collective-permute-done.2.refs_9_) | copy-start | bytes 3145732
  12.3 25.8 %collective-permute-start.3 = (f32[4,128,1024]{2,1,0:T(8,128)}, f32[4,128,1024]{2,1,0:T(8,128)}, u32[]{:S(2)}, u32[]{:S(2)}) collective-permute-start(f32[4,128,1024]{2,1,0:T(8,128)} %pad_maximum_fusion.2), channel_id=1, source_target_pairs={{0,2},{1,3},{2,4},{3,5},{4,6},{5,7},{6,0},{7,1},{8,14},{9,15},{10,... | collective-permute-start | bytes 6291464 | tf_op jit(solution)/shard_map/ppermute | solution.py:29
  16.8 25.6 %collective-permute-start.6 = (f32[2,128,1024]{2,1,0:T(8,128)S(1)}, f32[2,128,1024]{2,1,0:T(8,128)S(1)}, u32[]{:S(2)}, u32[]{:S(2)}) collective-permute-start(f32[2,128,1024]{2,1,0:T(8,128)S(1)} %copy-done.1), channel_id=1, source_target_pairs={{0,1},{1,0},{2,3},{3,2},{4,5},{5,4},{6,7},{7,6},{8,9},{9,8},{10,11... | collective-permute-start | bytes 3145736 | tf_op jit(solution)/shard_map/ppermute | solution.py:29
  19.3 23.8 %collective-permute-start.5 = (f32[2,128,1024]{2,1,0:T(8,128)S(1)}, f32[2,128,1024]{2,1,0:T(8,128)S(1)}, u32[]{:S(2)}, u32[]{:S(2)}) collective-permute-start(f32[2,128,1024]{2,1,0:T(8,128)S(1)} %collective-permute-done.2.refs_9_), channel_id=1, source_target_pairs={{0,16},{1,17},{2,18},{3,19},{4,20},{5,21},{6,22},{7,23},{8,56},{9,... | collective-permute-start | bytes 3145736 | tf_op jit(solution)/shard_map/ppermute | solution.py:29
  21.1 21.9 %collective-permute-start.7 = (f32[64,1536]{1,0:T(8,128)S(1)}, f32[64,1536]{1,0:T(8,128)S(1)}, u32[]{:S(2)}, u32[]{:S(2)}) collective-permute-start(f32[64,1536]{1,0:T(8,128)S(1)} %get-tuple-element.35), channel_id=1, source_target_pairs={{0,16},{1,17},{2,18},{3,19},{4,20},{5,21},{6,22},{7,23},{8,24},{9,... | collective-permute-start | bytes 1179656 | tf_op jit(solution)/shard_map/ppermute | solution.py:29
  21.9 21.2 %collective-permute-start.1 = (f32[64,1536]{1,0:T(8,128)S(1)}, f32[64,1536]{1,0:T(8,128)S(1)}, u32[]{:S(2)}, u32[]{:S(2)}) collective-permute-start(f32[64,1536]{1,0:T(8,128)S(1)} %get-tuple-element.35), channel_id=1, source_target_pairs={{0,48},{1,49},{2,50},{3,51},{4,52},{5,53},{6,54},{7,55},{8,56},{9,... | collective-permute-start | bytes 1179656 | tf_op jit(solution)/shard_map/ppermute | solution.py:29
  43.0 17.4 %copy-start.3 = (f32[64,1536]{1,0:T(8,128)}, f32[64,1536]{1,0:T(8,128)S(1)}, u32[]{:S(2)}) copy-start(f32[64,1536]{1,0:T(8,128)S(1)} %collective-permute-done.7) | copy-start | bytes 1179652
  43.1 17.4 %copy-start.4 = (f32[64,1536]{1,0:T(8,128)}, f32[64,1536]{1,0:T(8,128)S(1)}, u32[]{:S(2)}) copy-start(f32[64,1536]{1,0:T(8,128)S(1)} %collective-permute-done.1) | copy-start | bytes 1179652
  43.1 17.3 %copy-start.6 = (f32[2,128,1024]{2,1,0:T(8,128)}, f32[2,128,1024]{2,1,0:T(8,128)S(1)}, u32[]{:S(2)}) copy-start(f32[2,128,1024]{2,1,0:T(8,128)S(1)} %collective-permute-done.5.refs_13_) | copy-start | bytes 3145732
  43.1 16.1 %collective-permute-start.9 = (f32[4,128,1024]{2,1,0:T(8,128)S(1)}, f32[4,128,1024]{2,1,0:T(8,128)S(1)}, u32[]{:S(2)}, u32[]{:S(2)}) collective-permute-start(f32[4,128,1024]{2,1,0:T(8,128)S(1)} %get-tuple-element.36), channel_id=1, source_target_pairs={{0,8},{1,9},{2,10},{3,11},{4,12},{5,13},{6,14},{7,15},{8,0},{9,1},... | collective-permute-start | bytes 6291464 | tf_op jit(solution)/shard_map/ppermute | solution.py:29
  44.3 25.2 %collective-permute-start.10 = (f32[4,128,1024]{2,1,0:T(8,128)S(1)}, f32[4,128,1024]{2,1,0:T(8,128)S(1)}, u32[]{:S(2)}, u32[]{:S(2)}) collective-permute-start(f32[4,128,1024]{2,1,0:T(8,128)S(1)} %get-tuple-element.37), channel_id=1, source_target_pairs={{0,2},{1,3},{2,4},{3,5},{4,6},{5,7},{6,0},{7,1},{8,14},{9,15},{10,... | collective-permute-start | bytes 6291464 | tf_op jit(solution)/shard_map/ppermute | solution.py:29
  45.6 12.4 %collective-permute-start.8 = (f32[64,1536]{1,0:T(8,128)S(1)}, f32[64,1536]{1,0:T(8,128)S(1)}, u32[]{:S(2)}, u32[]{:S(2)}) collective-permute-start(f32[64,1536]{1,0:T(8,128)S(1)} %get-tuple-element.35), channel_id=1, source_target_pairs={{0,32},{1,33},{2,34},{3,35},{4,36},{5,37},{6,38},{7,39},{8,40},{9,... | collective-permute-start | bytes 1179656 | tf_op jit(solution)/shard_map/ppermute | solution.py:29
  47.2 26.3 %collective-permute-start.12 = (f32[2,128,1024]{2,1,0:T(8,128)S(1)}, f32[2,128,1024]{2,1,0:T(8,128)S(1)}, u32[]{:S(2)}, u32[]{:S(2)}) collective-permute-start(f32[2,128,1024]{2,1,0:T(8,128)S(1)} %copy-done.1), channel_id=1, source_target_pairs={{0,64},{1,65},{2,66},{3,67},{4,68},{5,69},{6,70},{7,71},{8,72},{9,... | collective-permute-start | bytes 3145736 | tf_op jit(solution)/shard_map/ppermute | solution.py:29
  50.1 24.4 %collective-permute-start.11 = (f32[2,128,1024]{2,1,0:T(8,128)}, f32[2,128,1024]{2,1,0:T(8,128)S(1)}, u32[]{:S(2)}, u32[]{:S(2)}) collective-permute-start(f32[2,128,1024]{2,1,0:T(8,128)} %collective-permute-done.4.refs_12_), channel_id=1, source_target_pairs={{0,16},{1,17},{2,18},{3,19},{4,20},{5,21},{6,22},{7,23},{8,56},{9,... | collective-permute-start | bytes 3145736 | tf_op jit(solution)/shard_map/ppermute | solution.py:29
  57.9 2.5 %copy-start.5 = (f32[64,1536]{1,0:T(8,128)}, f32[64,1536]{1,0:T(8,128)S(1)}, u32[]{:S(2)}) copy-start(f32[64,1536]{1,0:T(8,128)S(1)} %collective-permute-done.8) | copy-start | bytes 1179652
  73.5 1.0 copy-start.8
  74.5 1.0 copy-start.10
  75.5 5.7 %collective-permute-start.13 = (f32[4,64,1536]{2,1,0:T(8,128)}, f32[4,64,1536]{2,1,0:T(8,128)}, u32[]{:S(2)}, u32[]{:S(2)}) collective-permute-start(f32[4,64,1536]{2,1,0:T(8,128)} %pad_maximum_fusion.8), channel_id=1, source_target_pairs={{0,8},{1,9},{2,10},{3,11},{4,12},{5,13},{6,14},{7,15},{8,0},{9,1},... | collective-permute-start | bytes 4718600 | tf_op jit(solution)/shard_map/ppermute | solution.py:29
  76.4 30.9 %collective-permute-start.23 = (f32[2,128,1024]{2,1,0:T(8,128)}, f32[2,128,1024]{2,1,0:T(8,128)}, u32[]{:S(2)}, u32[]{:S(2)}) collective-permute-start(f32[2,128,1024]{2,1,0:T(8,128)} %copy-done.8), channel_id=1, source_target_pairs={{0,48},{1,49},{2,50},{3,51},{4,52},{5,53},{6,54},{7,55},{8,56},{9,... | collective-permute-start | bytes 3145736 | tf_op jit(solution)/shard_map/ppermute | solution.py:29
  76.7 31.1 %collective-permute-start.22 = (f32[2,128,1024]{2,1,0:T(8,128)}, f32[2,128,1024]{2,1,0:T(8,128)}, u32[]{:S(2)}, u32[]{:S(2)}) collective-permute-start(f32[2,128,1024]{2,1,0:T(8,128)} %copy-done.8), channel_id=1, source_target_pairs={{0,16},{1,17},{2,18},{3,19},{4,20},{5,21},{6,22},{7,23},{8,24},{9,... | collective-permute-start | bytes 3145736 | tf_op jit(solution)/shard_map/ppermute | solution.py:29
  77.8 29.1 %collective-permute-start.14 = (f32[4,128,1024]{2,1,0:T(8,128)}, f32[4,128,1024]{2,1,0:T(8,128)S(1)}, u32[]{:S(2)}, u32[]{:S(2)}) collective-permute-start(f32[4,128,1024]{2,1,0:T(8,128)} %pad_maximum_fusion.5), channel_id=1, source_target_pairs={{0,2},{1,3},{2,4},{3,5},{4,6},{5,7},{6,0},{7,1},{8,14},{9,15},{10,... | collective-permute-start | bytes 6291464 | tf_op jit(solution)/shard_map/ppermute | solution.py:29
  78.2 29.7 %collective-permute-start.20 = (f32[2,128,1024]{2,1,0:T(8,128)}, f32[2,128,1024]{2,1,0:T(8,128)}, u32[]{:S(2)}, u32[]{:S(2)}) collective-permute-start(f32[2,128,1024]{2,1,0:T(8,128)} %copy-done.10), channel_id=1, source_target_pairs={{0,64},{1,65},{2,66},{3,67},{4,68},{5,69},{6,70},{7,71},{8,72},{9,... | collective-permute-start | bytes 3145736 | tf_op jit(solution)/shard_map/ppermute | solution.py:29
  83.9 1.7 %copy-start.9 = (f32[2,128,1024]{2,1,0:T(8,128)S(1)}, f32[2,128,1024]{2,1,0:T(8,128)}, u32[]{:S(2)}) copy-start(f32[2,128,1024]{2,1,0:T(8,128)} %copy-done.8) | copy-start | bytes 3145732
  85.5 22.8 %collective-permute-start.19 = (f32[2,128,1024]{2,1,0:T(8,128)S(1)}, f32[2,128,1024]{2,1,0:T(8,128)S(1)}, u32[]{:S(2)}, u32[]{:S(2)}) collective-permute-start(f32[2,128,1024]{2,1,0:T(8,128)S(1)} %copy-done.9), channel_id=1, source_target_pairs={{0,8},{1,9},{2,10},{3,11},{4,12},{5,13},{6,14},{7,15},{8,0},{9,1},... | collective-permute-start | bytes 3145736 | tf_op jit(solution)/shard_map/ppermute | solution.py:29
  91.8 5.0 %copy-start = (f32[1024,1024]{1,0:T(8,128)}, f32[1024,1024]{1,0:T(8,128)S(1)}, u32[]{:S(2)}) copy-start(f32[1024,1024]{1,0:T(8,128)S(1)} %fusion.17) | copy-start | bytes 12582916
  91.9 5.0 %copy-start.16 = (f32[2,1,128,1024]{3,2,0,1:T(8,128)S(1)}, f32[2,1,128,1024]{3,2,0,1:T(8,128)}, u32[]{:S(2)}) copy-start(f32[2,1,128,1024]{3,2,0,1:T(8,128)} %get-tuple-element.79) | copy-start | bytes 3145732
  96.8 1.2 copy-start.12
  96.8 1.5 copy-start.14
  98.3 8.6 %copy-start.11 = (f32[2,128,1024]{2,1,0:T(8,128)S(1)}, f32[2,128,1024]{2,1,0:T(8,128)}, u32[]{:S(2)}) copy-start(f32[2,128,1024]{2,1,0:T(8,128)} %copy-done.10) | copy-start | bytes 3145732
  106.9 1.2 copy-start.7
  107.0 2.7 %collective-permute-start.16 = (f32[2,128,1024]{2,1,0:T(8,128)S(1)}, f32[2,128,1024]{2,1,0:T(8,128)S(1)}, u32[]{:S(2)}, u32[]{:S(2)}) collective-permute-start(f32[2,128,1024]{2,1,0:T(8,128)S(1)} %copy-done.11), channel_id=1, source_target_pairs={{0,8},{1,9},{2,10},{3,11},{4,12},{5,13},{6,14},{7,15},{8,0},{9,1},... | collective-permute-start | bytes 3145736 | tf_op jit(solution)/shard_map/ppermute | solution.py:29
  107.3 6.9 %collective-permute-start.15 = (f32[2,128,1024]{2,1,0:T(8,128)S(1)}, f32[2,128,1024]{2,1,0:T(8,128)S(1)}, u32[]{:S(2)}, u32[]{:S(2)}) collective-permute-start(f32[2,128,1024]{2,1,0:T(8,128)S(1)} %get-tuple-element.42), channel_id=1, source_target_pairs={{0,8},{1,9},{2,10},{3,11},{4,12},{5,13},{6,14},{7,15},{8,0},{9,1},... | collective-permute-start | bytes 3145736 | tf_op jit(solution)/shard_map/ppermute | solution.py:29
  107.8 16.4 %collective-permute-start.17 = (f32[2,128,1024]{2,1,0:T(8,128)}, f32[2,128,1024]{2,1,0:T(8,128)}, u32[]{:S(2)}, u32[]{:S(2)}) collective-permute-start(f32[2,128,1024]{2,1,0:T(8,128)} %collective-permute-done.4.refs_12_), channel_id=1, source_target_pairs={{0,8},{1,9},{2,10},{3,11},{4,12},{5,13},{6,14},{7,15},{8,0},{9,1},... | collective-permute-start | bytes 3145736 | tf_op jit(solution)/shard_map/ppermute | solution.py:29
  108.2 16.0 %collective-permute-start.18 = (f32[2,128,1024]{2,1,0:T(8,128)S(1)}, f32[2,128,1024]{2,1,0:T(8,128)}, u32[]{:S(2)}, u32[]{:S(2)}) collective-permute-start(f32[2,128,1024]{2,1,0:T(8,128)S(1)} %copy-done.7), channel_id=1, source_target_pairs={{0,8},{1,9},{2,10},{3,11},{4,12},{5,13},{6,14},{7,15},{8,0},{9,1},... | collective-permute-start | bytes 3145736 | tf_op jit(solution)/shard_map/ppermute | solution.py:29
  108.3 1.3 copy-start.13
  108.4 15.9 %collective-permute-start.21 = (f32[2,128,1024]{2,1,0:T(8,128)}, f32[2,128,1024]{2,1,0:T(8,128)}, u32[]{:S(2)}, u32[]{:S(2)}) collective-permute-start(f32[2,128,1024]{2,1,0:T(8,128)} %collective-permute-done.20.refs_18_), channel_id=1, source_target_pairs={{0,8},{1,9},{2,10},{3,11},{4,12},{5,13},{6,14},{7,15},{8,0},{9,1},... | collective-permute-start | bytes 3145736 | tf_op jit(solution)/shard_map/ppermute | solution.py:29
  109.7 1.0 copy-start.15
  109.7 14.5 %collective-permute-start.24 = (f32[2,128,1024]{2,1,0:T(8,128)}, f32[2,128,1024]{2,1,0:T(8,128)}, u32[]{:S(2)}, u32[]{:S(2)}) collective-permute-start(f32[2,128,1024]{2,1,0:T(8,128)} %collective-permute-done.22.refs_20_), channel_id=1, source_target_pairs={{0,8},{1,9},{2,10},{3,11},{4,12},{5,13},{6,14},{7,15},{8,0},{9,1},... | collective-permute-start | bytes 3145736 | tf_op jit(solution)/shard_map/ppermute | solution.py:29
  114.2 1.1 copy-start.17
  115.2 9.0 %collective-permute-start.25 = (f32[2,128,1024]{2,1,0:T(8,128)}, f32[2,128,1024]{2,1,0:T(8,128)}, u32[]{:S(2)}, u32[]{:S(2)}) collective-permute-start(f32[2,128,1024]{2,1,0:T(8,128)} %collective-permute-done.23.refs_21_), channel_id=1, source_target_pairs={{0,8},{1,9},{2,10},{3,11},{4,12},{5,13},{6,14},{7,15},{8,0},{9,1},... | collective-permute-start | bytes 3145736 | tf_op jit(solution)/shard_map/ppermute | solution.py:29

commit v4 on v3

--- a/solution.py
+++ b/solution.py
@@ -247,19 +247,19 @@
     upper = jnp.where(far == 0, pivot_inverse, other)[:, :half]
     lower = jnp.where(far == 0, other, pivot_inverse)
     mine = jnp.concatenate([lower, upper], 1)
-    chip = jnp.concatenate([panel, sib], 0)
-    x1 = send(chip, along_x)
+    x1a = send(panel, along_x)
+    x1b = send(after(sib, x1a), along_x)
     z1b = send(after(sib, z1a), along_z)
     from_down = send(mine, turn_z(1))
     from_up = send(mine, turn_z(-1))
 
-    done = (x1, z1a, z1b, near_own, from_down, from_up, *tables)
+    done = (x1a, x1b, z1a, z1b, near_own, from_down, from_up, *tables)
     z2 = send(after(z1a, *done), along_z)
     across = send(after(mine, *done), turn_z(2))
-    x2n = send(after(jnp.concatenate([x1[:2], near_own], 0), *done), along_x)
+    x2n = send(after(jnp.concatenate([x1a, near_own], 0), *done), along_x)
     far_own = send(after(panel, *done), far_y)
     quarters = jnp.stack([mine, from_up, across, from_down], 0)
-    both_sib = swap(after(jnp.concatenate([near_own, x1[2:]], 0), *done))
+    both_sib = swap(after(jnp.concatenate([near_own, x1b], 0), *done))
     near_sib, sx1 = both_sib[:2], both_sib[2:]
     x2, nx1a = x2n[:2], x2n[2:]
 
@@ -279,18 +279,19 @@
     whole = jnp.stack([first, second], 1).reshape(half, ORDER + half)
     lower, upper = whole[:, :ORDER], whole[:, ORDER:]
     square = square_of(lower, upper)
-    own_left = times([panel, x1[:2], sx1, x2], square)
+    own_first = times([panel, x1a], square)
+    own_second = times([sx1, x2], square)
     near_first = times([near_own, nx1a], square)
     solved = solve(panel, lower, upper, z)
-    ready = (solved, *own_left, *near_first)
+    ready = (solved, *own_first, *near_first)
     nsx1 = swap(after(nx1b, *ready))
     near_second = times([nsx1, nx2], square)
-    sfz_down, sfz_up, sfz2 = [swap(after(part, *ready)) for part in (fz_down, fz_up, fz2)]
+    sfz_down, sfz_up, sfz2 = [swap(after(part, *ready, *own_second)) for part in (fz_down, fz_up, fz2)]
 
     sources = [panel, sib, z2, sz2, z1a, z1b, sz1a, sz1b]
     sources += [far_own, far_sib, fz2, sfz2, fz_down, fz_up, sfz_down, sfz_up]
-    lefts = own_left + near_first + near_second
-    return solved, update(trailing, (4, 2, 2), lefts, sources, tables)
+    lefts = own_first + own_second + near_first + near_second
+    return solved, update(trailing, (2, 2, 2, 2), lefts, sources, tables)
 
 
 def solution(mesh):

time: 156 us -> 159 us (1.019)
  waiting for transfers between devices: 37.7 us -> 44.8 us
  local copies, waits for them, and re-layouts: 13.4 us -> 9.68 us
  other arithmetic: 15.4 us -> 12.8 us
    ppermute x26 -> x27, waiting for transfers between devices: 37.7 us -> 44.8 us  [send(): return lax.ppermute(value, AXES, pairs)]
    concatenate x2 -> x1, other arithmetic: 3.83 us -> 0.63 us  [per_device(): both_sib = swap(after(jnp.concatenate([near_own, x1b], 0), *done))]
    another operation x3 -> x2, local copies, waits for them, and re-layouts: 5.27 us -> 2.78 us  [times(): jnp.stack(blocks, 1)]
    ppermute x26 -> x27, starting transfers between devices: 27.8 us -> 29 us  [send(): return lax.ppermute(value, AXES, pairs)]
    unnamed x39 -> x35, local copies, waits for them, and re-layouts: 6.91 us -> 5.84 us
    dot_general x3 -> x4, matrix products: 21 us -> 21.7 us  [times(): jnp.einsum('pxak,kj->pxaj', jnp.stack(blocks, 1), square, precision=high)]
  transfers between devices with their start and end apart: 26 -> 27, of which waited for: 7 -> 9; matrix products, arithmetic and copies ran while one was open for 33% -> 29% of each run, Pallas kernels for 0% -> 0%
where the time goes in v4:
time: 159 us; the launch traced here: 158 us
  waiting for transfers between devices  44.8 us (28%)
  Pallas kernels  31 us (19%)
  starting transfers between devices  29 us (18%)
  matrix products  28.3 us (18%)
  other arithmetic  12.8 us (8%)
  local copies, waits for them, and re-layouts  9.68 us (6%)
  between operations  2.5 us (2%)
    ppermute x27, waiting for transfers between devices, send(): return lax.ppermute(value, AXES, pairs)  44.8 us
    pallas_call x1, Pallas kernels, update(): pl.pallas_call(functools.partial(update_kernel, (blocks, len(sources))),...  31 us
    ppermute x27, starting transfers between devices, send(): return lax.ppermute(value, AXES, pairs)  29 us
    dot_general x4, matrix products, times(): jnp.einsum('pxak,kj->pxaj', jnp.stack(blocks, 1), square, precision=high)  21.7 us
    unnamed x35, local copies, waits for them, and re-layouts  5.84 us
    dot_general x1, matrix products, square_of(): whole = jnp.einsum('ki,kj->ij', lower, lower, precision=high)  3.68 us
  transfers between devices with their start and end apart: 27, of which 9 were waited for; matrix products, arithmetic and copies ran while one was open for 29% of the time, Pallas kernels for 0%

profile of v4, /device:TPU:17, one launch (start us, length us, event | category | flops | bytes accessed | tf_op | source)
XLA Modules:
  0.0 158.0 jit_solution(312076874470540167)
XLA Ops:
  0.6 3.8 %collective-permute-start.5 = (f32[2,128,1024]{2,1,0:T(8,128)}, f32[2,128,1024]{2,1,0:T(8,128)S(1)}, u32[]{:S(2)}, u32[]{:S(2)}) collective-permute-start(f32[2,128,1024]{2,1,0:T(8,128)} %refs_10_.1), channel_id=1, source_target_pairs={{0,16},{1,17},{2,18},{3,19},{4,20},{5,21},{6,22},{7,23},{8,56},{9,... | collective-permute-start | bytes 3145736 | tf_op jit(solution)/shard_map/ppermute | solution.py:29
  4.5 2.5 %collective-permute-start.2 = (f32[2,128,1024]{2,1,0:T(8,128)}, f32[2,128,1024]{2,1,0:T(8,128)S(1)}, u32[]{:S(2)}, u32[]{:S(2)}) collective-permute-start(f32[2,128,1024]{2,1,0:T(8,128)} %refs_10_.1), channel_id=1, source_target_pairs={{0,2},{1,3},{2,4},{3,5},{4,6},{5,7},{6,0},{7,1},{8,14},{9,15},{10,... | collective-permute-start | bytes 3145736 | tf_op jit(solution)/shard_map/ppermute | solution.py:29
  7.0 0.7 fusion.36
  7.7 1.4 fusion.40
  10.7 0.7 compare_select_fusion.7
  11.9 0.6 compare_select_fusion.6.left
  12.5 0.6 slice_bitcast_fusion.3
  13.1 3.9 %collective-permute-done = f32[64,1024]{1,0:T(8,128)S(1)} collective-permute-done((f32[64,1024]{1,0:T(8,128)}, f32[64,1024]{1,0:T(8,128)S(1)}, u32[]{:S(2)}, u32[]{:S(2)}) %collective-permute-start) | collective-permute-done | bytes 262176 | tf_op jit(solution)/shard_map/ppermute | solution.py:29
  17.0 1.0 collective-permute-start.7
  17.9 1.1 collective-permute-done.2
  19.0 3.0 %collective-permute-start.4 = (f32[2,128,1024]{2,1,0:T(8,128)}, f32[2,128,1024]{2,1,0:T(8,128)S(1)}, u32[]{:S(2)}, u32[]{:S(2)}) collective-permute-start(f32[2,128,1024]{2,1,0:T(8,128)} %collective-permute-done.3.refs_11_), channel_id=1, source_target_pairs={{0,2},{1,3},{2,4},{3,5},{4,6},{5,7},{6,0},{7,1},{8,14},{9,15},{10,... | collective-permute-start | bytes 3145736 | tf_op jit(solution)/shard_map/ppermute | solution.py:29
  22.0 0.6 add_multiply_fusion.1.meta
  22.6 0.8 collective-permute-start.6
  23.4 0.9 slice_select_fusion
  24.3 1.0 broadcast_select_fusion
  25.4 0.8 collective-permute-start.8
  26.1 2.0 %collective-permute-start.1 = (f32[64,1536]{1,0:T(8,128)S(1)}, f32[64,1536]{1,0:T(8,128)S(1)}, u32[]{:S(2)}, u32[]{:S(2)}) collective-permute-start(f32[64,1536]{1,0:T(8,128)S(1)} %get-tuple-element.37), channel_id=1, source_target_pairs={{0,48},{1,49},{2,50},{3,51},{4,52},{5,53},{6,54},{7,55},{8,56},{9,... | collective-permute-start | bytes 1179656 | tf_op jit(solution)/shard_map/ppermute | solution.py:29
  28.1 0.5 bitcast_select_fusion.kind
  28.7 13.0 %collective-permute-done.7 = f32[2,128,1024]{2,1,0:T(8,128)S(1)} collective-permute-done((f32[2,128,1024]{2,1,0:T(8,128)}, f32[2,128,1024]{2,1,0:T(8,128)S(1)}, u32[]{:S(2)}, u32[]{:S(2)}) %collective-permute-start.7) | collective-permute-done | bytes 1048608 | tf_op jit(solution)/shard_map/ppermute | solution.py:29
  41.7 0.6 pad_maximum_fusion.1
  42.3 0.5 copy-done.2
  42.8 2.4 %collective-permute-done.1 = f32[64,1536]{1,0:T(8,128)S(1)} collective-permute-done((f32[64,1536]{1,0:T(8,128)S(1)}, f32[64,1536]{1,0:T(8,128)S(1)}, u32[]{:S(2)}, u32[]{:S(2)}) %collective-permute-start.1) | collective-permute-done | bytes 393248 | tf_op jit(solution)/shard_map/ppermute | solution.py:29
  45.2 1.5 collective-permute-start.10
  46.7 2.7 %collective-permute-start.11 = (f32[4,128,1024]{2,1,0:T(8,128)S(1)}, f32[4,128,1024]{2,1,0:T(8,128)S(1)}, u32[]{:S(2)}, u32[]{:S(2)}) collective-permute-start(f32[4,128,1024]{2,1,0:T(8,128)S(1)} %get-tuple-element.39), channel_id=1, source_target_pairs={{0,2},{1,3},{2,4},{3,5},{4,6},{5,7},{6,0},{7,1},{8,14},{9,15},{10,... | collective-permute-start | bytes 6291464 | tf_op jit(solution)/shard_map/ppermute | solution.py:29
  49.4 0.4 collective-permute-start.9
  49.8 0.7 collective-permute-start.12
  50.6 11.2 %collective-permute-done.9 = f32[64,1536]{1,0:T(8,128)S(1)} collective-permute-done((f32[64,1536]{1,0:T(8,128)S(1)}, f32[64,1536]{1,0:T(8,128)S(1)}, u32[]{:S(2)}, u32[]{:S(2)}) %collective-permute-start.9) | collective-permute-done | bytes 393248 | tf_op jit(solution)/shard_map/ppermute | solution.py:29
  61.8 1.3 pad_maximum_fusion.8
  63.1 1.2 slice_bitcast_fusion.2
  64.2 8.2 %collective-permute-done.11 = f32[4,128,1024]{2,1,0:T(8,128)S(1)} collective-permute-done((f32[4,128,1024]{2,1,0:T(8,128)S(1)}, f32[4,128,1024]{2,1,0:T(8,128)S(1)}, u32[]{:S(2)}, u32[]{:S(2)}) %collective-permute-start.11) | collective-permute-done | bytes 2097184 | tf_op jit(solution)/shard_map/ppermute | solution.py:29
  72.4 1.6 %slice_bitcast_fusion.6 = (f32[2,1,128,1024]{3,2,0,1:T(8,128)}, f32[2,1,128,1024]{3,2,0,1:T(8,128)}, f32[2,128,1024]{2,1,0:T(8,128)S(1)}) fusion(f32[4,128,1024]{2,1,0:T(8,128)S(1)} %collective-permute-done.11), kind=kLoop, calls=%fused_computation.128 | loop fusion | bytes 5242880 | tf_op jit(solution)/shard_map/stack | solution.py:199
  74.0 1.4 pad_maximum_fusion.3
  75.4 0.4 collective-permute-done.13.refs_18_
  75.9 0.5 copy-done.11
  76.4 1.0 copy-done.13
  77.4 1.7 %collective-permute-start.14 = (f32[4,64,1536]{2,1,0:T(8,128)}, f32[4,64,1536]{2,1,0:T(8,128)}, u32[]{:S(2)}, u32[]{:S(2)}) collective-permute-start(f32[4,64,1536]{2,1,0:T(8,128)} %pad_maximum_fusion.8), channel_id=1, source_target_pairs={{0,8},{1,9},{2,10},{3,11},{4,12},{5,13},{6,14},{7,15},{8,0},{9,1},... | collective-permute-start | bytes 4718600 | tf_op jit(solution)/shard_map/ppermute | solution.py:29
  79.1 1.1 collective-permute-start.24
  80.2 0.4 collective-permute-start.23
  80.5 1.6 %collective-permute-start.15 = (f32[4,128,1024]{2,1,0:T(8,128)}, f32[4,128,1024]{2,1,0:T(8,128)S(1)}, u32[]{:S(2)}, u32[]{:S(2)}) collective-permute-start(f32[4,128,1024]{2,1,0:T(8,128)} %pad_maximum_fusion.3), channel_id=1, source_target_pairs={{0,2},{1,3},{2,4},{3,5},{4,6},{5,7},{6,0},{7,1},{8,14},{9,15},{10,... | collective-permute-start | bytes 6291464 | tf_op jit(solution)/shard_map/ppermute | solution.py:29
  82.1 0.3 collective-permute-done.14
  82.5 0.4 collective-permute-start.20
  82.8 1.8 %select_bitcast_fusion.1 = (f32[4,1,64,1536]{3,2,0,1:T(8,128)S(1)}, f32[4,1,64,1536]{3,2,0,1:T(8,128)S(1)}) fusion(f32[4,64,1536]{2,1,0:T(8,128)} %collective-permute-done.14, pred[]{:T(512)S(6)} %eq.132, f32[1,64,1536]{2,1,0:T(8,128)S(1)} %bitcast.110, f32[1,64,1536]{2,1,0:T(8,128)} %bitcast.114, f32[1,64,1536]{2,1,0:T(8,128)S(1)} %bitcast.112, ...), kind=kLoop, calls=%fused_computation.39 | loop fusion | flops 1966080 | bytes 6291457 | tf_op jit(solution)/shard_map/stack | solution.py:279
  85.0 1.0 fusion.22
  86.1 0.6 convolution_bitcast_fusion
  86.7 0.3 fusion.28
  87.1 3.7 %fusion.18 = f32[1024,1024]{1,0:T(8,128)S(1)} fusion(f32[512,1536]{1,0:T(8,128)S(1)} %bitcast.96), kind=kOutput, calls=%fused_computation.34 | convolution fusion | flops 3221225472 | bytes 6291456 | tf_op jit(solution)/shard_map/ki,kj->ij/dot_general | solution.py:74
  90.8 1.2 fusion.21
  92.1 0.3 copy-done.5
  92.3 4.7 %fusion.10 = (bf16[2,2,128,1024]{3,2,1,0:T(8,128)(2,1)}, bf16[2,2,128,1024]{3,2,1,0:T(8,128)(2,1)}) fusion(f32[1024,1024]{1,0:T(8,128)S(1)} %fusion.21, f32[2,1,128,1024]{3,2,0,1:T(8,128)S(1)} %copy-done.5, f32[2,1,128,1024]{3,2,0,1:T(8,128)S(1)} %bitcast.100), kind=kOutput, calls=%fused_computation.19 | convolution fusion | flops 3223846912 | bytes 8388608 | tf_op jit(solution)/shard_map/pxak,kj->pxaj/dot_general | solution.py:199
  97.1 4.7 %fusion.8 = (bf16[2,2,128,1024]{3,2,1,0:T(8,128)(2,1)}, bf16[2,2,128,1024]{3,2,1,0:T(8,128)(2,1)}) fusion(f32[1024,1024]{1,0:T(8,128)S(1)} %fusion.21, f32[2,1,128,1024]{3,2,0,1:T(8,128)S(1)} %bitcast.99, f32[2,1,128,1024]{3,2,0,1:T(8,128)S(1)} %bitcast.98), kind=kOutput, calls=%fused_computation.17 | convolution fusion | flops 3223846912 | bytes 8388608 | tf_op jit(solution)/shard_map/pxak,kj->pxaj/dot_general | solution.py:199
  101.8 4.2 %collective-permute-done.15 = f32[4,128,1024]{2,1,0:T(8,128)S(1)} collective-permute-done((f32[4,128,1024]{2,1,0:T(8,128)}, f32[4,128,1024]{2,1,0:T(8,128)S(1)}, u32[]{:S(2)}, u32[]{:S(2)}) %collective-permute-start.15) | collective-permute-done | bytes 2097184 | tf_op jit(solution)/shard_map/ppermute | solution.py:29
  106.0 2.5 %collective-permute-start.17 = (f32[2,128,1024]{2,1,0:T(8,128)S(1)}, f32[2,128,1024]{2,1,0:T(8,128)S(1)}, u32[]{:S(2)}, u32[]{:S(2)}) collective-permute-start(f32[2,128,1024]{2,1,0:T(8,128)S(1)} %copy-done.12), channel_id=1, source_target_pairs={{0,8},{1,9},{2,10},{3,11},{4,12},{5,13},{6,14},{7,15},{8,0},{9,1},... | collective-permute-start | bytes 3145736 | tf_op jit(solution)/shard_map/ppermute | solution.py:29
  108.8 0.3 collective-permute-start.16
  109.1 4.8 %fusion.9 = (bf16[2,2,128,1024]{3,2,1,0:T(8,128)(2,1)}, bf16[2,2,128,1024]{3,2,1,0:T(8,128)(2,1)}) fusion(f32[1024,1024]{1,0:T(8,128)S(1)} %fusion.21, f32[2,1,128,1024]{3,2,0,1:T(8,128)S(1)} %copy-done.4, f32[2,1,128,1024]{3,2,0,1:T(8,128)S(1)} %copy-done.6), kind=kOutput, calls=%fused_computation.18 | convolution fusion | flops 3223846912 | bytes 8388608 | tf_op jit(solution)/shard_map/pxak,kj->pxaj/dot_general | solution.py:199
  113.9 0.5 collective-permute-start.18
  114.5 0.4 collective-permute-start.22
  115.0 0.6 copy-done.14
  115.5 0.4 collective-permute-start.25
  116.0 0.6 copy-done.15
  116.6 1.0 copy-done.16
  117.6 0.4 collective-permute-start.26
  118.0 1.3 copy.18
  119.3 7.5 %fusion.11 = (bf16[2,2,128,1024]{3,2,1,0:T(8,128)(2,1)}, bf16[2,2,128,1024]{3,2,1,0:T(8,128)(2,1)}) fusion(f32[1024,1024]{1,0:T(8,128)} %copy-done, f32[2,1,128,1024]{3,2,0,1:T(8,128)S(1)} %get-tuple-element.70, f32[2,1,128,1024]{3,2,0,1:T(8,128)} %bitcast.115), kind=kOutput, calls=%fused_computation.20 | convolution fusion | flops 3223846912 | bytes 8388608 | tf_op jit(solution)/shard_map/pxak,kj->pxaj/dot_general | solution.py:199
  126.8 31.0 %shard_map.59 = f32[20,1024,128]{2,1,0:T(8,128)} custom-call(s32[24]{0:T(128)} %get-tuple-element.88.slots, s32[12]{0:T(128)} %compare_select_fusion.6.left, s32[24]{0:T(128)} %get-tuple-element.87.buffer, s32[24]{0:T(128)} %get-tuple-element.86.position, s32[24]{0:T(128)} %bitcast_select_fusion.kind, s32[8]{0:T(128)} %add_multiply_fusion.1.meta, ...), custom_call_target="tpu_custom_call" | custom-call | tf_op jit(solution)/shard_map/pallas_call | solution.py:171
  (68 shorter events, 1.6 us)
Async XLA Ops:
  0.6 22.0 %collective-permute-start.5 = (f32[2,128,1024]{2,1,0:T(8,128)}, f32[2,128,1024]{2,1,0:T(8,128)S(1)}, u32[]{:S(2)}, u32[]{:S(2)}) collective-permute-start(f32[2,128,1024]{2,1,0:T(8,128)} %refs_10_.1), channel_id=1, source_target_pairs={{0,16},{1,17},{2,18},{3,19},{4,20},{5,21},{6,22},{7,23},{8,56},{9,... | collective-permute-start | bytes 3145736 | tf_op jit(solution)/shard_map/ppermute | solution.py:29
  4.5 13.5 %collective-permute-start.3 = (f32[2,128,1024]{2,1,0:T(8,128)}, f32[2,128,1024]{2,1,0:T(8,128)}, u32[]{:S(2)}, u32[]{:S(2)}) collective-permute-start(f32[2,128,1024]{2,1,0:T(8,128)} %refs_10_.1), channel_id=1, source_target_pairs={{0,8},{1,9},{2,10},{3,11},{4,12},{5,13},{6,14},{7,15},{8,0},{9,1},... | collective-permute-start | bytes 3145736 | tf_op jit(solution)/shard_map/ppermute | solution.py:29
  4.5 14.5 %collective-permute-start.2 = (f32[2,128,1024]{2,1,0:T(8,128)}, f32[2,128,1024]{2,1,0:T(8,128)S(1)}, u32[]{:S(2)}, u32[]{:S(2)}) collective-permute-start(f32[2,128,1024]{2,1,0:T(8,128)} %refs_10_.1), channel_id=1, source_target_pairs={{0,2},{1,3},{2,4},{3,5},{4,6},{5,7},{6,0},{7,1},{8,14},{9,15},{10,... | collective-permute-start | bytes 3145736 | tf_op jit(solution)/shard_map/ppermute | solution.py:29
  6.9 10.0 %collective-permute-start = (f32[64,1024]{1,0:T(8,128)}, f32[64,1024]{1,0:T(8,128)S(1)}, u32[]{:S(2)}, u32[]{:S(2)}) collective-permute-start(f32[64,1024]{1,0:T(8,128)} %param.6), channel_id=1, source_target_pairs={{0,64},{1,65},{2,66},{3,67},{4,68},{5,69},{6,70},{7,71},{8,72},{9,... | collective-permute-start | bytes 786440 | tf_op jit(solution)/shard_map/ppermute | solution.py:29
  17.0 24.7 %collective-permute-start.7 = (f32[2,128,1024]{2,1,0:T(8,128)}, f32[2,128,1024]{2,1,0:T(8,128)S(1)}, u32[]{:S(2)}, u32[]{:S(2)}) collective-permute-start(f32[2,128,1024]{2,1,0:T(8,128)} %refs_10_.1), channel_id=1, source_target_pairs={{0,1},{1,0},{2,3},{3,2},{4,5},{5,4},{6,7},{7,6},{8,9},{9,8},{10,11... | collective-permute-start | bytes 3145736 | tf_op jit(solution)/shard_map/ppermute | solution.py:29
  19.0 22.7 %collective-permute-start.4 = (f32[2,128,1024]{2,1,0:T(8,128)}, f32[2,128,1024]{2,1,0:T(8,128)S(1)}, u32[]{:S(2)}, u32[]{:S(2)}) collective-permute-start(f32[2,128,1024]{2,1,0:T(8,128)} %collective-permute-done.3.refs_11_), channel_id=1, source_target_pairs={{0,2},{1,3},{2,4},{3,5},{4,6},{5,7},{6,0},{7,1},{8,14},{9,15},{10,... | collective-permute-start | bytes 3145736 | tf_op jit(solution)/shard_map/ppermute | solution.py:29
  22.6 5.5 %copy-start.8 = (f32[2,128,1024]{2,1,0:T(8,128)}, f32[2,128,1024]{2,1,0:T(8,128)S(1)}, u32[]{:S(2)}) copy-start(f32[2,128,1024]{2,1,0:T(8,128)S(1)} %collective-permute-done.5.refs_14_) | copy-start | bytes 3145732
  22.6 22.6 %collective-permute-start.6 = (f32[2,128,1024]{2,1,0:T(8,128)}, f32[2,128,1024]{2,1,0:T(8,128)}, u32[]{:S(2)}, u32[]{:S(2)}) collective-permute-start(f32[2,128,1024]{2,1,0:T(8,128)} %collective-permute-done.3.refs_11_), channel_id=1, source_target_pairs={{0,16},{1,17},{2,18},{3,19},{4,20},{5,21},{6,22},{7,23},{8,56},{9,... | collective-permute-start | bytes 3145736 | tf_op jit(solution)/shard_map/ppermute | solution.py:29
  25.4 17.4 %collective-permute-start.8 = (f32[64,1536]{1,0:T(8,128)S(1)}, f32[64,1536]{1,0:T(8,128)S(1)}, u32[]{:S(2)}, u32[]{:S(2)}) collective-permute-start(f32[64,1536]{1,0:T(8,128)S(1)} %get-tuple-element.37), channel_id=1, source_target_pairs={{0,16},{1,17},{2,18},{3,19},{4,20},{5,21},{6,22},{7,23},{8,24},{9,... | collective-permute-start | bytes 1179656 | tf_op jit(solution)/shard_map/ppermute | solution.py:29
  26.1 19.1 %collective-permute-start.1 = (f32[64,1536]{1,0:T(8,128)S(1)}, f32[64,1536]{1,0:T(8,128)S(1)}, u32[]{:S(2)}, u32[]{:S(2)}) collective-permute-start(f32[64,1536]{1,0:T(8,128)S(1)} %get-tuple-element.37), channel_id=1, source_target_pairs={{0,48},{1,49},{2,50},{3,51},{4,52},{5,53},{6,54},{7,55},{8,56},{9,... | collective-permute-start | bytes 1179656 | tf_op jit(solution)/shard_map/ppermute | solution.py:29
  28.7 21.2 %copy-start.9 = (f32[2,128,1024]{2,1,0:T(8,128)S(1)}, f32[2,128,1024]{2,1,0:T(8,128)}, u32[]{:S(2)}) copy-start(f32[2,128,1024]{2,1,0:T(8,128)} %copy-done.8) | copy-start | bytes 3145732
  28.7 21.9 %copy-start.1 = (f32[2,128,1024]{2,1,0:T(8,128)S(1)}, f32[2,128,1024]{2,1,0:T(8,128)}, u32[]{:S(2)}) copy-start(f32[2,128,1024]{2,1,0:T(8,128)} %refs_10_.1) | copy-start | bytes 3145732
  41.6 1.1 copy-start.2
  45.2 17.8 %collective-permute-start.10 = (f32[4,128,1024]{2,1,0:T(8,128)S(1)}, f32[4,128,1024]{2,1,0:T(8,128)S(1)}, u32[]{:S(2)}, u32[]{:S(2)}) collective-permute-start(f32[4,128,1024]{2,1,0:T(8,128)S(1)} %get-tuple-element.38), channel_id=1, source_target_pairs={{0,8},{1,9},{2,10},{3,11},{4,12},{5,13},{6,14},{7,15},{8,0},{9,1},... | collective-permute-start | bytes 6291464 | tf_op jit(solution)/shard_map/ppermute | solution.py:29
  46.7 25.7 %collective-permute-start.11 = (f32[4,128,1024]{2,1,0:T(8,128)S(1)}, f32[4,128,1024]{2,1,0:T(8,128)S(1)}, u32[]{:S(2)}, u32[]{:S(2)}) collective-permute-start(f32[4,128,1024]{2,1,0:T(8,128)S(1)} %get-tuple-element.39), channel_id=1, source_target_pairs={{0,2},{1,3},{2,4},{3,5},{4,6},{5,7},{6,0},{7,1},{8,14},{9,15},{10,... | collective-permute-start | bytes 6291464 | tf_op jit(solution)/shard_map/ppermute | solution.py:29
  49.4 12.3 %collective-permute-start.9 = (f32[64,1536]{1,0:T(8,128)S(1)}, f32[64,1536]{1,0:T(8,128)S(1)}, u32[]{:S(2)}, u32[]{:S(2)}) collective-permute-start(f32[64,1536]{1,0:T(8,128)S(1)} %get-tuple-element.37), channel_id=1, source_target_pairs={{0,32},{1,33},{2,34},{3,35},{4,36},{5,37},{6,38},{7,39},{8,40},{9,... | collective-permute-start | bytes 1179656 | tf_op jit(solution)/shard_map/ppermute | solution.py:29
  49.8 25.6 %collective-permute-start.12 = (f32[2,128,1024]{2,1,0:T(8,128)S(1)}, f32[2,128,1024]{2,1,0:T(8,128)S(1)}, u32[]{:S(2)}, u32[]{:S(2)}) collective-permute-start(f32[2,128,1024]{2,1,0:T(8,128)S(1)} %copy-done.9), channel_id=1, source_target_pairs={{0,16},{1,17},{2,18},{3,19},{4,20},{5,21},{6,22},{7,23},{8,56},{9,... | collective-permute-start | bytes 3145736 | tf_op jit(solution)/shard_map/ppermute | solution.py:29
  50.6 25.3 %collective-permute-start.13 = (f32[2,128,1024]{2,1,0:T(8,128)S(1)}, f32[2,128,1024]{2,1,0:T(8,128)S(1)}, u32[]{:S(2)}, u32[]{:S(2)}) collective-permute-start(f32[2,128,1024]{2,1,0:T(8,128)S(1)} %copy-done.1), channel_id=1, source_target_pairs={{0,64},{1,65},{2,66},{3,67},{4,68},{5,69},{6,70},{7,71},{8,72},{9,... | collective-permute-start | bytes 3145736 | tf_op jit(solution)/shard_map/ppermute | solution.py:29
  61.8 1.3 copy-start.7
  75.4 1.0 copy-start.11
  76.4 1.0 copy-start.13
  77.4 5.0 %collective-permute-start.14 = (f32[4,64,1536]{2,1,0:T(8,128)}, f32[4,64,1536]{2,1,0:T(8,128)}, u32[]{:S(2)}, u32[]{:S(2)}) collective-permute-start(f32[4,64,1536]{2,1,0:T(8,128)} %pad_maximum_fusion.8), channel_id=1, source_target_pairs={{0,8},{1,9},{2,10},{3,11},{4,12},{5,13},{6,14},{7,15},{8,0},{9,1},... | collective-permute-start | bytes 4718600 | tf_op jit(solution)/shard_map/ppermute | solution.py:29
  79.1 29.7 %collective-permute-start.24 = (f32[2,128,1024]{2,1,0:T(8,128)}, f32[2,128,1024]{2,1,0:T(8,128)}, u32[]{:S(2)}, u32[]{:S(2)}) collective-permute-start(f32[2,128,1024]{2,1,0:T(8,128)} %copy-done.13), channel_id=1, source_target_pairs={{0,48},{1,49},{2,50},{3,51},{4,52},{5,53},{6,54},{7,55},{8,56},{9,... | collective-permute-start | bytes 3145736 | tf_op jit(solution)/shard_map/ppermute | solution.py:29
  80.2 33.7 %collective-permute-start.23 = (f32[2,128,1024]{2,1,0:T(8,128)}, f32[2,128,1024]{2,1,0:T(8,128)}, u32[]{:S(2)}, u32[]{:S(2)}) collective-permute-start(f32[2,128,1024]{2,1,0:T(8,128)} %copy-done.13), channel_id=1, source_target_pairs={{0,16},{1,17},{2,18},{3,19},{4,20},{5,21},{6,22},{7,23},{8,24},{9,... | collective-permute-start | bytes 3145736 | tf_op jit(solution)/shard_map/ppermute | solution.py:29
  80.5 25.5 %collective-permute-start.15 = (f32[4,128,1024]{2,1,0:T(8,128)}, f32[4,128,1024]{2,1,0:T(8,128)S(1)}, u32[]{:S(2)}, u32[]{:S(2)}) collective-permute-start(f32[4,128,1024]{2,1,0:T(8,128)} %pad_maximum_fusion.3), channel_id=1, source_target_pairs={{0,2},{1,3},{2,4},{3,5},{4,6},{5,7},{6,0},{7,1},{8,14},{9,15},{10,... | collective-permute-start | bytes 6291464 | tf_op jit(solution)/shard_map/ppermute | solution.py:29
  82.1 32.3 %collective-permute-start.21 = (f32[2,128,1024]{2,1,0:T(8,128)}, f32[2,128,1024]{2,1,0:T(8,128)}, u32[]{:S(2)}, u32[]{:S(2)}) collective-permute-start(f32[2,128,1024]{2,1,0:T(8,128)} %copy-done.11), channel_id=1, source_target_pairs={{0,64},{1,65},{2,66},{3,67},{4,68},{5,69},{6,70},{7,71},{8,72},{9,... | collective-permute-start | bytes 3145736 | tf_op jit(solution)/shard_map/ppermute | solution.py:29
  82.5 32.1 %collective-permute-start.20 = (f32[2,128,1024]{2,1,0:T(8,128)}, f32[2,128,1024]{2,1,0:T(8,128)S(1)}, u32[]{:S(2)}, u32[]{:S(2)}) collective-permute-start(f32[2,128,1024]{2,1,0:T(8,128)} %copy-done.13), channel_id=1, source_target_pairs={{0,8},{1,9},{2,10},{3,11},{4,12},{5,13},{6,14},{7,15},{8,0},{9,1},... | collective-permute-start | bytes 3145736 | tf_op jit(solution)/shard_map/ppermute | solution.py:29
  90.8 1.3 copy-start.3
  90.8 1.5 copy-start.5
  92.0 17.0 %copy-start = (f32[1024,1024]{1,0:T(8,128)}, f32[1024,1024]{1,0:T(8,128)S(1)}, u32[]{:S(2)}) copy-start(f32[1024,1024]{1,0:T(8,128)S(1)} %fusion.21) | copy-start | bytes 12582916
  97.1 9.0 %copy-start.12 = (f32[2,128,1024]{2,1,0:T(8,128)S(1)}, f32[2,128,1024]{2,1,0:T(8,128)}, u32[]{:S(2)}) copy-start(f32[2,128,1024]{2,1,0:T(8,128)} %copy-done.11) | copy-start | bytes 3145732
  101.8 7.3 %copy-start.4 = (f32[2,1,128,1024]{3,2,0,1:T(8,128)S(1)}, f32[2,1,128,1024]{3,2,0,1:T(8,128)}, u32[]{:S(2)}) copy-start(f32[2,1,128,1024]{3,2,0,1:T(8,128)} %get-tuple-element.74) | copy-start | bytes 3145732
  101.8 7.3 %copy-start.6 = (f32[2,1,128,1024]{3,2,0,1:T(8,128)S(1)}, f32[2,1,128,1024]{3,2,0,1:T(8,128)}, u32[]{:S(2)}) copy-start(f32[2,1,128,1024]{3,2,0,1:T(8,128)} %get-tuple-element.78) | copy-start | bytes 3145732
  106.0 8.9 %collective-permute-start.17 = (f32[2,128,1024]{2,1,0:T(8,128)S(1)}, f32[2,128,1024]{2,1,0:T(8,128)S(1)}, u32[]{:S(2)}, u32[]{:S(2)}) collective-permute-start(f32[2,128,1024]{2,1,0:T(8,128)S(1)} %copy-done.12), channel_id=1, source_target_pairs={{0,8},{1,9},{2,10},{3,11},{4,12},{5,13},{6,14},{7,15},{8,0},{9,1},... | collective-permute-start | bytes 3145736 | tf_op jit(solution)/shard_map/ppermute | solution.py:29
  108.8 7.8 %collective-permute-start.16 = (f32[2,128,1024]{2,1,0:T(8,128)S(1)}, f32[2,128,1024]{2,1,0:T(8,128)S(1)}, u32[]{:S(2)}, u32[]{:S(2)}) collective-permute-start(f32[2,128,1024]{2,1,0:T(8,128)S(1)} %get-tuple-element.44), channel_id=1, source_target_pairs={{0,8},{1,9},{2,10},{3,11},{4,12},{5,13},{6,14},{7,15},{8,0},{9,1},... | collective-permute-start | bytes 3145736 | tf_op jit(solution)/shard_map/ppermute | solution.py:29
  109.1 4.8 %copy-start.10 = (f32[2,128,1024]{2,1,0:T(8,128)S(1)}, f32[2,128,1024]{2,1,0:T(8,128)}, u32[]{:S(2)}) copy-start(f32[2,128,1024]{2,1,0:T(8,128)} %copy-done.8) | copy-start | bytes 3145732
  113.9 12.9 %collective-permute-start.18 = (f32[2,128,1024]{2,1,0:T(8,128)S(1)}, f32[2,128,1024]{2,1,0:T(8,128)}, u32[]{:S(2)}, u32[]{:S(2)}) collective-permute-start(f32[2,128,1024]{2,1,0:T(8,128)S(1)} %copy-done.10), channel_id=1, source_target_pairs={{0,8},{1,9},{2,10},{3,11},{4,12},{5,13},{6,14},{7,15},{8,0},{9,1},... | collective-permute-start | bytes 3145736 | tf_op jit(solution)/shard_map/ppermute | solution.py:29
  114.4 12.4 %collective-permute-start.19 = (f32[2,128,1024]{2,1,0:T(8,128)}, f32[2,128,1024]{2,1,0:T(8,128)}, u32[]{:S(2)}, u32[]{:S(2)}) collective-permute-start(f32[2,128,1024]{2,1,0:T(8,128)} %collective-permute-done.6.refs_15_), channel_id=1, source_target_pairs={{0,8},{1,9},{2,10},{3,11},{4,12},{5,13},{6,14},{7,15},{8,0},{9,1},... | collective-permute-start | bytes 3145736 | tf_op jit(solution)/shard_map/ppermute | solution.py:29
  114.5 1.0 copy-start.14
  114.5 12.3 %collective-permute-start.22 = (f32[2,128,1024]{2,1,0:T(8,128)}, f32[2,128,1024]{2,1,0:T(8,128)}, u32[]{:S(2)}, u32[]{:S(2)}) collective-permute-start(f32[2,128,1024]{2,1,0:T(8,128)} %collective-permute-done.21.refs_20_), channel_id=1, source_target_pairs={{0,8},{1,9},{2,10},{3,11},{4,12},{5,13},{6,14},{7,15},{8,0},{9,1},... | collective-permute-start | bytes 3145736 | tf_op jit(solution)/shard_map/ppermute | solution.py:29
  115.5 1.0 copy-start.15
  115.5 11.3 %collective-permute-start.25 = (f32[2,128,1024]{2,1,0:T(8,128)}, f32[2,128,1024]{2,1,0:T(8,128)}, u32[]{:S(2)}, u32[]{:S(2)}) collective-permute-start(f32[2,128,1024]{2,1,0:T(8,128)} %collective-permute-done.23.refs_22_), channel_id=1, source_target_pairs={{0,8},{1,9},{2,10},{3,11},{4,12},{5,13},{6,14},{7,15},{8,0},{9,1},... | collective-permute-start | bytes 3145736 | tf_op jit(solution)/shard_map/ppermute | solution.py:29
  116.6 1.0 copy-start.16
  117.6 9.2 %collective-permute-start.26 = (f32[2,128,1024]{2,1,0:T(8,128)}, f32[2,128,1024]{2,1,0:T(8,128)}, u32[]{:S(2)}, u32[]{:S(2)}) collective-permute-start(f32[2,128,1024]{2,1,0:T(8,128)} %collective-permute-done.24.refs_23_), channel_id=1, source_target_pairs={{0,8},{1,9},{2,10},{3,11},{4,12},{5,13},{6,14},{7,15},{8,0},{9,1},... | collective-permute-start | bytes 3145736 | tf_op jit(solution)/shard_map/ppermute | solution.py:29

commit v5 on v4

--- a/solution.py
+++ b/solution.py
@@ -77,11 +77,11 @@
 
 
 def update_kernel(counts, slots, left, buffer, position, kind, meta, *refs):
-    blocks, n_sources = counts
+    n_lefts, n_sources = counts
     trails, refs = refs[:2], refs[2:]
-    lefts, refs = refs[: 2 * len(blocks)], refs[2 * len(blocks) :]
+    lefts, refs = refs[:n_lefts], refs[n_lefts:]
     sources, refs = refs[:n_sources], refs[n_sources:]
-    out, slab, sems, done, done_sems = refs
+    out, slab, sems, done, done_sems, whole_left, left_sems = refs
     step = pl.program_id(0)
     half = step % 2
 
@@ -94,6 +94,20 @@
                         source.at[position[2 * at + q]], slab.at[at % 2, q], sems.at[at % 2, q]
                     ).start()
 
+    def left_copies(tile):
+        depth = ORDER // (n_lefts // 2)
+        for at, source in enumerate(lefts):
+            rows = pl.ds(at // 2 * depth, depth)
+            yield pltpu.make_async_copy(
+                source.at[tile], whole_left.at[tile, at % 2, rows, :], left_sems.at[tile, at]
+            )
+
+    @pl.when(step == 0)
+    def _():
+        for tile in range(2):
+            for copy in left_copies(tile):
+                copy.start()
+
     def written(at, q):
         return pltpu.make_async_copy(
             done.at[at % 2, q], out.at[slots[2 * at + q]], done_sems.at[at % 2, q]
@@ -114,6 +128,12 @@
         @pl.when(jnp.logical_and(step >= 2, kind[2 * before + q] > 0))
         def _():
             written(before, q).wait()
+
+    for tile in range(2):
+        @pl.when(step == meta[8 + tile])
+        def _():
+            for copy in left_copies(tile):
+                copy.wait()
 
     @pl.when(kind[2 * step] == 2)
     def _():
@@ -125,16 +145,13 @@
             tops.append(top)
             rests.append((right - top.astype(jnp.float32)).astype(jnp.bfloat16))
         top, rest = jnp.concatenate(tops, 0), jnp.concatenate(rests, 0)
-        first = 0
-        for at, size in enumerate(blocks):
-            hi, lo = lefts[2 * at][0], lefts[2 * at + 1][0]
-            term = product(hi, top) + product(hi, rest) + product(lo, top)
-            for j in range(size):
-                lane = pl.ds(pl.multiple_of(meta[first + j], ROWS), ROWS)
-                rows = slice(j * ROWS, (j + 1) * ROWS)
-                for q in range(2):
-                    done[half, q, lane, :] = trails[q][0, lane, :] - term[rows, q * ROWS : (q + 1) * ROWS]
-            first += size
+        hi, lo = whole_left[left[step], 0], whole_left[left[step], 1]
+        term = product(hi, top) + product(hi, rest) + product(lo, top)
+        for j in range(ORDER // ROWS):
+            lane = pl.ds(pl.multiple_of(meta[j], ROWS), ROWS)
+            rows = slice(j * ROWS, (j + 1) * ROWS)
+            for q in range(2):
+                done[half, q, lane, :] = trails[q][0, lane, :] - term[rows, q * ROWS : (q + 1) * ROWS]
 
     @pl.when(kind[2 * step] == 1)
     def _():
@@ -159,29 +176,26 @@
     return lax.dot_general(a, b, (((1,), (1,)), ((), ())), preferred_element_type=jnp.float32)
 
 
-def update(trailing, blocks, lefts, sources, tables):
+def update(trailing, lefts, sources, tables):
     def slot(q):
         return lambda step, slots, *_: (slots[2 * step + q], 0, 0)
 
-    def tile(step, slots, left, *_):
-        return left[step], 0, 0
-
-    left_specs = [pl.BlockSpec((1, p.shape[1], ORDER), tile) for p in lefts]
     hbm = pl.BlockSpec(memory_space=pl.ANY)
     return pl.pallas_call(
-        functools.partial(update_kernel, (blocks, len(sources))),
+        functools.partial(update_kernel, (len(lefts), len(sources))),
         grid_spec=pltpu.PrefetchScalarGridSpec(
             num_scalar_prefetch=len(tables),
             grid=(STEPS,),
             in_specs=[pl.BlockSpec((1, ORDER, ROWS), slot(q)) for q in range(2)]
-            + left_specs
-            + [hbm] * len(sources),
+            + [hbm] * (len(lefts) + len(sources)),
             out_specs=hbm,
             scratch_shapes=[
                 pltpu.VMEM((2, 2, ROWS, ORDER), jnp.float32),
                 pltpu.SemaphoreType.DMA((2, 2)),
                 pltpu.VMEM((2, 2, ORDER, ROWS), jnp.float32),
                 pltpu.SemaphoreType.DMA((2, 2)),
+                pltpu.VMEM((2, 2, ORDER, ORDER), jnp.bfloat16),
+                pltpu.SemaphoreType.DMA((2, len(lefts))),
             ],
         ),
         out_shape=jax.ShapeDtypeStruct(trailing.shape, trailing.dtype),
@@ -236,7 +250,8 @@
     chosen = jnp.where(filled[None] > 0, mine_rows, mate_rows)
     kind = jnp.where(filled > 0, chosen[3], 0)
     left_of = jnp.where(jnp.arange(STEPS, dtype=jnp.int32) < pairs[0], 0, 1).astype(jnp.int32)
-    tables = [chosen[0], left_of, chosen[1], chosen[2], kind, places.astype(jnp.int32)]
+    meta = jnp.concatenate([places, jnp.stack([jnp.zeros_like(pairs[0]), pairs[0]])]).astype(jnp.int32)
+    tables = [chosen[0], left_of, chosen[1], chosen[2], kind, meta]
 
     half = ORDER // 2
 
@@ -248,8 +263,9 @@
     lower = jnp.where(far == 0, other, pivot_inverse)
     mine = jnp.concatenate([lower, upper], 1)
     x1a = send(panel, along_x)
-    x1b = send(after(sib, x1a), along_x)
-    z1b = send(after(sib, z1a), along_z)
+    x1b = send(sib, along_x)
+    z1b = send(sib, along_z)
+    mine = after(mine, x1a, z1a)
     from_down = send(mine, turn_z(1))
     from_up = send(mine, turn_z(-1))
 
@@ -291,7 +307,7 @@
     sources = [panel, sib, z2, sz2, z1a, z1b, sz1a, sz1b]
     sources += [far_own, far_sib, fz2, sfz2, fz_down, fz_up, sfz_down, sfz_up]
     lefts = own_first + own_second + near_first + near_second
-    return solved, update(trailing, (2, 2, 2, 2), lefts, sources, tables)
+    return solved, update(trailing, lefts, sources, tables)
 
 
 def solution(mesh):

time: 159 us -> 155 us (0.975)
  waiting for transfers between devices: 44.8 us -> 42.2 us
    ppermute x27, waiting for transfers between devices: 44.8 us -> 42.2 us  [send(): return lax.ppermute(value, AXES, pairs)]
  transfers between devices with their start and end apart: 27 -> 27, of which waited for: 9 -> 8; matrix products, arithmetic and copies ran while one was open for 29% -> 30% of each run, Pallas kernels for 0% -> 0%
where the time goes in v5:
time: 155 us; the launch traced here: 154 us
  waiting for transfers between devices  42.2 us (27%)
  Pallas kernels  30 us (19%)
  starting transfers between devices  28.7 us (19%)
  matrix products  28.3 us (18%)
  other arithmetic  12.8 us (8%)
  local copies, waits for them, and re-layouts  9.6 us (6%)
  between operations  2.49 us (2%)
    ppermute x27, waiting for transfers between devices, send(): return lax.ppermute(value, AXES, pairs)  42.2 us
    pallas_call x1, Pallas kernels, update(): pl.pallas_call(functools.partial(update_kernel, (len(lefts), len(sources)...  30 us
    ppermute x27, starting transfers between devices, send(): return lax.ppermute(value, AXES, pairs)  28.7 us
    dot_general x4, matrix products, times(): jnp.einsum('pxak,kj->pxaj', jnp.stack(blocks, 1), square, precision=high)  21.7 us
    unnamed x35, local copies, waits for them, and re-layouts  5.81 us
    dot_general x1, matrix products, square_of(): whole = jnp.einsum('ki,kj->ij', lower, lower, precision=high)  3.68 us
  transfers between devices with their start and end apart: 27, of which 8 were waited for; matrix products, arithmetic and copies ran while one was open for 30% of the time, Pallas kernels for 0%

profile of v5, /device:TPU:17, one launch (start us, length us, event | category | flops | bytes accessed | tf_op | source)
XLA Modules:
  0.0 154.1 jit_solution(8043052570994002096)
XLA Ops:
  0.6 0.8 collective-permute-start.4
  1.4 3.8 %collective-permute-start.2 = (f32[2,128,1024]{2,1,0:T(8,128)}, f32[2,128,1024]{2,1,0:T(8,128)S(1)}, u32[]{:S(2)}, u32[]{:S(2)}) collective-permute-start(f32[2,128,1024]{2,1,0:T(8,128)} %refs_10_.1), channel_id=1, source_target_pairs={{0,16},{1,17},{2,18},{3,19},{4,20},{5,21},{6,22},{7,23},{8,56},{9,... | collective-permute-start | bytes 3145736 | tf_op jit(solution)/shard_map/ppermute | solution.py:29
  5.1 2.5 %collective-permute-start.1 = (f32[2,128,1024]{2,1,0:T(8,128)}, f32[2,128,1024]{2,1,0:T(8,128)S(1)}, u32[]{:S(2)}, u32[]{:S(2)}) collective-permute-start(f32[2,128,1024]{2,1,0:T(8,128)} %refs_10_.1), channel_id=1, source_target_pairs={{0,2},{1,3},{2,4},{3,5},{4,6},{5,7},{6,0},{7,1},{8,14},{9,15},{10,... | collective-permute-start | bytes 3145736 | tf_op jit(solution)/shard_map/ppermute | solution.py:29
  7.7 0.7 fusion.36
  8.4 1.4 fusion.40
  11.4 0.7 compare_select_fusion.7
  12.5 0.6 compare_select_fusion.6.left
  13.2 0.5 slice_bitcast_fusion.3
  13.7 1.7 %collective-permute-done = f32[64,1024]{1,0:T(8,128)S(1)} collective-permute-done((f32[64,1024]{1,0:T(8,128)}, f32[64,1024]{1,0:T(8,128)S(1)}, u32[]{:S(2)}, u32[]{:S(2)}) %collective-permute-start) | collective-permute-done | bytes 262176 | tf_op jit(solution)/shard_map/ppermute | solution.py:29
  15.4 0.7 collective-permute-start.7
  16.1 1.5 collective-permute-start.5
  17.6 0.6 pad_add_fusion.1.meta
  18.2 1.4 collective-permute-start.6
  19.6 0.9 slice_select_fusion
  20.5 1.0 broadcast_select_fusion
  21.7 2.6 %collective-permute-start.3 = (f32[64,1536]{1,0:T(8,128)S(1)}, f32[64,1536]{1,0:T(8,128)S(1)}, u32[]{:S(2)}, u32[]{:S(2)}) collective-permute-start(f32[64,1536]{1,0:T(8,128)S(1)} %pad_maximum_fusion.10), channel_id=1, source_target_pairs={{0,48},{1,49},{2,50},{3,51},{4,52},{5,53},{6,54},{7,55},{8,56},{9,... | collective-permute-start | bytes 1179656 | tf_op jit(solution)/shard_map/ppermute | solution.py:29
  24.3 0.6 bitcast_select_fusion.kind
  24.9 14.3 %collective-permute-done.7 = f32[2,128,1024]{2,1,0:T(8,128)S(1)} collective-permute-done((f32[2,128,1024]{2,1,0:T(8,128)}, f32[2,128,1024]{2,1,0:T(8,128)S(1)}, u32[]{:S(2)}, u32[]{:S(2)}) %collective-permute-start.7) | collective-permute-done | bytes 1048608 | tf_op jit(solution)/shard_map/ppermute | solution.py:29
  39.3 0.6 pad_maximum_fusion.1
  39.9 0.5 copy-done.2
  40.4 0.3 collective-permute-done.3
  40.8 3.0 %collective-permute-start.10 = (f32[4,128,1024]{2,1,0:T(8,128)S(1)}, f32[4,128,1024]{2,1,0:T(8,128)S(1)}, u32[]{:S(2)}, u32[]{:S(2)}) collective-permute-start(f32[4,128,1024]{2,1,0:T(8,128)S(1)} %get-tuple-element.36), channel_id=1, source_target_pairs={{0,8},{1,9},{2,10},{3,11},{4,12},{5,13},{6,14},{7,15},{8,0},{9,1},... | collective-permute-start | bytes 6291464 | tf_op jit(solution)/shard_map/ppermute | solution.py:29
  43.8 2.2 %collective-permute-start.9 = (f32[64,1536]{1,0:T(8,128)S(1)}, f32[64,1536]{1,0:T(8,128)S(1)}, u32[]{:S(2)}, u32[]{:S(2)}) collective-permute-start(f32[64,1536]{1,0:T(8,128)S(1)} %pad_maximum_fusion.10), channel_id=1, source_target_pairs={{0,32},{1,33},{2,34},{3,35},{4,36},{5,37},{6,38},{7,39},{8,40},{9,... | collective-permute-start | bytes 1179656 | tf_op jit(solution)/shard_map/ppermute | solution.py:29
  46.1 0.5 collective-permute-start.12
  46.6 0.3 collective-permute-start.13
  47.0 8.1 %collective-permute-done.9 = f32[64,1536]{1,0:T(8,128)S(1)} collective-permute-done((f32[64,1536]{1,0:T(8,128)S(1)}, f32[64,1536]{1,0:T(8,128)S(1)}, u32[]{:S(2)}, u32[]{:S(2)}) %collective-permute-start.9) | collective-permute-done | bytes 393248 | tf_op jit(solution)/shard_map/ppermute | solution.py:29
  55.1 1.3 pad_maximum_fusion.8
  56.4 1.2 slice_bitcast_fusion.2
  57.5 11.4 %collective-permute-done.11 = f32[4,128,1024]{2,1,0:T(8,128)S(1)} collective-permute-done((f32[4,128,1024]{2,1,0:T(8,128)S(1)}, f32[4,128,1024]{2,1,0:T(8,128)S(1)}, u32[]{:S(2)}, u32[]{:S(2)}) %collective-permute-start.11) | collective-permute-done | bytes 2097184 | tf_op jit(solution)/shard_map/ppermute | solution.py:29
  68.9 1.6 %slice_bitcast_fusion.6 = (f32[2,1,128,1024]{3,2,0,1:T(8,128)}, f32[2,1,128,1024]{3,2,0,1:T(8,128)}, f32[2,128,1024]{2,1,0:T(8,128)S(1)}) fusion(f32[4,128,1024]{2,1,0:T(8,128)S(1)} %collective-permute-done.11), kind=kLoop, calls=%fused_computation.129 | loop fusion | bytes 5242880 | tf_op jit(solution)/shard_map/stack | solution.py:213
  70.6 1.4 pad_maximum_fusion.3
  72.0 0.5 collective-permute-done.13.refs_18_
  72.5 0.5 copy-done.11
  73.0 1.0 copy-done.13
  74.0 2.1 %collective-permute-start.14 = (f32[4,64,1536]{2,1,0:T(8,128)}, f32[4,64,1536]{2,1,0:T(8,128)}, u32[]{:S(2)}, u32[]{:S(2)}) collective-permute-start(f32[4,64,1536]{2,1,0:T(8,128)} %pad_maximum_fusion.8), channel_id=1, source_target_pairs={{0,8},{1,9},{2,10},{3,11},{4,12},{5,13},{6,14},{7,15},{8,0},{9,1},... | collective-permute-start | bytes 4718600 | tf_op jit(solution)/shard_map/ppermute | solution.py:29
  76.1 0.6 collective-permute-start.24
  76.7 0.9 collective-permute-start.23
  77.6 0.3 collective-permute-start.21
  77.9 1.6 %collective-permute-done.14 = f32[4,64,1536]{2,1,0:T(8,128)} collective-permute-done((f32[4,64,1536]{2,1,0:T(8,128)}, f32[4,64,1536]{2,1,0:T(8,128)}, u32[]{:S(2)}, u32[]{:S(2)}) %collective-permute-start.14) | collective-permute-done | bytes 1572896 | tf_op jit(solution)/shard_map/ppermute | solution.py:29
  79.5 0.4 collective-permute-start.20
  79.9 1.8 %select_bitcast_fusion.1 = (f32[4,1,64,1536]{3,2,0,1:T(8,128)S(1)}, f32[4,1,64,1536]{3,2,0,1:T(8,128)S(1)}) fusion(f32[4,64,1536]{2,1,0:T(8,128)} %collective-permute-done.14, pred[]{:T(512)S(6)} %eq.132, f32[1,64,1536]{2,1,0:T(8,128)S(1)} %bitcast.112, f32[1,64,1536]{2,1,0:T(8,128)} %bitcast.116, f32[1,64,1536]{2,1,0:T(8,128)S(1)} %bitcast.114, ...), kind=kLoop, calls=%fused_computation.39 | loop fusion | flops 1966080 | bytes 6291457 | tf_op jit(solution)/shard_map/stack | solution.py:295
  81.6 0.2 pad_maximum_fusion
  82.1 1.0 fusion.22
  83.1 0.6 convolution_bitcast_fusion
  83.7 0.3 fusion.28
  84.1 3.7 %fusion.18 = f32[1024,1024]{1,0:T(8,128)S(1)} fusion(f32[512,1536]{1,0:T(8,128)S(1)} %bitcast.96), kind=kOutput, calls=%fused_computation.34 | convolution fusion | flops 3221225472 | bytes 6291456 | tf_op jit(solution)/shard_map/ki,kj->ij/dot_general | solution.py:74
  87.8 1.2 fusion.21
  89.1 0.3 copy-done.5
  89.4 4.7 %fusion.10 = (bf16[2,2,128,1024]{3,2,1,0:T(8,128)(2,1)}, bf16[2,2,128,1024]{3,2,1,0:T(8,128)(2,1)}) fusion(f32[1024,1024]{1,0:T(8,128)S(1)} %fusion.21, f32[2,1,128,1024]{3,2,0,1:T(8,128)S(1)} %copy-done.5, f32[2,1,128,1024]{3,2,0,1:T(8,128)S(1)} %bitcast.100), kind=kOutput, calls=%fused_computation.19 | convolution fusion | flops 3223846912 | bytes 8388608 | tf_op jit(solution)/shard_map/pxak,kj->pxaj/dot_general | solution.py:213
  94.1 4.7 %fusion.8 = (bf16[2,2,128,1024]{3,2,1,0:T(8,128)(2,1)}, bf16[2,2,128,1024]{3,2,1,0:T(8,128)(2,1)}) fusion(f32[1024,1024]{1,0:T(8,128)S(1)} %fusion.21, f32[2,1,128,1024]{3,2,0,1:T(8,128)S(1)} %bitcast.99, f32[2,1,128,1024]{3,2,0,1:T(8,128)S(1)} %bitcast.98), kind=kOutput, calls=%fused_computation.17 | convolution fusion | flops 3223846912 | bytes 8388608 | tf_op jit(solution)/shard_map/pxak,kj->pxaj/dot_general | solution.py:213
  98.8 4.2 %collective-permute-done.15 = f32[4,128,1024]{2,1,0:T(8,128)S(1)} collective-permute-done((f32[4,128,1024]{2,1,0:T(8,128)}, f32[4,128,1024]{2,1,0:T(8,128)S(1)}, u32[]{:S(2)}, u32[]{:S(2)}) %collective-permute-start.15) | collective-permute-done | bytes 2097184 | tf_op jit(solution)/shard_map/ppermute | solution.py:29
  103.1 2.5 %collective-permute-start.17 = (f32[2,128,1024]{2,1,0:T(8,128)S(1)}, f32[2,128,1024]{2,1,0:T(8,128)S(1)}, u32[]{:S(2)}, u32[]{:S(2)}) collective-permute-start(f32[2,128,1024]{2,1,0:T(8,128)S(1)} %copy-done.12), channel_id=1, source_target_pairs={{0,8},{1,9},{2,10},{3,11},{4,12},{5,13},{6,14},{7,15},{8,0},{9,1},... | collective-permute-start | bytes 3145736 | tf_op jit(solution)/shard_map/ppermute | solution.py:29
  105.8 0.3 collective-permute-start.16
  106.1 4.8 %fusion.9 = (bf16[2,2,128,1024]{3,2,1,0:T(8,128)(2,1)}, bf16[2,2,128,1024]{3,2,1,0:T(8,128)(2,1)}) fusion(f32[1024,1024]{1,0:T(8,128)S(1)} %fusion.21, f32[2,1,128,1024]{3,2,0,1:T(8,128)S(1)} %copy-done.4, f32[2,1,128,1024]{3,2,0,1:T(8,128)S(1)} %copy-done.6), kind=kOutput, calls=%fused_computation.18 | convolution fusion | flops 3223846912 | bytes 8388608 | tf_op jit(solution)/shard_map/pxak,kj->pxaj/dot_general | solution.py:213
  110.9 0.6 collective-permute-start.18
  111.6 0.4 collective-permute-start.22
  112.0 0.6 copy-done.14
  112.6 0.4 collective-permute-start.25
  113.0 0.6 copy-done.15
  113.6 1.0 copy-done.16
  114.6 0.4 collective-permute-start.26
  115.0 1.3 copy.18
  116.3 7.5 %fusion.11 = (bf16[2,2,128,1024]{3,2,1,0:T(8,128)(2,1)}, bf16[2,2,128,1024]{3,2,1,0:T(8,128)(2,1)}) fusion(f32[1024,1024]{1,0:T(8,128)} %copy-done, f32[2,1,128,1024]{3,2,0,1:T(8,128)S(1)} %get-tuple-element.68, f32[2,1,128,1024]{3,2,0,1:T(8,128)} %bitcast.117), kind=kOutput, calls=%fused_computation.20 | convolution fusion | flops 3223846912 | bytes 8388608 | tf_op jit(solution)/shard_map/pxak,kj->pxaj/dot_general | solution.py:213
  123.9 30.0 %shard_map.59 = f32[20,1024,128]{2,1,0:T(8,128)} custom-call(s32[24]{0:T(128)} %get-tuple-element.84.slots, s32[12]{0:T(128)} %compare_select_fusion.6.left, s32[24]{0:T(128)} %get-tuple-element.83.buffer, s32[24]{0:T(128)} %get-tuple-element.82.position, s32[24]{0:T(128)} %bitcast_select_fusion.kind, s32[10]{0:T(128)} %pad_add_fusion.1.meta, ...), custom_call_target="tpu_custom_call" | custom-call | tf_op jit(solution)/shard_map/pallas_call | solution.py:184
  (69 shorter events, 1.7 us)
Async XLA Ops:
  0.6 15.5 %collective-permute-start.4 = (f32[2,128,1024]{2,1,0:T(8,128)}, f32[2,128,1024]{2,1,0:T(8,128)}, u32[]{:S(2)}, u32[]{:S(2)}) collective-permute-start(f32[2,128,1024]{2,1,0:T(8,128)} %refs_10_.1), channel_id=1, source_target_pairs={{0,8},{1,9},{2,10},{3,11},{4,12},{5,13},{6,14},{7,15},{8,0},{9,1},... | collective-permute-start | bytes 3145736 | tf_op jit(solution)/shard_map/ppermute | solution.py:29
  1.4 20.2 %collective-permute-start.2 = (f32[2,128,1024]{2,1,0:T(8,128)}, f32[2,128,1024]{2,1,0:T(8,128)S(1)}, u32[]{:S(2)}, u32[]{:S(2)}) collective-permute-start(f32[2,128,1024]{2,1,0:T(8,128)} %refs_10_.1), channel_id=1, source_target_pairs={{0,16},{1,17},{2,18},{3,19},{4,20},{5,21},{6,22},{7,23},{8,56},{9,... | collective-permute-start | bytes 3145736 | tf_op jit(solution)/shard_map/ppermute | solution.py:29
  5.1 16.4 %collective-permute-start.1 = (f32[2,128,1024]{2,1,0:T(8,128)}, f32[2,128,1024]{2,1,0:T(8,128)S(1)}, u32[]{:S(2)}, u32[]{:S(2)}) collective-permute-start(f32[2,128,1024]{2,1,0:T(8,128)} %refs_10_.1), channel_id=1, source_target_pairs={{0,2},{1,3},{2,4},{3,5},{4,6},{5,7},{6,0},{7,1},{8,14},{9,15},{10,... | collective-permute-start | bytes 3145736 | tf_op jit(solution)/shard_map/ppermute | solution.py:29
  7.6 7.8 %collective-permute-start = (f32[64,1024]{1,0:T(8,128)}, f32[64,1024]{1,0:T(8,128)S(1)}, u32[]{:S(2)}, u32[]{:S(2)}) collective-permute-start(f32[64,1024]{1,0:T(8,128)} %param.6), channel_id=1, source_target_pairs={{0,64},{1,65},{2,66},{3,67},{4,68},{5,69},{6,70},{7,71},{8,72},{9,... | collective-permute-start | bytes 786440 | tf_op jit(solution)/shard_map/ppermute | solution.py:29
  15.4 23.9 %collective-permute-start.7 = (f32[2,128,1024]{2,1,0:T(8,128)}, f32[2,128,1024]{2,1,0:T(8,128)S(1)}, u32[]{:S(2)}, u32[]{:S(2)}) collective-permute-start(f32[2,128,1024]{2,1,0:T(8,128)} %refs_10_.1), channel_id=1, source_target_pairs={{0,1},{1,0},{2,3},{3,2},{4,5},{5,4},{6,7},{7,6},{8,9},{9,8},{10,11... | collective-permute-start | bytes 3145736 | tf_op jit(solution)/shard_map/ppermute | solution.py:29
  16.1 23.2 %collective-permute-start.5 = (f32[2,128,1024]{2,1,0:T(8,128)}, f32[2,128,1024]{2,1,0:T(8,128)S(1)}, u32[]{:S(2)}, u32[]{:S(2)}) collective-permute-start(f32[2,128,1024]{2,1,0:T(8,128)} %collective-permute-done.4.refs_11_), channel_id=1, source_target_pairs={{0,2},{1,3},{2,4},{3,5},{4,6},{5,7},{6,0},{7,1},{8,14},{9,15},{10,... | collective-permute-start | bytes 3145736 | tf_op jit(solution)/shard_map/ppermute | solution.py:29
  18.2 22.6 %collective-permute-start.6 = (f32[2,128,1024]{2,1,0:T(8,128)}, f32[2,128,1024]{2,1,0:T(8,128)}, u32[]{:S(2)}, u32[]{:S(2)}) collective-permute-start(f32[2,128,1024]{2,1,0:T(8,128)} %collective-permute-done.4.refs_11_), channel_id=1, source_target_pairs={{0,16},{1,17},{2,18},{3,19},{4,20},{5,21},{6,22},{7,23},{8,56},{9,... | collective-permute-start | bytes 3145736 | tf_op jit(solution)/shard_map/ppermute | solution.py:29
  21.6 2.8 %copy-start.8 = (f32[2,128,1024]{2,1,0:T(8,128)}, f32[2,128,1024]{2,1,0:T(8,128)S(1)}, u32[]{:S(2)}) copy-start(f32[2,128,1024]{2,1,0:T(8,128)S(1)} %collective-permute-done.2.refs_14_) | copy-start | bytes 3145732
  21.6 18.8 %collective-permute-start.8 = (f32[64,1536]{1,0:T(8,128)S(1)}, f32[64,1536]{1,0:T(8,128)S(1)}, u32[]{:S(2)}, u32[]{:S(2)}) collective-permute-start(f32[64,1536]{1,0:T(8,128)S(1)} %pad_maximum_fusion.10), channel_id=1, source_target_pairs={{0,16},{1,17},{2,18},{3,19},{4,20},{5,21},{6,22},{7,23},{8,24},{9,... | collective-permute-start | bytes 1179656 | tf_op jit(solution)/shard_map/ppermute | solution.py:29
  21.7 19.1 %collective-permute-start.3 = (f32[64,1536]{1,0:T(8,128)S(1)}, f32[64,1536]{1,0:T(8,128)S(1)}, u32[]{:S(2)}, u32[]{:S(2)}) collective-permute-start(f32[64,1536]{1,0:T(8,128)S(1)} %pad_maximum_fusion.10), channel_id=1, source_target_pairs={{0,48},{1,49},{2,50},{3,51},{4,52},{5,53},{6,54},{7,55},{8,56},{9,... | collective-permute-start | bytes 1179656 | tf_op jit(solution)/shard_map/ppermute | solution.py:29
  24.9 21.2 %copy-start.9 = (f32[2,128,1024]{2,1,0:T(8,128)S(1)}, f32[2,128,1024]{2,1,0:T(8,128)}, u32[]{:S(2)}) copy-start(f32[2,128,1024]{2,1,0:T(8,128)} %copy-done.8) | copy-start | bytes 3145732
  24.9 21.7 %copy-start.1 = (f32[2,128,1024]{2,1,0:T(8,128)S(1)}, f32[2,128,1024]{2,1,0:T(8,128)}, u32[]{:S(2)}) copy-start(f32[2,128,1024]{2,1,0:T(8,128)} %refs_10_.1) | copy-start | bytes 3145732
  39.3 1.1 copy-start.2
  40.8 15.6 %collective-permute-start.10 = (f32[4,128,1024]{2,1,0:T(8,128)S(1)}, f32[4,128,1024]{2,1,0:T(8,128)S(1)}, u32[]{:S(2)}, u32[]{:S(2)}) collective-permute-start(f32[4,128,1024]{2,1,0:T(8,128)S(1)} %get-tuple-element.36), channel_id=1, source_target_pairs={{0,8},{1,9},{2,10},{3,11},{4,12},{5,13},{6,14},{7,15},{8,0},{9,1},... | collective-permute-start | bytes 6291464 | tf_op jit(solution)/shard_map/ppermute | solution.py:29
  43.8 25.2 %collective-permute-start.11 = (f32[4,128,1024]{2,1,0:T(8,128)S(1)}, f32[4,128,1024]{2,1,0:T(8,128)S(1)}, u32[]{:S(2)}, u32[]{:S(2)}) collective-permute-start(f32[4,128,1024]{2,1,0:T(8,128)S(1)} %get-tuple-element.37), channel_id=1, source_target_pairs={{0,2},{1,3},{2,4},{3,5},{4,6},{5,7},{6,0},{7,1},{8,14},{9,15},{10,... | collective-permute-start | bytes 6291464 | tf_op jit(solution)/shard_map/ppermute | solution.py:29
  43.8 11.2 %collective-permute-start.9 = (f32[64,1536]{1,0:T(8,128)S(1)}, f32[64,1536]{1,0:T(8,128)S(1)}, u32[]{:S(2)}, u32[]{:S(2)}) collective-permute-start(f32[64,1536]{1,0:T(8,128)S(1)} %pad_maximum_fusion.10), channel_id=1, source_target_pairs={{0,32},{1,33},{2,34},{3,35},{4,36},{5,37},{6,38},{7,39},{8,40},{9,... | collective-permute-start | bytes 1179656 | tf_op jit(solution)/shard_map/ppermute | solution.py:29
  46.1 25.9 %collective-permute-start.12 = (f32[2,128,1024]{2,1,0:T(8,128)S(1)}, f32[2,128,1024]{2,1,0:T(8,128)S(1)}, u32[]{:S(2)}, u32[]{:S(2)}) collective-permute-start(f32[2,128,1024]{2,1,0:T(8,128)S(1)} %copy-done.9), channel_id=1, source_target_pairs={{0,16},{1,17},{2,18},{3,19},{4,20},{5,21},{6,22},{7,23},{8,56},{9,... | collective-permute-start | bytes 3145736 | tf_op jit(solution)/shard_map/ppermute | solution.py:29
  46.6 25.8 %collective-permute-start.13 = (f32[2,128,1024]{2,1,0:T(8,128)S(1)}, f32[2,128,1024]{2,1,0:T(8,128)S(1)}, u32[]{:S(2)}, u32[]{:S(2)}) collective-permute-start(f32[2,128,1024]{2,1,0:T(8,128)S(1)} %copy-done.1), channel_id=1, source_target_pairs={{0,64},{1,65},{2,66},{3,67},{4,68},{5,69},{6,70},{7,71},{8,72},{9,... | collective-permute-start | bytes 3145736 | tf_op jit(solution)/shard_map/ppermute | solution.py:29
  55.1 1.3 copy-start.7
  72.0 1.0 copy-start.11
  73.0 1.0 copy-start.13
  74.0 5.5 %collective-permute-start.14 = (f32[4,64,1536]{2,1,0:T(8,128)}, f32[4,64,1536]{2,1,0:T(8,128)}, u32[]{:S(2)}, u32[]{:S(2)}) collective-permute-start(f32[4,64,1536]{2,1,0:T(8,128)} %pad_maximum_fusion.8), channel_id=1, source_target_pairs={{0,8},{1,9},{2,10},{3,11},{4,12},{5,13},{6,14},{7,15},{8,0},{9,1},... | collective-permute-start | bytes 4718600 | tf_op jit(solution)/shard_map/ppermute | solution.py:29
  76.1 29.7 %collective-permute-start.24 = (f32[2,128,1024]{2,1,0:T(8,128)}, f32[2,128,1024]{2,1,0:T(8,128)}, u32[]{:S(2)}, u32[]{:S(2)}) collective-permute-start(f32[2,128,1024]{2,1,0:T(8,128)} %copy-done.13), channel_id=1, source_target_pairs={{0,48},{1,49},{2,50},{3,51},{4,52},{5,53},{6,54},{7,55},{8,56},{9,... | collective-permute-start | bytes 3145736 | tf_op jit(solution)/shard_map/ppermute | solution.py:29
  76.7 34.3 %collective-permute-start.23 = (f32[2,128,1024]{2,1,0:T(8,128)}, f32[2,128,1024]{2,1,0:T(8,128)}, u32[]{:S(2)}, u32[]{:S(2)}) collective-permute-start(f32[2,128,1024]{2,1,0:T(8,128)} %copy-done.13), channel_id=1, source_target_pairs={{0,16},{1,17},{2,18},{3,19},{4,20},{5,21},{6,22},{7,23},{8,24},{9,... | collective-permute-start | bytes 3145736 | tf_op jit(solution)/shard_map/ppermute | solution.py:29
  77.6 25.5 %collective-permute-start.15 = (f32[4,128,1024]{2,1,0:T(8,128)}, f32[4,128,1024]{2,1,0:T(8,128)S(1)}, u32[]{:S(2)}, u32[]{:S(2)}) collective-permute-start(f32[4,128,1024]{2,1,0:T(8,128)} %pad_maximum_fusion.3), channel_id=1, source_target_pairs={{0,2},{1,3},{2,4},{3,5},{4,6},{5,7},{6,0},{7,1},{8,14},{9,15},{10,... | collective-permute-start | bytes 6291464 | tf_op jit(solution)/shard_map/ppermute | solution.py:29
  77.6 33.9 %collective-permute-start.21 = (f32[2,128,1024]{2,1,0:T(8,128)}, f32[2,128,1024]{2,1,0:T(8,128)}, u32[]{:S(2)}, u32[]{:S(2)}) collective-permute-start(f32[2,128,1024]{2,1,0:T(8,128)} %copy-done.11), channel_id=1, source_target_pairs={{0,64},{1,65},{2,66},{3,67},{4,68},{5,69},{6,70},{7,71},{8,72},{9,... | collective-permute-start | bytes 3145736 | tf_op jit(solution)/shard_map/ppermute | solution.py:29
  79.5 32.1 %collective-permute-start.20 = (f32[2,128,1024]{2,1,0:T(8,128)}, f32[2,128,1024]{2,1,0:T(8,128)S(1)}, u32[]{:S(2)}, u32[]{:S(2)}) collective-permute-start(f32[2,128,1024]{2,1,0:T(8,128)} %copy-done.13), channel_id=1, source_target_pairs={{0,8},{1,9},{2,10},{3,11},{4,12},{5,13},{6,14},{7,15},{8,0},{9,1},... | collective-permute-start | bytes 3145736 | tf_op jit(solution)/shard_map/ppermute | solution.py:29
  87.8 1.3 copy-start.3
  87.8 1.5 copy-start.5
  89.1 17.0 %copy-start = (f32[1024,1024]{1,0:T(8,128)}, f32[1024,1024]{1,0:T(8,128)S(1)}, u32[]{:S(2)}) copy-start(f32[1024,1024]{1,0:T(8,128)S(1)} %fusion.21) | copy-start | bytes 12582916
  94.1 9.0 %copy-start.12 = (f32[2,128,1024]{2,1,0:T(8,128)S(1)}, f32[2,128,1024]{2,1,0:T(8,128)}, u32[]{:S(2)}) copy-start(f32[2,128,1024]{2,1,0:T(8,128)} %copy-done.11) | copy-start | bytes 3145732
  98.8 7.3 %copy-start.4 = (f32[2,1,128,1024]{3,2,0,1:T(8,128)S(1)}, f32[2,1,128,1024]{3,2,0,1:T(8,128)}, u32[]{:S(2)}) copy-start(f32[2,1,128,1024]{3,2,0,1:T(8,128)} %get-tuple-element.72) | copy-start | bytes 3145732
  98.8 7.3 %copy-start.6 = (f32[2,1,128,1024]{3,2,0,1:T(8,128)S(1)}, f32[2,1,128,1024]{3,2,0,1:T(8,128)}, u32[]{:S(2)}) copy-start(f32[2,1,128,1024]{3,2,0,1:T(8,128)} %get-tuple-element.76) | copy-start | bytes 3145732
  103.1 8.9 %collective-permute-start.17 = (f32[2,128,1024]{2,1,0:T(8,128)S(1)}, f32[2,128,1024]{2,1,0:T(8,128)S(1)}, u32[]{:S(2)}, u32[]{:S(2)}) collective-permute-start(f32[2,128,1024]{2,1,0:T(8,128)S(1)} %copy-done.12), channel_id=1, source_target_pairs={{0,8},{1,9},{2,10},{3,11},{4,12},{5,13},{6,14},{7,15},{8,0},{9,1},... | collective-permute-start | bytes 3145736 | tf_op jit(solution)/shard_map/ppermute | solution.py:29
  105.8 7.8 %collective-permute-start.16 = (f32[2,128,1024]{2,1,0:T(8,128)S(1)}, f32[2,128,1024]{2,1,0:T(8,128)S(1)}, u32[]{:S(2)}, u32[]{:S(2)}) collective-permute-start(f32[2,128,1024]{2,1,0:T(8,128)S(1)} %get-tuple-element.42), channel_id=1, source_target_pairs={{0,8},{1,9},{2,10},{3,11},{4,12},{5,13},{6,14},{7,15},{8,0},{9,1},... | collective-permute-start | bytes 3145736 | tf_op jit(solution)/shard_map/ppermute | solution.py:29
  106.1 4.8 %copy-start.10 = (f32[2,128,1024]{2,1,0:T(8,128)S(1)}, f32[2,128,1024]{2,1,0:T(8,128)}, u32[]{:S(2)}) copy-start(f32[2,128,1024]{2,1,0:T(8,128)} %copy-done.8) | copy-start | bytes 3145732
  110.9 12.9 %collective-permute-start.18 = (f32[2,128,1024]{2,1,0:T(8,128)S(1)}, f32[2,128,1024]{2,1,0:T(8,128)}, u32[]{:S(2)}, u32[]{:S(2)}) collective-permute-start(f32[2,128,1024]{2,1,0:T(8,128)S(1)} %copy-done.10), channel_id=1, source_target_pairs={{0,8},{1,9},{2,10},{3,11},{4,12},{5,13},{6,14},{7,15},{8,0},{9,1},... | collective-permute-start | bytes 3145736 | tf_op jit(solution)/shard_map/ppermute | solution.py:29
  111.5 12.4 %collective-permute-start.19 = (f32[2,128,1024]{2,1,0:T(8,128)}, f32[2,128,1024]{2,1,0:T(8,128)}, u32[]{:S(2)}, u32[]{:S(2)}) collective-permute-start(f32[2,128,1024]{2,1,0:T(8,128)} %collective-permute-done.6.refs_15_), channel_id=1, source_target_pairs={{0,8},{1,9},{2,10},{3,11},{4,12},{5,13},{6,14},{7,15},{8,0},{9,1},... | collective-permute-start | bytes 3145736 | tf_op jit(solution)/shard_map/ppermute | solution.py:29
  111.6 1.0 copy-start.14
  111.6 12.3 %collective-permute-start.22 = (f32[2,128,1024]{2,1,0:T(8,128)}, f32[2,128,1024]{2,1,0:T(8,128)}, u32[]{:S(2)}, u32[]{:S(2)}) collective-permute-start(f32[2,128,1024]{2,1,0:T(8,128)} %collective-permute-done.21.refs_20_), channel_id=1, source_target_pairs={{0,8},{1,9},{2,10},{3,11},{4,12},{5,13},{6,14},{7,15},{8,0},{9,1},... | collective-permute-start | bytes 3145736 | tf_op jit(solution)/shard_map/ppermute | solution.py:29
  112.6 1.0 copy-start.15
  112.6 11.3 %collective-permute-start.25 = (f32[2,128,1024]{2,1,0:T(8,128)}, f32[2,128,1024]{2,1,0:T(8,128)}, u32[]{:S(2)}, u32[]{:S(2)}) collective-permute-start(f32[2,128,1024]{2,1,0:T(8,128)} %collective-permute-done.23.refs_22_), channel_id=1, source_target_pairs={{0,8},{1,9},{2,10},{3,11},{4,12},{5,13},{6,14},{7,15},{8,0},{9,1},... | collective-permute-start | bytes 3145736 | tf_op jit(solution)/shard_map/ppermute | solution.py:29
  113.6 1.0 copy-start.16
  114.6 9.2 %collective-permute-start.26 = (f32[2,128,1024]{2,1,0:T(8,128)}, f32[2,128,1024]{2,1,0:T(8,128)}, u32[]{:S(2)}, u32[]{:S(2)}) collective-permute-start(f32[2,128,1024]{2,1,0:T(8,128)} %collective-permute-done.24.refs_23_), channel_id=1, source_target_pairs={{0,8},{1,9},{2,10},{3,11},{4,12},{5,13},{6,14},{7,15},{8,0},{9,1},... | collective-permute-start | bytes 3145736 | tf_op jit(solution)/shard_map/ppermute | solution.py:29

commit v6 on v5

--- a/solution.py
+++ b/solution.py
@@ -102,12 +102,6 @@
                 source.at[tile], whole_left.at[tile, at % 2, rows, :], left_sems.at[tile, at]
             )
 
-    @pl.when(step == 0)
-    def _():
-        for tile in range(2):
-            for copy in left_copies(tile):
-                copy.start()
-
     def written(at, q):
         return pltpu.make_async_copy(
             done.at[at % 2, q], out.at[slots[2 * at + q]], done_sems.at[at % 2, q]
@@ -129,11 +123,19 @@
         def _():
             written(before, q).wait()
 
-    for tile in range(2):
-        @pl.when(step == meta[8 + tile])
-        def _():
-            for copy in left_copies(tile):
-                copy.wait()
+    @pl.when(step == 0)
+    def _():
+        for copy in left_copies(0):
+            copy.start()
+        for copy in left_copies(0):
+            copy.wait()
+        for copy in left_copies(1):
+            copy.start()
+
+    @pl.when(step == meta[8])
+    def _():
+        for copy in left_copies(1):
+            copy.wait()
 
     @pl.when(kind[2 * step] == 2)
     def _():
@@ -250,7 +252,7 @@
     chosen = jnp.where(filled[None] > 0, mine_rows, mate_rows)
     kind = jnp.where(filled > 0, chosen[3], 0)
     left_of = jnp.where(jnp.arange(STEPS, dtype=jnp.int32) < pairs[0], 0, 1).astype(jnp.int32)
-    meta = jnp.concatenate([places, jnp.stack([jnp.zeros_like(pairs[0]), pairs[0]])]).astype(jnp.int32)
+    meta = jnp.concatenate([places, pairs[0][None]]).astype(jnp.int32)
     tables = [chosen[0], left_of, chosen[1], chosen[2], kind, meta]
 
     half = ORDER // 2
@@ -299,7 +301,7 @@
     own_second = times([sx1, x2], square)
     near_first = times([near_own, nx1a], square)
     solved = solve(panel, lower, upper, z)
-    ready = (solved, *own_first, *near_first)
+    ready = (solved[0, :8, :ROWS], *own_first, *near_first)
     nsx1 = swap(after(nx1b, *ready))
     near_second = times([nsx1, nx2], square)
     sfz_down, sfz_up, sfz2 = [swap(after(part, *ready, *own_second)) for part in (fz_down, fz_up, fz2)]

time: 155 us -> 151 us (0.974)
  Pallas kernels: 30 us -> 27.1 us
  local copies, waits for them, and re-layouts: 9.6 us -> 6.82 us
  waiting for transfers between devices: 42.2 us -> 44 us
    pallas_call x1, Pallas kernels: 30 us -> 27.1 us  [update(): pl.pallas_call(functools.partial(update_kernel, (len(lefts), len(sources)...]
    unnamed x35, local copies, waits for them, and re-layouts: 5.81 us -> 2.97 us
    ppermute x27, waiting for transfers between devices: 42.2 us -> 44 us  [send(): return lax.ppermute(value, AXES, pairs)]
  transfers between devices with their start and end apart: 27 -> 27, of which waited for: 8 -> 8; matrix products, arithmetic and copies ran while one was open for 30% -> 31% of each run, Pallas kernels for 0% -> 0%
where the time goes in v6:
time: 151 us; the launch traced here: 150 us
  waiting for transfers between devices  44 us (29%)
  starting transfers between devices  28.4 us (19%)
  matrix products  28.1 us (19%)
  Pallas kernels  27.1 us (18%)
  other arithmetic  13.1 us (9%)
  local copies, waits for them, and re-layouts  6.82 us (5%)
  between operations  2.53 us (2%)
    ppermute x27, waiting for transfers between devices, send(): return lax.ppermute(value, AXES, pairs)  44 us
    ppermute x27, starting transfers between devices, send(): return lax.ppermute(value, AXES, pairs)  28.4 us
    pallas_call x1, Pallas kernels, update(): pl.pallas_call(functools.partial(update_kernel, (len(lefts), len(sources)...  27.1 us
    dot_general x4, matrix products, times(): jnp.einsum('pxak,kj->pxaj', jnp.stack(blocks, 1), square, precision=high)  21.8 us
    dot_general x1, matrix products, square_of(): whole = jnp.einsum('ki,kj->ij', lower, lower, precision=high)  3.53 us
  transfers between devices with their start and end apart: 27, of which 8 were waited for; matrix products, arithmetic and copies ran while one was open for 31% of the time, Pallas kernels for 0%

profile of v6, /device:TPU:17, one launch (start us, length us, event | category | flops | bytes accessed | tf_op | source)
XLA Modules:
  0.0 150.2 jit_solution(3399880987366393025)
XLA Ops:
  0.6 0.8 collective-permute-start.4
  1.4 3.8 %collective-permute-start.2 = (f32[2,128,1024]{2,1,0:T(8,128)}, f32[2,128,1024]{2,1,0:T(8,128)S(1)}, u32[]{:S(2)}, u32[]{:S(2)}) collective-permute-start(f32[2,128,1024]{2,1,0:T(8,128)} %refs_10_.1), channel_id=1, source_target_pairs={{0,16},{1,17},{2,18},{3,19},{4,20},{5,21},{6,22},{7,23},{8,56},{9,... | collective-permute-start | bytes 3145736 | tf_op jit(solution)/shard_map/ppermute | solution.py:29
  5.1 2.5 %collective-permute-start.1 = (f32[2,128,1024]{2,1,0:T(8,128)}, f32[2,128,1024]{2,1,0:T(8,128)S(1)}, u32[]{:S(2)}, u32[]{:S(2)}) collective-permute-start(f32[2,128,1024]{2,1,0:T(8,128)} %refs_10_.1), channel_id=1, source_target_pairs={{0,2},{1,3},{2,4},{3,5},{4,6},{5,7},{6,0},{7,1},{8,14},{9,15},{10,... | collective-permute-start | bytes 3145736 | tf_op jit(solution)/shard_map/ppermute | solution.py:29
  7.7 0.7 fusion.36
  8.4 1.4 fusion.40
  11.1 0.2 convert_reduce_fusion
  11.4 0.7 compare_select_fusion.7
  12.5 0.5 compare_select_fusion.6.left
  13.1 0.6 slice_bitcast_fusion.4
  13.7 1.7 %collective-permute-done = f32[64,1024]{1,0:T(8,128)S(1)} collective-permute-done((f32[64,1024]{1,0:T(8,128)}, f32[64,1024]{1,0:T(8,128)S(1)}, u32[]{:S(2)}, u32[]{:S(2)}) %collective-permute-start) | collective-permute-done | bytes 262176 | tf_op jit(solution)/shard_map/ppermute | solution.py:29
  15.4 0.7 collective-permute-start.7
  16.1 1.5 collective-permute-start.5
  17.6 0.7 pad_add_fusion.1.meta
  18.2 1.4 collective-permute-start.6
  19.6 0.9 slice_select_fusion
  20.6 1.0 broadcast_select_fusion
  21.6 0.1 collective-permute-start.8
  21.7 2.6 %collective-permute-start.3 = (f32[64,1536]{1,0:T(8,128)S(1)}, f32[64,1536]{1,0:T(8,128)S(1)}, u32[]{:S(2)}, u32[]{:S(2)}) collective-permute-start(f32[64,1536]{1,0:T(8,128)S(1)} %pad_maximum_fusion.10), channel_id=1, source_target_pairs={{0,48},{1,49},{2,50},{3,51},{4,52},{5,53},{6,54},{7,55},{8,56},{9,... | collective-permute-start | bytes 1179656 | tf_op jit(solution)/shard_map/ppermute | solution.py:29
  24.4 0.6 bitcast_select_fusion.kind
  25.0 14.3 %collective-permute-done.7 = f32[2,128,1024]{2,1,0:T(8,128)S(1)} collective-permute-done((f32[2,128,1024]{2,1,0:T(8,128)}, f32[2,128,1024]{2,1,0:T(8,128)S(1)}, u32[]{:S(2)}, u32[]{:S(2)}) %collective-permute-start.7) | collective-permute-done | bytes 1048608 | tf_op jit(solution)/shard_map/ppermute | solution.py:29
  39.3 0.6 pad_maximum_fusion.1
  39.9 0.9 collective-permute-done.3
  40.8 3.1 %collective-permute-start.10 = (f32[4,128,1024]{2,1,0:T(8,128)S(1)}, f32[4,128,1024]{2,1,0:T(8,128)S(1)}, u32[]{:S(2)}, u32[]{:S(2)}) collective-permute-start(f32[4,128,1024]{2,1,0:T(8,128)S(1)} %get-tuple-element.36), channel_id=1, source_target_pairs={{0,8},{1,9},{2,10},{3,11},{4,12},{5,13},{6,14},{7,15},{8,0},{9,1},... | collective-permute-start | bytes 6291464 | tf_op jit(solution)/shard_map/ppermute | solution.py:29
  44.0 2.2 %collective-permute-start.9 = (f32[64,1536]{1,0:T(8,128)S(1)}, f32[64,1536]{1,0:T(8,128)S(1)}, u32[]{:S(2)}, u32[]{:S(2)}) collective-permute-start(f32[64,1536]{1,0:T(8,128)S(1)} %pad_maximum_fusion.10), channel_id=1, source_target_pairs={{0,32},{1,33},{2,34},{3,35},{4,36},{5,37},{6,38},{7,39},{8,40},{9,... | collective-permute-start | bytes 1179656 | tf_op jit(solution)/shard_map/ppermute | solution.py:29
  46.2 0.5 collective-permute-start.12
  46.8 0.3 collective-permute-start.13
  47.1 8.1 %collective-permute-done.9 = f32[64,1536]{1,0:T(8,128)S(1)} collective-permute-done((f32[64,1536]{1,0:T(8,128)S(1)}, f32[64,1536]{1,0:T(8,128)S(1)}, u32[]{:S(2)}, u32[]{:S(2)}) %collective-permute-start.9) | collective-permute-done | bytes 393248 | tf_op jit(solution)/shard_map/ppermute | solution.py:29
  55.2 1.3 pad_maximum_fusion.8
  56.5 1.2 slice_bitcast_fusion.2
  57.7 11.4 %collective-permute-done.11 = f32[4,128,1024]{2,1,0:T(8,128)S(1)} collective-permute-done((f32[4,128,1024]{2,1,0:T(8,128)S(1)}, f32[4,128,1024]{2,1,0:T(8,128)S(1)}, u32[]{:S(2)}, u32[]{:S(2)}) %collective-permute-start.11) | collective-permute-done | bytes 2097184 | tf_op jit(solution)/shard_map/ppermute | solution.py:29
  69.1 1.6 %slice_bitcast_fusion.7 = (f32[2,1,128,1024]{3,2,0,1:T(8,128)}, f32[2,1,128,1024]{3,2,0,1:T(8,128)}, f32[2,128,1024]{2,1,0:T(8,128)S(1)}) fusion(f32[4,128,1024]{2,1,0:T(8,128)S(1)} %collective-permute-done.11), kind=kLoop, calls=%fused_computation.130 | loop fusion | bytes 5242880 | tf_op jit(solution)/shard_map/stack | solution.py:215
  70.7 1.4 pad_maximum_fusion.3
  72.1 0.4 collective-permute-done.13.refs_18_
  72.5 0.6 copy-done.11
  73.1 1.0 copy-done.13
  74.1 2.1 %collective-permute-start.14 = (f32[4,64,1536]{2,1,0:T(8,128)}, f32[4,64,1536]{2,1,0:T(8,128)}, u32[]{:S(2)}, u32[]{:S(2)}) collective-permute-start(f32[4,64,1536]{2,1,0:T(8,128)} %pad_maximum_fusion.8), channel_id=1, source_target_pairs={{0,8},{1,9},{2,10},{3,11},{4,12},{5,13},{6,14},{7,15},{8,0},{9,1},... | collective-permute-start | bytes 4718600 | tf_op jit(solution)/shard_map/ppermute | solution.py:29
  76.2 1.5 collective-permute-start.23
  77.7 0.3 collective-permute-start.21
  78.1 1.6 %collective-permute-done.14 = f32[4,64,1536]{2,1,0:T(8,128)} collective-permute-done((f32[4,64,1536]{2,1,0:T(8,128)}, f32[4,64,1536]{2,1,0:T(8,128)}, u32[]{:S(2)}, u32[]{:S(2)}) %collective-permute-start.14) | collective-permute-done | bytes 1572896 | tf_op jit(solution)/shard_map/ppermute | solution.py:29
  79.6 0.4 collective-permute-start.20
  80.0 2.0 %select_bitcast_fusion.1 = (f32[4,1,64,1536]{3,2,0,1:T(8,128)S(1)}, f32[4,1,64,1536]{3,2,0,1:T(8,128)S(1)}) fusion(f32[4,64,1536]{2,1,0:T(8,128)} %collective-permute-done.14, pred[]{:T(512)S(6)} %eq.132, f32[1,64,1536]{2,1,0:T(8,128)} %bitcast.114, f32[1,64,1536]{2,1,0:T(8,128)} %bitcast.118, f32[1,64,1536]{2,1,0:T(8,128)} %bitcast.116, ...), kind=kLoop, calls=%fused_computation.39 | loop fusion | flops 1966080 | bytes 6291457 | tf_op jit(solution)/shard_map/stack | solution.py:297
  82.0 0.2 pad_maximum_fusion
  82.2 0.2 copy.13
  82.4 0.6 convolution_bitcast_fusion
  83.1 0.2 fusion.29
  83.3 3.5 %fusion.18 = f32[1024,1024]{1,0:T(8,128)S(1)} fusion(f32[512,1536]{1,0:T(8,128)S(1)} %bitcast.97), kind=kOutput, calls=%fused_computation.34 | convolution fusion | flops 3221225472 | bytes 6291456 | tf_op jit(solution)/shard_map/ki,kj->ij/dot_general | solution.py:74
  86.8 1.2 fusion.21
  88.0 4.7 %fusion.10 = (bf16[2,2,128,1024]{3,2,1,0:T(8,128)(2,1)}, bf16[2,2,128,1024]{3,2,1,0:T(8,128)(2,1)}) fusion(f32[1024,1024]{1,0:T(8,128)S(1)} %fusion.21, f32[2,1,128,1024]{3,2,0,1:T(8,128)S(1)} %copy-done.3, f32[2,1,128,1024]{3,2,0,1:T(8,128)S(1)} %bitcast.102), kind=kOutput, calls=%fused_computation.19 | convolution fusion | flops 3223846912 | bytes 8388608 | tf_op jit(solution)/shard_map/pxak,kj->pxaj/dot_general | solution.py:215
  92.8 4.7 %fusion.8 = (bf16[2,2,128,1024]{3,2,1,0:T(8,128)(2,1)}, bf16[2,2,128,1024]{3,2,1,0:T(8,128)(2,1)}) fusion(f32[1024,1024]{1,0:T(8,128)S(1)} %fusion.21, f32[2,1,128,1024]{3,2,0,1:T(8,128)S(1)} %bitcast.101, f32[2,1,128,1024]{3,2,0,1:T(8,128)S(1)} %bitcast.100), kind=kOutput, calls=%fused_computation.17 | convolution fusion | flops 3223846912 | bytes 8388608 | tf_op jit(solution)/shard_map/pxak,kj->pxaj/dot_general | solution.py:215
  97.6 5.6 %collective-permute-done.15 = f32[4,128,1024]{2,1,0:T(8,128)S(1)} collective-permute-done((f32[4,128,1024]{2,1,0:T(8,128)}, f32[4,128,1024]{2,1,0:T(8,128)S(1)}, u32[]{:S(2)}, u32[]{:S(2)}) %collective-permute-start.15) | collective-permute-done | bytes 2097184 | tf_op jit(solution)/shard_map/ppermute | solution.py:29
  103.2 2.5 %collective-permute-start.17 = (f32[2,128,1024]{2,1,0:T(8,128)S(1)}, f32[2,128,1024]{2,1,0:T(8,128)S(1)}, u32[]{:S(2)}, u32[]{:S(2)}) collective-permute-start(f32[2,128,1024]{2,1,0:T(8,128)S(1)} %copy-done.12), channel_id=1, source_target_pairs={{0,8},{1,9},{2,10},{3,11},{4,12},{5,13},{6,14},{7,15},{8,0},{9,1},... | collective-permute-start | bytes 3145736 | tf_op jit(solution)/shard_map/ppermute | solution.py:29
  105.7 0.2 fusion.48
  105.9 0.3 collective-permute-start.16
  106.3 4.8 %fusion.9 = (bf16[2,2,128,1024]{3,2,1,0:T(8,128)(2,1)}, bf16[2,2,128,1024]{3,2,1,0:T(8,128)(2,1)}) fusion(f32[1024,1024]{1,0:T(8,128)S(1)} %fusion.21, f32[2,1,128,1024]{3,2,0,1:T(8,128)S(1)} %copy-done.2, f32[2,1,128,1024]{3,2,0,1:T(8,128)S(1)} %copy-done.4), kind=kOutput, calls=%fused_computation.18 | convolution fusion | flops 3223846912 | bytes 8388608 | tf_op jit(solution)/shard_map/pxak,kj->pxaj/dot_general | solution.py:215
  111.0 0.6 collective-permute-start.18
  111.6 0.1 collective-permute-start.19
  111.7 0.4 collective-permute-start.22
  112.1 0.1 collective-permute-start.25
  112.2 0.4 collective-permute-start.26
  112.6 1.0 fusion.22
  113.7 0.2 fusion.28
  114.0 1.3 copy.18
  115.3 7.5 %fusion.11 = (bf16[2,2,128,1024]{3,2,1,0:T(8,128)(2,1)}, bf16[2,2,128,1024]{3,2,1,0:T(8,128)(2,1)}) fusion(f32[1024,1024]{1,0:T(8,128)} %copy-done, f32[2,1,128,1024]{3,2,0,1:T(8,128)S(1)} %get-tuple-element.68, f32[2,1,128,1024]{3,2,0,1:T(8,128)} %bitcast.119), kind=kOutput, calls=%fused_computation.20 | convolution fusion | flops 3223846912 | bytes 8388608 | tf_op jit(solution)/shard_map/pxak,kj->pxaj/dot_general | solution.py:215
  122.9 27.1 %shard_map.59 = f32[20,1024,128]{2,1,0:T(8,128)} custom-call(s32[24]{0:T(128)} %get-tuple-element.84.slots, s32[12]{0:T(128)} %compare_select_fusion.6.left, s32[24]{0:T(128)} %get-tuple-element.83.buffer, s32[24]{0:T(128)} %get-tuple-element.82.position, s32[24]{0:T(128)} %bitcast_select_fusion.kind, s32[9]{0:T(128)} %pad_add_fusion.1.meta, ...), custom_call_target="tpu_custom_call" | custom-call | tf_op jit(solution)/shard_map/pallas_call | solution.py:186
  (70 shorter events, 0.9 us)
Async XLA Ops:
  0.6 15.5 %collective-permute-start.4 = (f32[2,128,1024]{2,1,0:T(8,128)}, f32[2,128,1024]{2,1,0:T(8,128)}, u32[]{:S(2)}, u32[]{:S(2)}) collective-permute-start(f32[2,128,1024]{2,1,0:T(8,128)} %refs_10_.1), channel_id=1, source_target_pairs={{0,8},{1,9},{2,10},{3,11},{4,12},{5,13},{6,14},{7,15},{8,0},{9,1},... | collective-permute-start | bytes 3145736 | tf_op jit(solution)/shard_map/ppermute | solution.py:29
  1.4 20.2 %collective-permute-start.2 = (f32[2,128,1024]{2,1,0:T(8,128)}, f32[2,128,1024]{2,1,0:T(8,128)S(1)}, u32[]{:S(2)}, u32[]{:S(2)}) collective-permute-start(f32[2,128,1024]{2,1,0:T(8,128)} %refs_10_.1), channel_id=1, source_target_pairs={{0,16},{1,17},{2,18},{3,19},{4,20},{5,21},{6,22},{7,23},{8,56},{9,... | collective-permute-start | bytes 3145736 | tf_op jit(solution)/shard_map/ppermute | solution.py:29
  5.1 16.5 %collective-permute-start.1 = (f32[2,128,1024]{2,1,0:T(8,128)}, f32[2,128,1024]{2,1,0:T(8,128)S(1)}, u32[]{:S(2)}, u32[]{:S(2)}) collective-permute-start(f32[2,128,1024]{2,1,0:T(8,128)} %refs_10_.1), channel_id=1, source_target_pairs={{0,2},{1,3},{2,4},{3,5},{4,6},{5,7},{6,0},{7,1},{8,14},{9,15},{10,... | collective-permute-start | bytes 3145736 | tf_op jit(solution)/shard_map/ppermute | solution.py:29
  7.6 7.8 %collective-permute-start = (f32[64,1024]{1,0:T(8,128)}, f32[64,1024]{1,0:T(8,128)S(1)}, u32[]{:S(2)}, u32[]{:S(2)}) collective-permute-start(f32[64,1024]{1,0:T(8,128)} %param.6), channel_id=1, source_target_pairs={{0,64},{1,65},{2,66},{3,67},{4,68},{5,69},{6,70},{7,71},{8,72},{9,... | collective-permute-start | bytes 786440 | tf_op jit(solution)/shard_map/ppermute | solution.py:29
  15.4 23.9 %collective-permute-start.7 = (f32[2,128,1024]{2,1,0:T(8,128)}, f32[2,128,1024]{2,1,0:T(8,128)S(1)}, u32[]{:S(2)}, u32[]{:S(2)}) collective-permute-start(f32[2,128,1024]{2,1,0:T(8,128)} %refs_10_.1), channel_id=1, source_target_pairs={{0,1},{1,0},{2,3},{3,2},{4,5},{5,4},{6,7},{7,6},{8,9},{9,8},{10,11... | collective-permute-start | bytes 3145736 | tf_op jit(solution)/shard_map/ppermute | solution.py:29
  16.1 23.2 %collective-permute-start.5 = (f32[2,128,1024]{2,1,0:T(8,128)}, f32[2,128,1024]{2,1,0:T(8,128)S(1)}, u32[]{:S(2)}, u32[]{:S(2)}) collective-permute-start(f32[2,128,1024]{2,1,0:T(8,128)} %collective-permute-done.4.refs_11_), channel_id=1, source_target_pairs={{0,2},{1,3},{2,4},{3,5},{4,6},{5,7},{6,0},{7,1},{8,14},{9,15},{10,... | collective-permute-start | bytes 3145736 | tf_op jit(solution)/shard_map/ppermute | solution.py:29
  18.2 22.6 %collective-permute-start.6 = (f32[2,128,1024]{2,1,0:T(8,128)}, f32[2,128,1024]{2,1,0:T(8,128)}, u32[]{:S(2)}, u32[]{:S(2)}) collective-permute-start(f32[2,128,1024]{2,1,0:T(8,128)} %collective-permute-done.4.refs_11_), channel_id=1, source_target_pairs={{0,16},{1,17},{2,18},{3,19},{4,20},{5,21},{6,22},{7,23},{8,56},{9,... | collective-permute-start | bytes 3145736 | tf_op jit(solution)/shard_map/ppermute | solution.py:29
  21.6 2.8 %copy-start.8 = (f32[2,128,1024]{2,1,0:T(8,128)}, f32[2,128,1024]{2,1,0:T(8,128)S(1)}, u32[]{:S(2)}) copy-start(f32[2,128,1024]{2,1,0:T(8,128)S(1)} %collective-permute-done.2.refs_14_) | copy-start | bytes 3145732
  21.6 18.2 %collective-permute-start.8 = (f32[64,1536]{1,0:T(8,128)S(1)}, f32[64,1536]{1,0:T(8,128)S(1)}, u32[]{:S(2)}, u32[]{:S(2)}) collective-permute-start(f32[64,1536]{1,0:T(8,128)S(1)} %pad_maximum_fusion.10), channel_id=1, source_target_pairs={{0,16},{1,17},{2,18},{3,19},{4,20},{5,21},{6,22},{7,23},{8,24},{9,... | collective-permute-start | bytes 1179656 | tf_op jit(solution)/shard_map/ppermute | solution.py:29
  21.7 19.1 %collective-permute-start.3 = (f32[64,1536]{1,0:T(8,128)S(1)}, f32[64,1536]{1,0:T(8,128)S(1)}, u32[]{:S(2)}, u32[]{:S(2)}) collective-permute-start(f32[64,1536]{1,0:T(8,128)S(1)} %pad_maximum_fusion.10), channel_id=1, source_target_pairs={{0,48},{1,49},{2,50},{3,51},{4,52},{5,53},{6,54},{7,55},{8,56},{9,... | collective-permute-start | bytes 1179656 | tf_op jit(solution)/shard_map/ppermute | solution.py:29
  25.0 21.3 %copy-start.9 = (f32[2,128,1024]{2,1,0:T(8,128)S(1)}, f32[2,128,1024]{2,1,0:T(8,128)}, u32[]{:S(2)}) copy-start(f32[2,128,1024]{2,1,0:T(8,128)} %copy-done.8) | copy-start | bytes 3145732
  25.0 21.8 %copy-start.1 = (f32[2,128,1024]{2,1,0:T(8,128)S(1)}, f32[2,128,1024]{2,1,0:T(8,128)}, u32[]{:S(2)}) copy-start(f32[2,128,1024]{2,1,0:T(8,128)} %refs_10_.1) | copy-start | bytes 3145732
  39.9 17.8 %copy-start.5 = (f32[64,1536]{1,0:T(8,128)}, f32[64,1536]{1,0:T(8,128)S(1)}, u32[]{:S(2)}) copy-start(f32[64,1536]{1,0:T(8,128)S(1)} %collective-permute-done.8) | copy-start | bytes 1179652
  40.8 16.9 %copy-start.6 = (f32[64,1536]{1,0:T(8,128)}, f32[64,1536]{1,0:T(8,128)S(1)}, u32[]{:S(2)}) copy-start(f32[64,1536]{1,0:T(8,128)S(1)} %collective-permute-done.3) | copy-start | bytes 1179652
  40.8 15.7 %collective-permute-start.10 = (f32[4,128,1024]{2,1,0:T(8,128)S(1)}, f32[4,128,1024]{2,1,0:T(8,128)S(1)}, u32[]{:S(2)}, u32[]{:S(2)}) collective-permute-start(f32[4,128,1024]{2,1,0:T(8,128)S(1)} %get-tuple-element.36), channel_id=1, source_target_pairs={{0,8},{1,9},{2,10},{3,11},{4,12},{5,13},{6,14},{7,15},{8,0},{9,1},... | collective-permute-start | bytes 6291464 | tf_op jit(solution)/shard_map/ppermute | solution.py:29
  43.9 25.2 %collective-permute-start.11 = (f32[4,128,1024]{2,1,0:T(8,128)S(1)}, f32[4,128,1024]{2,1,0:T(8,128)S(1)}, u32[]{:S(2)}, u32[]{:S(2)}) collective-permute-start(f32[4,128,1024]{2,1,0:T(8,128)S(1)} %get-tuple-element.37), channel_id=1, source_target_pairs={{0,2},{1,3},{2,4},{3,5},{4,6},{5,7},{6,0},{7,1},{8,14},{9,15},{10,... | collective-permute-start | bytes 6291464 | tf_op jit(solution)/shard_map/ppermute | solution.py:29
  44.0 11.2 %collective-permute-start.9 = (f32[64,1536]{1,0:T(8,128)S(1)}, f32[64,1536]{1,0:T(8,128)S(1)}, u32[]{:S(2)}, u32[]{:S(2)}) collective-permute-start(f32[64,1536]{1,0:T(8,128)S(1)} %pad_maximum_fusion.10), channel_id=1, source_target_pairs={{0,32},{1,33},{2,34},{3,35},{4,36},{5,37},{6,38},{7,39},{8,40},{9,... | collective-permute-start | bytes 1179656 | tf_op jit(solution)/shard_map/ppermute | solution.py:29
  46.2 25.9 %collective-permute-start.12 = (f32[2,128,1024]{2,1,0:T(8,128)S(1)}, f32[2,128,1024]{2,1,0:T(8,128)S(1)}, u32[]{:S(2)}, u32[]{:S(2)}) collective-permute-start(f32[2,128,1024]{2,1,0:T(8,128)S(1)} %copy-done.9), channel_id=1, source_target_pairs={{0,16},{1,17},{2,18},{3,19},{4,20},{5,21},{6,22},{7,23},{8,56},{9,... | collective-permute-start | bytes 3145736 | tf_op jit(solution)/shard_map/ppermute | solution.py:29
  46.8 25.7 %collective-permute-start.13 = (f32[2,128,1024]{2,1,0:T(8,128)S(1)}, f32[2,128,1024]{2,1,0:T(8,128)S(1)}, u32[]{:S(2)}, u32[]{:S(2)}) collective-permute-start(f32[2,128,1024]{2,1,0:T(8,128)S(1)} %copy-done.1), channel_id=1, source_target_pairs={{0,64},{1,65},{2,66},{3,67},{4,68},{5,69},{6,70},{7,71},{8,72},{9,... | collective-permute-start | bytes 3145736 | tf_op jit(solution)/shard_map/ppermute | solution.py:29
  55.2 1.3 copy-start.7
  72.1 1.0 copy-start.11
  73.1 1.0 copy-start.13
  74.1 5.5 %collective-permute-start.14 = (f32[4,64,1536]{2,1,0:T(8,128)}, f32[4,64,1536]{2,1,0:T(8,128)}, u32[]{:S(2)}, u32[]{:S(2)}) collective-permute-start(f32[4,64,1536]{2,1,0:T(8,128)} %pad_maximum_fusion.8), channel_id=1, source_target_pairs={{0,8},{1,9},{2,10},{3,11},{4,12},{5,13},{6,14},{7,15},{8,0},{9,1},... | collective-permute-start | bytes 4718600 | tf_op jit(solution)/shard_map/ppermute | solution.py:29
  76.2 29.7 %collective-permute-start.24 = (f32[2,128,1024]{2,1,0:T(8,128)}, f32[2,128,1024]{2,1,0:T(8,128)}, u32[]{:S(2)}, u32[]{:S(2)}) collective-permute-start(f32[2,128,1024]{2,1,0:T(8,128)} %copy-done.13), channel_id=1, source_target_pairs={{0,48},{1,49},{2,50},{3,51},{4,52},{5,53},{6,54},{7,55},{8,56},{9,... | collective-permute-start | bytes 3145736 | tf_op jit(solution)/shard_map/ppermute | solution.py:29
  76.2 34.8 %collective-permute-start.23 = (f32[2,128,1024]{2,1,0:T(8,128)}, f32[2,128,1024]{2,1,0:T(8,128)}, u32[]{:S(2)}, u32[]{:S(2)}) collective-permute-start(f32[2,128,1024]{2,1,0:T(8,128)} %copy-done.13), channel_id=1, source_target_pairs={{0,16},{1,17},{2,18},{3,19},{4,20},{5,21},{6,22},{7,23},{8,24},{9,... | collective-permute-start | bytes 3145736 | tf_op jit(solution)/shard_map/ppermute | solution.py:29
  77.7 25.5 %collective-permute-start.15 = (f32[4,128,1024]{2,1,0:T(8,128)}, f32[4,128,1024]{2,1,0:T(8,128)S(1)}, u32[]{:S(2)}, u32[]{:S(2)}) collective-permute-start(f32[4,128,1024]{2,1,0:T(8,128)} %pad_maximum_fusion.3), channel_id=1, source_target_pairs={{0,2},{1,3},{2,4},{3,5},{4,6},{5,7},{6,0},{7,1},{8,14},{9,15},{10,... | collective-permute-start | bytes 6291464 | tf_op jit(solution)/shard_map/ppermute | solution.py:29
  77.7 33.9 %collective-permute-start.21 = (f32[2,128,1024]{2,1,0:T(8,128)}, f32[2,128,1024]{2,1,0:T(8,128)}, u32[]{:S(2)}, u32[]{:S(2)}) collective-permute-start(f32[2,128,1024]{2,1,0:T(8,128)} %copy-done.11), channel_id=1, source_target_pairs={{0,64},{1,65},{2,66},{3,67},{4,68},{5,69},{6,70},{7,71},{8,72},{9,... | collective-permute-start | bytes 3145736 | tf_op jit(solution)/shard_map/ppermute | solution.py:29
  79.6 32.1 %collective-permute-start.20 = (f32[2,128,1024]{2,1,0:T(8,128)}, f32[2,128,1024]{2,1,0:T(8,128)S(1)}, u32[]{:S(2)}, u32[]{:S(2)}) collective-permute-start(f32[2,128,1024]{2,1,0:T(8,128)} %copy-done.13), channel_id=1, source_target_pairs={{0,8},{1,9},{2,10},{3,11},{4,12},{5,13},{6,14},{7,15},{8,0},{9,1},... | collective-permute-start | bytes 3145736 | tf_op jit(solution)/shard_map/ppermute | solution.py:29
  86.8 1.2 copy-start.3
  88.0 18.2 %copy-start = (f32[1024,1024]{1,0:T(8,128)}, f32[1024,1024]{1,0:T(8,128)S(1)}, u32[]{:S(2)}) copy-start(f32[1024,1024]{1,0:T(8,128)S(1)} %fusion.21) | copy-start | bytes 12582916
  92.8 10.4 %copy-start.12 = (f32[2,128,1024]{2,1,0:T(8,128)S(1)}, f32[2,128,1024]{2,1,0:T(8,128)}, u32[]{:S(2)}) copy-start(f32[2,128,1024]{2,1,0:T(8,128)} %copy-done.11) | copy-start | bytes 3145732
  97.5 8.7 %copy-start.2 = (f32[2,1,128,1024]{3,2,0,1:T(8,128)S(1)}, f32[2,1,128,1024]{3,2,0,1:T(8,128)}, u32[]{:S(2)}) copy-start(f32[2,1,128,1024]{3,2,0,1:T(8,128)} %get-tuple-element.72) | copy-start | bytes 3145732
  97.5 8.7 %copy-start.4 = (f32[2,1,128,1024]{3,2,0,1:T(8,128)S(1)}, f32[2,1,128,1024]{3,2,0,1:T(8,128)}, u32[]{:S(2)}) copy-start(f32[2,1,128,1024]{3,2,0,1:T(8,128)} %get-tuple-element.76) | copy-start | bytes 3145732
  103.2 8.9 %collective-permute-start.17 = (f32[2,128,1024]{2,1,0:T(8,128)S(1)}, f32[2,128,1024]{2,1,0:T(8,128)S(1)}, u32[]{:S(2)}, u32[]{:S(2)}) collective-permute-start(f32[2,128,1024]{2,1,0:T(8,128)S(1)} %copy-done.12), channel_id=1, source_target_pairs={{0,8},{1,9},{2,10},{3,11},{4,12},{5,13},{6,14},{7,15},{8,0},{9,1},... | collective-permute-start | bytes 3145736 | tf_op jit(solution)/shard_map/ppermute | solution.py:29
  105.9 6.3 %collective-permute-start.16 = (f32[2,128,1024]{2,1,0:T(8,128)S(1)}, f32[2,128,1024]{2,1,0:T(8,128)S(1)}, u32[]{:S(2)}, u32[]{:S(2)}) collective-permute-start(f32[2,128,1024]{2,1,0:T(8,128)S(1)} %get-tuple-element.42), channel_id=1, source_target_pairs={{0,8},{1,9},{2,10},{3,11},{4,12},{5,13},{6,14},{7,15},{8,0},{9,1},... | collective-permute-start | bytes 3145736 | tf_op jit(solution)/shard_map/ppermute | solution.py:29
  106.3 4.8 %copy-start.10 = (f32[2,128,1024]{2,1,0:T(8,128)S(1)}, f32[2,128,1024]{2,1,0:T(8,128)}, u32[]{:S(2)}) copy-start(f32[2,128,1024]{2,1,0:T(8,128)} %copy-done.8) | copy-start | bytes 3145732
  111.0 11.8 %collective-permute-start.18 = (f32[2,128,1024]{2,1,0:T(8,128)S(1)}, f32[2,128,1024]{2,1,0:T(8,128)}, u32[]{:S(2)}, u32[]{:S(2)}) collective-permute-start(f32[2,128,1024]{2,1,0:T(8,128)S(1)} %copy-done.10), channel_id=1, source_target_pairs={{0,8},{1,9},{2,10},{3,11},{4,12},{5,13},{6,14},{7,15},{8,0},{9,1},... | collective-permute-start | bytes 3145736 | tf_op jit(solution)/shard_map/ppermute | solution.py:29
  111.6 11.2 %collective-permute-start.19 = (f32[2,128,1024]{2,1,0:T(8,128)}, f32[2,128,1024]{2,1,0:T(8,128)}, u32[]{:S(2)}, u32[]{:S(2)}) collective-permute-start(f32[2,128,1024]{2,1,0:T(8,128)} %collective-permute-done.6.refs_15_), channel_id=1, source_target_pairs={{0,8},{1,9},{2,10},{3,11},{4,12},{5,13},{6,14},{7,15},{8,0},{9,1},... | collective-permute-start | bytes 3145736 | tf_op jit(solution)/shard_map/ppermute | solution.py:29
  111.7 2.2 %copy-start.14 = (f32[2,128,1024]{2,1,0:T(8,128)}, f32[2,128,1024]{2,1,0:T(8,128)S(1)}, u32[]{:S(2)}) copy-start(f32[2,128,1024]{2,1,0:T(8,128)S(1)} %collective-permute-done.20.refs_19_) | copy-start | bytes 3145732
  111.7 11.1 %collective-permute-start.22 = (f32[2,128,1024]{2,1,0:T(8,128)}, f32[2,128,1024]{2,1,0:T(8,128)}, u32[]{:S(2)}, u32[]{:S(2)}) collective-permute-start(f32[2,128,1024]{2,1,0:T(8,128)} %collective-permute-done.21.refs_20_), channel_id=1, source_target_pairs={{0,8},{1,9},{2,10},{3,11},{4,12},{5,13},{6,14},{7,15},{8,0},{9,1},... | collective-permute-start | bytes 3145736 | tf_op jit(solution)/shard_map/ppermute | solution.py:29
  112.1 1.8 %copy-start.15 = (f32[2,128,1024]{2,1,0:T(8,128)}, f32[2,128,1024]{2,1,0:T(8,128)S(1)}, u32[]{:S(2)}) copy-start(f32[2,128,1024]{2,1,0:T(8,128)S(1)} %collective-permute-done.17.refs_13_) | copy-start | bytes 3145732
  112.1 10.7 %collective-permute-start.25 = (f32[2,128,1024]{2,1,0:T(8,128)}, f32[2,128,1024]{2,1,0:T(8,128)}, u32[]{:S(2)}, u32[]{:S(2)}) collective-permute-start(f32[2,128,1024]{2,1,0:T(8,128)} %collective-permute-done.23.refs_22_), channel_id=1, source_target_pairs={{0,8},{1,9},{2,10},{3,11},{4,12},{5,13},{6,14},{7,15},{8,0},{9,1},... | collective-permute-start | bytes 3145736 | tf_op jit(solution)/shard_map/ppermute | solution.py:29
  112.2 1.7 %copy-start.16 = (f32[2,128,1024]{2,1,0:T(8,128)}, f32[2,128,1024]{2,1,0:T(8,128)S(1)}, u32[]{:S(2)}) copy-start(f32[2,128,1024]{2,1,0:T(8,128)S(1)} %collective-permute-done.16) | copy-start | bytes 3145732
  112.2 10.6 %collective-permute-start.26 = (f32[2,128,1024]{2,1,0:T(8,128)}, f32[2,128,1024]{2,1,0:T(8,128)}, u32[]{:S(2)}, u32[]{:S(2)}) collective-permute-start(f32[2,128,1024]{2,1,0:T(8,128)} %collective-permute-done.24.refs_23_), channel_id=1, source_target_pairs={{0,8},{1,9},{2,10},{3,11},{4,12},{5,13},{6,14},{7,15},{8,0},{9,1},... | collective-permute-start | bytes 3145736 | tf_op jit(solution)/shard_map/ppermute | solution.py:29
